TPU v7x, 32 devices: a whole 2x2x4 slice. The times are simulated.
32 devices in a mesh: dp: 16 (over z, x, core), mod: 2 (over y).
Axes of the slice: x: 2, y: 2, z: 4, core: 2. Of those that a mesh axis runs over, the one named last changes fastest.
Arguments:
- x_in: bfloat16 [32768, 1152], P(('dp', 'mod')), may hold values from -6 to 6
- cond: bfloat16 [128, 1152], P('dp'), may hold values from -4 to 4
- segments: int32 [32768], P(('dp', 'mod')), may hold values from 0 to 3, as said below
- out_grad: bfloat16 [32768, 1152], P(('dp', 'mod')), may hold values from -6 to 6
- qkv_weight: float32 [1152, 3456], P('dp', 'mod'), may hold values from -0.11785113 to 0.11785113
- qkv_moment: float32 [1152, 3456], P('dp', 'mod'), may hold values from -448 to 448
- qkv_average: float32 [1152, 3456], P('dp', 'mod'), may hold values from -0.1875 to 0.1875
- proj_weight: float32 [1152, 1152], P('dp', 'mod'), may hold values from -0.375 to 0.375
- proj_moment: float32 [1152, 1152], P('dp', 'mod'), may hold values from -448 to 448
- proj_average: float32 [1152, 1152], P('dp', 'mod'), may hold values from -0.375 to 0.375
- fc1_weight: float32 [1152, 4608], P('dp', 'mod'), may hold values from -0.1875 to 0.1875
- fc1_moment: float32 [1152, 4608], P('dp', 'mod'), may hold values from -320 to 320
- fc1_average: float32 [1152, 4608], P('dp', 'mod'), may hold values from -0.1875 to 0.1875
- fc2_weight: float32 [4608, 1152], P('dp', 'mod'), may hold values from -0.09375 to 0.09375
- fc2_moment: float32 [4608, 1152], P('dp', 'mod'), may hold values from -384 to 384
- fc2_average: float32 [4608, 1152], P('dp', 'mod'), may hold values from -0.09375 to 0.09375
- bias_weight: float32 [9216], P(('dp', 'mod')), may hold values from -1.25 to 1.25
- bias_moment: float32 [9216], P(('dp', 'mod')), may hold values from -896 to 896
- bias_average: float32 [9216], P(('dp', 'mod')), may hold values from -1.25 to 1.25
- ada_weight: float32 [1152, 6912], P('dp', 'mod'), may hold values from -0.11785113 to 0.11785113
- ada_moment: float32 [1152, 6912], P('dp', 'mod'), may hold values from -512 to 512
- ada_average: float32 [1152, 6912], P('dp', 'mod'), may hold values from -0.1875 to 0.1875
- adab_weight: float32 [2, 3456], P('mod', 'dp'), may hold values from -0.8 to 0.8
- adab_moment: float32 [2, 3456], P('mod', 'dp'), may hold values from -768 to 768
- adab_average: float32 [2, 3456], P('mod', 'dp'), may hold values from -1.25 to 1.25
Outputs:
- block_out: bfloat16 [32768, 1152], P(('dp', 'mod'))
- x_grad: float32 [32768, 1152], P(('dp', 'mod'))
- cond_grad: float32 [128, 1152], P('dp')
- qkv_weight_next: float32 [1152, 3456], P('dp', 'mod')
- qkv_moment_next: float32 [1152, 3456], P('dp', 'mod')
- qkv_average_next: float32 [1152, 3456], P('dp', 'mod')
- proj_weight_next: float32 [1152, 1152], P('dp', 'mod')
- proj_moment_next: float32 [1152, 1152], P('dp', 'mod')
- proj_average_next: float32 [1152, 1152], P('dp', 'mod')
- fc1_weight_next: float32 [1152, 4608], P('dp', 'mod')
- fc1_moment_next: float32 [1152, 4608], P('dp', 'mod')
- fc1_average_next: float32 [1152, 4608], P('dp', 'mod')
- fc2_weight_next: float32 [4608, 1152], P('dp', 'mod')
- fc2_moment_next: float32 [4608, 1152], P('dp', 'mod')
- fc2_average_next: float32 [4608, 1152], P('dp', 'mod')
- bias_weight_next: float32 [9216], P(('dp', 'mod'))
- bias_moment_next: float32 [9216], P(('dp', 'mod'))
- bias_average_next: float32 [9216], P(('dp', 'mod'))
- ada_weight_next: float32 [1152, 6912], P('dp', 'mod')
- ada_moment_next: float32 [1152, 6912], P('dp', 'mod')
- ada_average_next: float32 [1152, 6912], P('dp', 'mod')
- adab_weight_next: float32 [2, 3456], P('mod', 'dp')
- adab_moment_next: float32 [2, 3456], P('mod', 'dp')
- adab_average_next: float32 [2, 3456], P('mod', 'dp')
Inputs may be any that keep to these rules, and one draw needn't show every extreme that they name: `segments`: each aligned block of 1024 tokens of one device holds either one image, all of whose tokens carry the slot number of the block's first 256 tokens, or 4 images of 256 tokens, each token carrying its position within the device's tokens // 256. Both kinds occur in every draw.
All inputs are finite; a program needn't handle non-finite values.
Results may differ from a plain program's by a relative error of at most 0.013.
Values may be sent and summed in bfloat16 or wider, within the bound.
A program may use at most 384 MiB of HBM per device.

v0:
```python
from functools import partial

import jax
import jax.numpy as jnp
from jax import lax
from jax.sharding import PartitionSpec as P

D = 1152
HEADS = 16
FF = 4608


EPS = 1e-06
MOMENTUM = 0.9
DECAY = 0.5


def normalize(values):
    centre = values - jnp.mean(values, axis=-1, keepdims=True)
    inverse = lax.rsqrt(jnp.mean(centre * centre, axis=-1, keepdims=True) + EPS)
    return (centre * inverse, inverse)


def normalize_back(upstream, normed, inverse):
    return inverse * (
        upstream
        - jnp.mean(upstream, axis=-1, keepdims=True)
        - normed * jnp.mean(upstream * normed, axis=-1, keepdims=True)
    )


def step_rates(tokens_all):
    base_rate = tokens_all ** (-0.5)
    return (
        2.5 * D ** (-0.5) * base_rate,
        3.0 * D ** (-0.5) * base_rate,
        3.3 * D ** (-0.5) * base_rate,
        2.8 * FF ** (-0.5) * base_rate,
        0.5 * base_rate,
        2.0 * D ** (-0.5) * base_rate,
        0.3 * base_rate,
    )


def nesterov(weight, moment, average, gradient, rate):
    moment = MOMENTUM * moment + gradient
    weight = weight - rate * (gradient + MOMENTUM * moment)
    average = DECAY * average + (1.0 - DECAY) * weight
    return (weight, moment, average)


def masked_scores(query_part, seg_part, key_rows, segments, scaling):
    scores = (
        jnp.einsum("qhd,khd->hqk", query_part, key_rows, preferred_element_type=jnp.float32)
        * scaling
    )
    allowed = seg_part[:, None] == segments[None, :]
    return jnp.where(allowed[None], scores, -1e30)


def attend_forward(query_rows, key_rows, value_rows, segments, block_rows):
    tokens, head_count, head_width = query_rows.shape
    scaling = head_width ** (-0.5)
    blocks = tokens // block_rows

    def one_block(inputs):
        query_part, seg_part = inputs
        scores = masked_scores(query_part, seg_part, key_rows, segments, scaling)
        largest = jnp.max(scores, axis=-1, keepdims=True)
        weights = jnp.exp(scores - largest)
        totals = jnp.sum(weights, axis=-1, keepdims=True)
        softmax_low = (weights / totals).astype(jnp.bfloat16)
        mixture = jnp.einsum(
            "hqk,khd->qhd", softmax_low, value_rows, preferred_element_type=jnp.float32
        )
        return (mixture.astype(jnp.bfloat16), (largest + jnp.log(totals))[..., 0])

    mixture, log_totals = lax.map(
        one_block,
        (
            query_rows.reshape(blocks, block_rows, head_count, head_width),
            segments.reshape(blocks, block_rows),
        ),
    )
    return (mixture.reshape(tokens, head_count * head_width), log_totals)


def attend_backward(query_rows, key_rows, value_rows, segments, log_totals, upstream, block_rows):
    tokens, head_count, head_width = query_rows.shape
    scaling = head_width ** (-0.5)
    blocks = tokens // block_rows

    def one_block(carried, inputs):
        key_grad, value_grad = carried
        query_part, seg_part, log_part, up_part = inputs
        scores = masked_scores(query_part, seg_part, key_rows, segments, scaling)
        softmax = jnp.exp(scores - log_part[..., None])
        softmax_low = softmax.astype(jnp.bfloat16)
        value_grad = value_grad + jnp.einsum(
            "hqk,qhd->khd", softmax_low, up_part, preferred_element_type=jnp.float32
        )
        prob_grad = jnp.einsum(
            "qhd,khd->hqk", up_part, value_rows, preferred_element_type=jnp.float32
        )
        centred = prob_grad - jnp.sum(softmax * prob_grad, axis=-1, keepdims=True)
        score_grad = (softmax * centred).astype(jnp.bfloat16)
        query_grad = (
            jnp.einsum("hqk,khd->qhd", score_grad, key_rows, preferred_element_type=jnp.float32)
            * scaling
        )
        key_grad = (
            key_grad
            + jnp.einsum("hqk,qhd->khd", score_grad, query_part, preferred_element_type=jnp.float32)
            * scaling
        )
        return ((key_grad, value_grad), query_grad.astype(jnp.bfloat16))

    zeroes = jnp.zeros(key_rows.shape, jnp.float32)
    carried, query_grad = lax.scan(
        one_block,
        (zeroes, zeroes),
        (
            query_rows.reshape(blocks, block_rows, head_count, head_width),
            segments.reshape(blocks, block_rows),
            log_totals,
            upstream.reshape(blocks, block_rows, head_count, head_width),
        ),
    )
    full_width = head_count * head_width
    return (
        query_grad.reshape(tokens, full_width),
        carried[0].reshape(tokens, full_width).astype(jnp.bfloat16),
        carried[1].reshape(tokens, full_width).astype(jnp.bfloat16),
    )


def body(
    x_in,
    cond,
    segments,
    out_grad,
    qkv_weight,
    qkv_moment,
    qkv_average,
    proj_weight,
    proj_moment,
    proj_average,
    fc1_weight,
    fc1_moment,
    fc1_average,
    fc2_weight,
    fc2_moment,
    fc2_average,
    bias_weight,
    bias_moment,
    bias_average,
    ada_weight,
    ada_moment,
    ada_average,
    adab_weight,
    adab_moment,
    adab_average,
):
    tokens, model_width = x_in.shape
    pair_count = lax.axis_size("mod")
    data_count = lax.axis_size("dp")
    slot_count = cond.shape[0] // pair_count
    head_width = model_width // HEADS
    block_rows = min(512, tokens)
    halves_low = (
        lax.all_gather(qkv_weight.astype(jnp.bfloat16), "mod", axis=1, tiled=True),
        lax.all_gather(proj_weight.astype(jnp.bfloat16), "mod", axis=1, tiled=True),
        lax.all_gather(fc1_weight.astype(jnp.bfloat16), "mod", axis=1, tiled=True),
        lax.all_gather(fc2_weight.astype(jnp.bfloat16), "mod", axis=1, tiled=True),
        lax.all_gather(bias_weight.reshape(1, -1).astype(jnp.bfloat16), "mod", axis=1, tiled=True),
    )
    qkv_low, proj_low, fc1_low, fc2_low, bias_low, ada_low, adab_low = (
        lax.all_gather(halves_low[0], "dp", axis=0, tiled=True),
        lax.all_gather(halves_low[1], "dp", axis=0, tiled=True),
        lax.all_gather(halves_low[2], "dp", axis=0, tiled=True),
        lax.all_gather(halves_low[3], "dp", axis=0, tiled=True),
        lax.all_gather(halves_low[4], "dp", axis=0, tiled=True),
        lax.all_gather(ada_weight.astype(jnp.bfloat16), "dp", axis=0, tiled=True),
        lax.all_gather(adab_weight.reshape(-1).astype(jnp.bfloat16), "dp", axis=0, tiled=True),
    )
    hidden_width = fc1_low.shape[1]
    bias_full = bias_low.reshape(-1).astype(jnp.float32)
    cond_silu, silu_back = jax.vjp(jax.nn.silu, cond.astype(jnp.float32))
    silu_low = cond_silu.astype(jnp.bfloat16)
    half_mod = (
        jnp.dot(silu_low, ada_low, preferred_element_type=jnp.float32)
        + adab_low.astype(jnp.float32)
    ).astype(jnp.bfloat16)
    modulation = lax.all_to_all(half_mod, "mod", split_axis=0, concat_axis=1, tiled=True)
    chooser = segments[:, None] == jnp.arange(slot_count, dtype=jnp.int32)[None, :]
    per_token = jnp.dot(
        chooser.astype(jnp.bfloat16), modulation, preferred_element_type=jnp.float32
    )
    shift_attn, scale_attn, gate_attn, shift_mlp, scale_mlp, gate_mlp = [
        per_token[:, column_group * model_width : (column_group + 1) * model_width]
        for column_group in range(6)
    ]
    residual = x_in.astype(jnp.float32)
    first_norm, first_inverse = normalize(residual)
    attn_input = (first_norm * (1.0 + scale_attn) + shift_attn).astype(jnp.bfloat16)
    joint_proj = jnp.dot(attn_input, qkv_low, preferred_element_type=jnp.float32)
    query_rows = (joint_proj[:, 0:model_width] + bias_full[0:model_width]).astype(jnp.bfloat16)
    key_rows = joint_proj[:, model_width : 2 * model_width].astype(jnp.bfloat16)
    value_rows = (
        joint_proj[:, 2 * model_width : 3 * model_width] + bias_full[model_width : 2 * model_width]
    ).astype(jnp.bfloat16)
    head_shape = (tokens, HEADS, head_width)
    query_heads = query_rows.reshape(head_shape)
    key_heads = key_rows.reshape(head_shape)
    value_heads = value_rows.reshape(head_shape)
    mixture, log_totals = attend_forward(query_heads, key_heads, value_heads, segments, block_rows)
    attn_out = (
        jnp.dot(mixture, proj_low, preferred_element_type=jnp.float32)
        + bias_full[2 * model_width : 3 * model_width]
    )
    residual_mid = residual + gate_attn * attn_out
    second_norm, second_inverse = normalize(residual_mid)
    mlp_input = (second_norm * (1.0 + scale_mlp) + shift_mlp).astype(jnp.bfloat16)
    pre_act = (
        jnp.dot(mlp_input, fc1_low, preferred_element_type=jnp.float32)
        + bias_full[3 * model_width : 3 * model_width + hidden_width]
    )
    hidden_full, gelu_back = jax.vjp(partial(jax.nn.gelu, approximate=True), pre_act)
    hidden = hidden_full.astype(jnp.bfloat16)
    branch = (
        jnp.dot(hidden, fc2_low, preferred_element_type=jnp.float32)
        + bias_full[3 * model_width + hidden_width :]
    )
    block_out = (residual_mid + gate_mlp * branch).astype(jnp.bfloat16)
    upstream = out_grad.astype(jnp.float32)
    branch_grad = (gate_mlp * upstream).astype(jnp.bfloat16)
    gate_mlp_grad = upstream * branch
    grad_fc2 = jnp.einsum("tf,td->fd", hidden, branch_grad, preferred_element_type=jnp.float32)
    bias_fc2_grad = jnp.sum(branch_grad.astype(jnp.float32), axis=0)
    hidden_grad = jnp.einsum("td,fd->tf", branch_grad, fc2_low, preferred_element_type=jnp.float32)
    pre_grad = gelu_back(hidden_grad)[0].astype(jnp.bfloat16)
    grad_fc1 = jnp.einsum("td,tf->df", mlp_input, pre_grad, preferred_element_type=jnp.float32)
    bias_fc1_grad = jnp.sum(pre_grad.astype(jnp.float32), axis=0)
    mlp_grad = jnp.einsum("tf,df->td", pre_grad, fc1_low, preferred_element_type=jnp.float32)
    scale_mlp_grad = mlp_grad * second_norm
    middle_grad = upstream + normalize_back(
        mlp_grad * (1.0 + scale_mlp), second_norm, second_inverse
    )
    attn_grad = (gate_attn * middle_grad).astype(jnp.bfloat16)
    gate_attn_grad = middle_grad * attn_out
    grad_proj = jnp.einsum("tc,td->cd", mixture, attn_grad, preferred_element_type=jnp.float32)
    bias_proj_grad = jnp.sum(attn_grad.astype(jnp.float32), axis=0)
    mixture_grad = jnp.einsum(
        "td,cd->tc", attn_grad, proj_low, preferred_element_type=jnp.float32
    ).astype(jnp.bfloat16)
    query_grad, key_grad, value_grad = attend_backward(
        query_heads,
        key_heads,
        value_heads,
        segments,
        log_totals,
        mixture_grad.reshape(head_shape),
        block_rows,
    )
    joint_grad = jnp.concatenate([query_grad, key_grad, value_grad], axis=1)
    grad_qkv = jnp.einsum("tc,te->ce", attn_input, joint_grad, preferred_element_type=jnp.float32)
    bias_query_grad = jnp.sum(query_grad.astype(jnp.float32), axis=0)
    bias_value_grad = jnp.sum(value_grad.astype(jnp.float32), axis=0)
    input_grad = jnp.einsum("te,ce->tc", joint_grad, qkv_low, preferred_element_type=jnp.float32)
    scale_attn_grad = input_grad * first_norm
    x_grad = middle_grad + normalize_back(
        input_grad * (1.0 + scale_attn), first_norm, first_inverse
    )
    token_mod_grad = jnp.concatenate(
        [input_grad, scale_attn_grad, gate_attn_grad, mlp_grad, scale_mlp_grad, gate_mlp_grad],
        axis=1,
    )
    slot_mod_grad = jnp.einsum(
        "ts,tc->sc", chooser.astype(jnp.float32), token_mod_grad, precision=lax.Precision.HIGHEST
    ).astype(jnp.bfloat16)
    half_grad = lax.all_to_all(slot_mod_grad, "mod", split_axis=1, concat_axis=0, tiled=True)
    grad_ada = jnp.einsum("ic,io->co", silu_low, half_grad, preferred_element_type=jnp.float32)
    grad_adab = jnp.sum(half_grad.astype(jnp.float32), axis=0)
    silu_grad = lax.psum(
        jnp.einsum("io,co->ic", half_grad, ada_low, preferred_element_type=jnp.float32).astype(
            jnp.bfloat16
        ),
        "mod",
    ).astype(jnp.float32)
    cond_grad = silu_back(silu_grad)[0]
    grad_bias = jnp.concatenate(
        [bias_query_grad, bias_value_grad, bias_proj_grad, bias_fc1_grad, bias_fc2_grad]
    ).reshape(data_count, -1)
    rates = step_rates(tokens * data_count * pair_count)
    halves = (
        lax.psum_scatter(
            grad_qkv.astype(jnp.bfloat16), "mod", scatter_dimension=1, tiled=True
        ).astype(jnp.float32),
        lax.psum_scatter(
            grad_proj.astype(jnp.bfloat16), "mod", scatter_dimension=1, tiled=True
        ).astype(jnp.float32),
        lax.psum_scatter(
            grad_fc1.astype(jnp.bfloat16), "mod", scatter_dimension=1, tiled=True
        ).astype(jnp.float32),
        lax.psum_scatter(
            grad_fc2.astype(jnp.bfloat16), "mod", scatter_dimension=1, tiled=True
        ).astype(jnp.float32),
        lax.psum_scatter(
            grad_bias.astype(jnp.bfloat16), "mod", scatter_dimension=1, tiled=True
        ).astype(jnp.float32),
    )
    shard = (
        lax.psum_scatter(halves[0], "dp", scatter_dimension=0, tiled=True),
        lax.psum_scatter(halves[1], "dp", scatter_dimension=0, tiled=True),
        lax.psum_scatter(halves[2], "dp", scatter_dimension=0, tiled=True),
        lax.psum_scatter(halves[3], "dp", scatter_dimension=0, tiled=True),
        lax.psum_scatter(halves[4], "dp", scatter_dimension=0, tiled=True),
        lax.psum_scatter(grad_ada, "dp", scatter_dimension=0, tiled=True),
        lax.psum_scatter(grad_adab, "dp", scatter_dimension=0, tiled=True),
    )
    trunk = shard[0:5]
    ada_shard = shard[5]
    adab_shard = shard[6]
    states_out = []
    states_out.extend(nesterov(qkv_weight, qkv_moment, qkv_average, trunk[0], rates[0]))
    states_out.extend(nesterov(proj_weight, proj_moment, proj_average, trunk[1], rates[1]))
    states_out.extend(nesterov(fc1_weight, fc1_moment, fc1_average, trunk[2], rates[2]))
    states_out.extend(nesterov(fc2_weight, fc2_moment, fc2_average, trunk[3], rates[3]))
    states_out.extend(
        nesterov(bias_weight, bias_moment, bias_average, trunk[4].reshape(-1), rates[4])
    )
    states_out.extend(nesterov(ada_weight, ada_moment, ada_average, ada_shard, rates[5]))
    states_out.extend(
        nesterov(adab_weight, adab_moment, adab_average, adab_shard.reshape(1, -1), rates[6])
    )
    return (block_out, x_grad, cond_grad) + tuple(states_out)


def solution(mesh):
    placed = (
        P(("dp", "mod"), None),
        P("dp", None),
        P(("dp", "mod")),
        P(("dp", "mod"), None),
        P("dp", "mod"),
        P("dp", "mod"),
        P("dp", "mod"),
        P("dp", "mod"),
        P("dp", "mod"),
        P("dp", "mod"),
        P("dp", "mod"),
        P("dp", "mod"),
        P("dp", "mod"),
        P("dp", "mod"),
        P("dp", "mod"),
        P("dp", "mod"),
        P(("dp", "mod")),
        P(("dp", "mod")),
        P(("dp", "mod")),
        P("dp", "mod"),
        P("dp", "mod"),
        P("dp", "mod"),
        P("mod", "dp"),
        P("mod", "dp"),
        P("mod", "dp"),
    )
    return jax.shard_map(
        body,
        mesh=mesh,
        in_specs=placed,
        out_specs=(
            P(("dp", "mod"), None),
            P(("dp", "mod"), None),
            P("dp", None),
            P("dp", "mod"),
            P("dp", "mod"),
            P("dp", "mod"),
            P("dp", "mod"),
            P("dp", "mod"),
            P("dp", "mod"),
            P("dp", "mod"),
            P("dp", "mod"),
            P("dp", "mod"),
            P("dp", "mod"),
            P("dp", "mod"),
            P("dp", "mod"),
            P(("dp", "mod")),
            P(("dp", "mod")),
            P(("dp", "mod")),
            P("dp", "mod"),
            P("dp", "mod"),
            P("dp", "mod"),
            P("mod", "dp"),
            P("mod", "dp"),
            P("mod", "dp"),
        ),
        check_vma=False,
    )
```

profile of v0, /device:TPU:0, one launch (start us, length us, event | category | flops | bytes accessed | tf_op | source)
XLA Modules:
  0.0 1695.3 jit_solution(17952873754723075779)
XLA Ops:
  10.5 9.8 all-gather.3
  29.5 9.0 all_gather.44
  38.7 8.8 all-gather.5
  59.4 58.9 %all-reduce.8 = (bf16[3456]{0:T(1024)(128)(2,1)S(1)}, bf16[9216]{0:T(1024)(128)(2,1)S(1)}) all-reduce(bf16[3456]{0:T(1024)(128)(2,1)S(1)} %dynamic-update-slice, bf16[9216]{0:T(1024)(128)(2,1)S(1)} %dynamic-update-slice.2), channel_id=2, replica_groups=mesh['dp'=16,'mod'=2] {'dp'}, use_global_device_ids=true, to_apply=%add | all-reduce | flops 12672 | bytes 50688
  132.2 11.4 fusion.66
  149.4 10.2 all-gather.14.cloned.1.call-done
  159.6 13.0 fusion.91
  182.6 9.6 reshape.288
  199.6 96.7 %while.27 = (s32[]{:T(128)}, bf16[2,512,16,72]{1,3,2,0:T(8,128)(2,1)S(1)}, f32[2,16,512]{2,1,0:T(8,128)S(1)}, s32[2,512]{1,0:T(2,128)S(1)}, s32[1024]{0:T(1024)S...) while((s32[]{:T(128)}, ...), condition=%wide.region_5.6_spmd, body=%wide.region_2.5_spmd.sunk | while | flops 2517688320 | bytes 110110832 | solution.py:78
  200.5 16.5 fusion.144
  217.0 15.1 fusion.145
  232.1 16.5 fusion.146
  249.0 16.1 fusion.144
  265.1 15.3 fusion.145
  280.5 15.6 fusion.146
  300.8 12.1 fusion.88
  324.2 19.6 %fusion.92 = f32[1024,4608]{1,0:T(8,128)} fusion(bf16[1024,1152]{1,0:T(8,128)(2,1)} %fusion.59, bf16[1152,4608]{1,0:T(8,128)(2,1)} %all-gather.18.cloned.1.call-done), kind=kOutput, calls=%fused_computation.176 | convolution fusion | flops 10871635968 | bytes 31850496 | tf_op jit(solution)/shard_map/dot_general | solution.py:225
  343.8 39.4 %all-gather.20.cloned.1.call-done = bf16[4608,1152]{1,0:T(8,128)(2,1)} async-done(((bf16[288,1152]{1,0:T(8,128)(2,1)}), bf16[4608,1152]{1,0:T(8,128)(2,1)}) %all-gather.20.cloned.1.call-update) | async-done | bytes 10616848 | tf_op jit(solution)/shard_map/all_gather | solution.py:181
  383.2 21.9 %convolution_add_fusion = f32[1024,1152]{1,0:T(8,128)} fusion(bf16[4608,1152]{1,0:T(8,128)(2,1)} %all-gather.20.cloned.1.call-done, f32[1152]{0:T(1024)S(1)} %copy-done.52, f32[1024,4608]{1,0:T(8,128)} %fusion.92, f32[4608]{0:T(1024)S(1)} %copy-done.45), kind=kOutput, calls=%fused_computation.76 | convolution fusion | flops 10920001536 | bytes 34232832 | tf_op jit(solution)/shard_map/dot_general | solution.py:231
  405.2 29.4 %fusion.84 = (bf16[4608]{0:T(1024)(128)(2,1)}, bf16[1024,4608]{1,0:T(8,128)(2,1)}) fusion(f32[1024,4608]{1,0:T(8,128)} %fusion.92, f32[4608]{0:T(1024)S(1)} %copy-done.45, bf16[1024,1152]{1,0:T(8,128)(2,1)S(1)} %copy-done.20, bf16[4608,1152]{1,0:T(8,128)(2,1)} %all-gather.20.cloned.1.call-done), kind=kOutput, calls=%fused_computation.169 | convolution fusion | flops 10975440896 | bytes 41315328 | tf_op jit(solution)/shard_map/td,fd->tf/dot_general | solution.py:240
  434.6 21.0 %fusion.80 = (f32[1024]{0:T(1024)S(1)}, f32[1024]{0:T(1024)S(1)}, bf16[1024,1152]{1,0:T(8,128)(2,1)}, f32[1024,1152]{1,0:T(8,128)S(1)}) fusion(f32[1024,6912]{1,0:T(8,128)} %fusion.66, f32[1024]{0:T(1024)S(1)} %add_rsqrt_fusion, f32[1024,1152]{1,0:T(8,128)S(1)} %bitcast.165, f32[1024]{0:T(1024)S(1)} %broadcast_multiply_fusion.4, ...), kind=kOutput, calls=%fused_computation.166 | convolution fusion | flops 10883430400 | bytes 46022656 | tf_op jit(solution)/shard_map/tf,df->td/dot_general | solution.py:244
  455.6 9.3 fusion.86
  487.2 220.4 %while.28 = (s32[]{:T(128)}, f32[1024,16,72]{0,2,1:T(8,128)}, f32[1024,16,72]{0,2,1:T(8,128)}, bf16[2,512,16,72]{1,3,2,0:T(8,128)(2,1)}, bf16[2,512,16,72]{1,3,2...) while((s32[]{:T(128)}, f32[1024,16,72]{0,2,1:T(8,128)}, ...), condition=%wide.region_12.13_spmd.clone, body=%wide.region_10.12_spmd.clone.sunk | while | flops 6173220864 | bytes 352954528 | solution.py:119
  487.8 17.7 %fusion.156 = f32[16,512,1024]{2,1,0:T(8,128)} fusion(bf16[1024,16,72]{0,2,1:T(8,128)(2,1)} %get-tuple-element.580, bf16[2,512,16,72]{1,3,2,0:T(8,128)(2,1)} %get-tuple-element.577, s32[]{:T(128)S(6)} %copy.169), kind=kOutput, calls=%fused_computation.33.clone.1 | convolution fusion | flops 1207959552 | bytes 37093380 | tf_op jit(solution)/shard_map/while/body/eval_jaxpr/qhd,khd->hqk/dot_general | solution.py:54
  505.4 17.8 %bitcast_add_fusion.5 = f32[1024,16,72]{0,2,1:T(8,128)} fusion(f32[1024,16,72]{0,2,1:T(8,128)} %get-tuple-element.562, pred[]{:T(512)S(6)} %compare.3, f32[16,512,1024]{2,1,0:T(8,128)} %fusion.156, f32[16,512]{1,0:T(8,128)S(1)} %dynamic-slice_bitcast_fusion.2, pred[512,1024]{1,0:T(8,128)(4,1)S(1)} %broadcast_compare_fusion.5, ...), kind=kOutput, calls=%fused_computation.24.clone.1 | convolution fusion | flops 1243873280 | bytes 44728324 | tf_op jit(solution)/shard_map/while/body/eval_jaxpr/hqk,qhd->khd/dot_general | solution.py:99
  523.2 26.5 %multiply_reduce_fusion.4 = (f32[16,512]{1,0:T(8,128)S(1)}, f32[16,512,1024]{2,1,0:T(8,128)}) fusion(f32[16,512,1024]{2,1,0:T(8,128)} %fusion.156, f32[16,512]{1,0:T(8,128)S(1)} %dynamic-slice_bitcast_fusion.2, pred[512,1024]{1,0:T(8,128)(4,1)S(1)} %broadcast_compare_fusion.5, bf16[1024,16,72]{0,2,1:T(8,128)(2,1)} %get-tuple-element.583, ...), kind=kOutput, calls=%fused_computation.19.clone.1 | convolution fusion | flops 1249894400 | bytes 71237632 | tf_op jit(solution)/shard_map/while/body/eval_jaxpr/qhd,khd->hqk/dot_general | solution.py:102
  549.7 27.8 %multiply_convert_fusion.8 = bf16[16,512,1024]{2,1,0:T(8,128)(2,1)} fusion(f32[16,512,1024]{2,1,0:T(8,128)} %get-tuple-element.518, f32[16,512,1024]{2,1,0:T(8,128)} %fusion.156, f32[16,512]{1,0:T(8,128)S(1)} %get-tuple-element.519, f32[16,512]{1,0:T(8,128)S(1)} %dynamic-slice_bitcast_fusion.2, pred[512,1024]{1,0:T(8,128)(4,1)S(1)} %broadcast_compare_fusion.5), kind=kLoop, calls=%fused_computation.18.clone.1 | loop fusion | flops 50331648 | bytes 84475904 | tf_op jit(solution)/shard_map/while/body/eval_jaxpr/convert_element_type | solution.py:106
  577.5 10.4 fusion.157
  596.3 17.7 %fusion.156 = f32[16,512,1024]{2,1,0:T(8,128)} fusion(bf16[1024,16,72]{0,2,1:T(8,128)(2,1)} %get-tuple-element.580, bf16[2,512,16,72]{1,3,2,0:T(8,128)(2,1)} %get-tuple-element.577, s32[]{:T(128)S(6)} %copy.169), kind=kOutput, calls=%fused_computation.33.clone.1 | convolution fusion | flops 1207959552 | bytes 37093380 | tf_op jit(solution)/shard_map/while/body/eval_jaxpr/qhd,khd->hqk/dot_general | solution.py:54
  614.0 19.1 %bitcast_add_fusion.5 = f32[1024,16,72]{0,2,1:T(8,128)} fusion(f32[1024,16,72]{0,2,1:T(8,128)} %get-tuple-element.562, pred[]{:T(512)S(6)} %compare.3, f32[16,512,1024]{2,1,0:T(8,128)} %fusion.156, f32[16,512]{1,0:T(8,128)S(1)} %dynamic-slice_bitcast_fusion.2, pred[512,1024]{1,0:T(8,128)(4,1)S(1)} %broadcast_compare_fusion.5, ...), kind=kOutput, calls=%fused_computation.24.clone.1 | convolution fusion | flops 1243873280 | bytes 44728324 | tf_op jit(solution)/shard_map/while/body/eval_jaxpr/hqk,qhd->khd/dot_general | solution.py:99
  633.1 26.4 %multiply_reduce_fusion.4 = (f32[16,512]{1,0:T(8,128)S(1)}, f32[16,512,1024]{2,1,0:T(8,128)}) fusion(f32[16,512,1024]{2,1,0:T(8,128)} %fusion.156, f32[16,512]{1,0:T(8,128)S(1)} %dynamic-slice_bitcast_fusion.2, pred[512,1024]{1,0:T(8,128)(4,1)S(1)} %broadcast_compare_fusion.5, bf16[1024,16,72]{0,2,1:T(8,128)(2,1)} %get-tuple-element.583, ...), kind=kOutput, calls=%fused_computation.19.clone.1 | convolution fusion | flops 1249894400 | bytes 71237632 | tf_op jit(solution)/shard_map/while/body/eval_jaxpr/qhd,khd->hqk/dot_general | solution.py:102
  659.5 27.8 %multiply_convert_fusion.8 = bf16[16,512,1024]{2,1,0:T(8,128)(2,1)} fusion(f32[16,512,1024]{2,1,0:T(8,128)} %get-tuple-element.518, f32[16,512,1024]{2,1,0:T(8,128)} %fusion.156, f32[16,512]{1,0:T(8,128)S(1)} %get-tuple-element.519, f32[16,512]{1,0:T(8,128)S(1)} %dynamic-slice_bitcast_fusion.2, pred[512,1024]{1,0:T(8,128)(4,1)S(1)} %broadcast_compare_fusion.5), kind=kLoop, calls=%fused_computation.18.clone.1 | loop fusion | flops 50331648 | bytes 84475904 | tf_op jit(solution)/shard_map/while/body/eval_jaxpr/convert_element_type | solution.py:106
  687.3 10.4 fusion.157
  717.1 17.0 %convolution_convert_fusion.2 = bf16[1152,3456]{0,1:T(8,128)(2,1)} fusion(bf16[1024,1152]{1,0:T(8,128)(2,1)S(1)} %copy-done.19, bf16[1024,1152]{0,1:T(8,128)(2,1)S(1)} %bitcast.177, bf16[1024,1152]{0,1:T(8,128)(2,1)S(1)} %bitcast.175, bf16[1024,1152]{0,1:T(8,128)(2,1)S(1)} %bitcast.181), kind=kOutput, calls=%fused_computation.60 | convolution fusion | flops 8178941952 | bytes 17399808 | tf_op jit(solution)/shard_map/tc,te->ce/dot_general | solution.py:266
  734.8 19.7 %convolution_convert_fusion = bf16[4608,1152]{0,1:T(8,128)(2,1)} fusion(bf16[1024,1152]{1,0:T(8,128)(2,1)} %get-tuple-element.361, f32[1024,4608]{1,0:T(8,128)} %fusion.92, f32[4608]{0:T(1024)S(1)} %copy-done.46), kind=kOutput, calls=%fused_computation.50 | convolution fusion | flops 10924130304 | bytes 31868928 | tf_op jit(solution)/shard_map/tf,td->fd/dot_general | solution.py:238
  754.6 17.0 %convolution_convert_fusion.1 = bf16[1152,4608]{1,0:T(8,128)(2,1)} fusion(bf16[1024,1152]{1,0:T(8,128)(2,1)} %fusion.59, bf16[1024,4608]{1,0:T(8,128)(2,1)} %get-tuple-element.363), kind=kOutput, calls=%fused_computation.51 | convolution fusion | flops 10876944384 | bytes 22413312 | tf_op jit(solution)/shard_map/td,tf->df/dot_general | solution.py:242
  774.8 16.6 constant_dynamic-update-slice_fusion.1
  802.8 9.4 fusion.55
  831.6 13.9 convolution_convert_fusion.3
  867.6 85.8 %reduce-scatter.27.cloned.1.call-done = bf16[4608,576]{0,1:T(8,128)(2,1)} async-done(((bf16[4608,1152]{0,1:T(8,128)(2,1)}), bf16[4608,576]{0,1:T(8,128)(2,1)}) %reduce-scatter.27.cloned.1.call-update) | async-done | bytes 5308432 | tf_op jit(solution)/shard_map/reduce_scatter | solution.py:305
  953.4 8.8 copy.142
  962.2 116.8 %reduce-scatter.23.cloned.1.call-done = bf16[1152,2304]{1,0:T(8,128)(2,1)} async-done(((bf16[1152,4608]{1,0:T(8,128)(2,1)}), bf16[1152,2304]{1,0:T(8,128)(2,1)}) %reduce-scatter.23.cloned.1.call-update) | async-done | bytes 5308432 | tf_op jit(solution)/shard_map/reduce_scatter | solution.py:302
  1114.0 19.0 %reduce-scatter.21.cloned.1.call-done = bf16[1152,576]{0,1:T(8,128)(2,1)} async-done(((bf16[1152,1152]{0,1:T(8,128)(2,1)}), bf16[1152,576]{0,1:T(8,128)(2,1)}) %reduce-scatter.21.cloned.1.call-update) | async-done | bytes 1327120 | tf_op jit(solution)/shard_map/reduce_scatter | solution.py:299
  1133.0 90.1 %all-reduce.10 = (f32[1152,576]{0,1:T(8,128)}, f32[16,288]{1,0:T(8,128)S(1)}, f32[3456]{0:T(1024)S(1)}) all-reduce(bf16[1152,576]{0,1:T(8,128)(2,1)} %reduce-scatter.21.cloned.1.call-done, bf16[16,288]{1,0:T(8,128)(2,1)S(1)} %copy.145, f32[3456]{0:T(1024)S(1)} %convert_reduce_fusion.1), channel_id=8, replica_groups=mesh['dp'=16,'mod'=2] {'dp'}, use_global_device_ids=true, to_apply=%region_19.20.clone | all-reduce | flops 671616 | bytes 4036608
  1232.6 89.3 %reduce-scatter.35.cloned.1.call-done = f32[72,3456]{1,0:T(8,128)} async-done(((f32[1152,3456]{1,0:T(8,128)}), f32[72,3456]{1,0:T(8,128)}) %reduce-scatter.35.cloned.1.call-update) | async-done | bytes 995344
  1325.6 103.9 %reduce-scatter.29.cloned.1.call-done = f32[72,1728]{1,0:T(8,128)} async-done(((f32[1152,1728]{1,0:T(8,128)}), f32[72,1728]{1,0:T(8,128)}) %reduce-scatter.29.cloned.1.call-update) | async-done | bytes 497680
  1442.2 119.8 %reduce-scatter.31.cloned.1.call-done = f32[288,576]{1,0:T(8,128)} async-done(((f32[4608,576]{1,0:T(8,128)}), f32[288,576]{1,0:T(8,128)}) %reduce-scatter.31.cloned.1.call-update) | async-done | bytes 663568
  1574.5 111.5 %reduce-scatter.25.cloned.1.call-done = f32[72,2304]{1,0:T(8,128)} async-done(((f32[1152,2304]{1,0:T(8,128)}), f32[72,2304]{1,0:T(8,128)}) %reduce-scatter.25.cloned.1.call-update) | async-done | bytes 663568 | tf_op jit(solution)/shard_map/reduce_scatter | solution.py:315
  (314 shorter events, 257.1 us)
Async XLA Ops:
  7.2 111.7 %all-gather.12.cloned.1.call-start = ((), (), s32[]{:S(2)}) async-start(), calls=%async_computation.11 | async-start | bytes 8460288 | tf_op jit(solution)/shard_map/all_gather | solution.py:183
  9.3 29.3 %copy-start.10 = (f32[288,576]{1,0:T(8,128)S(1)}, f32[288,576]{1,0:T(8,128)}, u32[]{:S(2)}) copy-start(f32[288,576]{1,0:T(8,128)} %param.42) | copy-start | bytes 1990660
  9.4 150.3 %all-gather.14.cloned.1.call-start = ((), (), s32[]{:S(2)}) async-start(), calls=%async_computation.12 | async-start | bytes 8460288 | tf_op jit(solution)/shard_map/all_gather | solution.py:178
  22.0 278.8 %all-gather.16.cloned.1.call-start = ((), (), s32[]{:S(2)}) async-start(), calls=%async_computation.13 | async-start | bytes 2820096 | tf_op jit(solution)/shard_map/all_gather | solution.py:179
  27.3 22.1 %copy-start.62 = (u32[32]{0:T(128)S(1)}, u32[32]{0:T(128)}, u32[]{:S(2)}) copy-start(u32[32]{0:T(128)} %constant.132) | copy-start | bytes 388
  27.3 22.7 %copy-start.56 = (u32[32]{0:T(128)S(1)}, u32[32]{0:T(128)}, u32[]{:S(2)}) copy-start(u32[32]{0:T(128)} %constant.127) | copy-start | bytes 388
  27.3 24.6 %copy-start.57 = (f32[1,216]{1,0:T(1,128)S(1)}, f32[1,216]{1,0:T(1,128)}, u32[]{:S(2)}) copy-start(f32[1,216]{1,0:T(1,128)} %param.51) | copy-start | bytes 2596
  27.3 24.6 %copy-start.50 = (f32[288]{0:T(512)S(1)}, f32[288]{0:T(512)}, u32[]{:S(2)}) copy-start(f32[288]{0:T(512)} %param.45) | copy-start | bytes 3460
  27.3 30.4 %copy-start.3 = (bf16[1024,1152]{1,0:T(8,128)(2,1)S(1)}, bf16[1024,1152]{1,0:T(8,128)(2,1)}, u32[]{:S(2)}) copy-start(bf16[1024,1152]{1,0:T(8,128)(2,1)} %param.29) | copy-start | bytes 7077892
  28.3 295.9 %all-gather.18.cloned.1.call-start = ((), (), s32[]{:S(2)}) async-start(), calls=%async_computation.14 | async-start | bytes 11280384 | tf_op jit(solution)/shard_map/all_gather | solution.py:180
  38.5 344.7 %all-gather.20.cloned.1.call-start = ((), (), s32[]{:S(2)}) async-start(), calls=%async_computation.15 | async-start | bytes 11280384 | tf_op jit(solution)/shard_map/all_gather | solution.py:181
  38.6 80.2 %copy-start.31 = (bf16[8,1152]{1,0:T(8,128)(2,1)S(1)}, bf16[8,1152]{1,0:T(8,128)(2,1)}, u32[]{:S(2)}) copy-start(bf16[8,1152]{1,0:T(8,128)(2,1)} %param.30) | copy-start | bytes 55300
  58.1 85.6 %copy-start.39 = (f32[1024]{0:T(1024)}, f32[1024]{0:T(1024)S(1)}, u32[]{:S(2)}) copy-start(f32[1024]{0:T(1024)S(1)} %broadcast_multiply_fusion.5) | copy-start | bytes 12292
  124.9 7.3 all-to-all-start
  128.2 732.2 %reduce-scatter.19.cloned.1.call-start = ((), (), s32[]{:S(2)}) async-start(), calls=%async_computation.16 | async-start | bytes 11943936 | tf_op jit(solution)/shard_map/reduce_scatter | solution.py:296
  300.7 16.7 copy-start.1
  312.8 142.8 %copy-start.37 = (f32[1024]{0:T(1024)}, f32[1024]{0:T(1024)S(1)}, u32[]{:S(2)}) copy-start(f32[1024]{0:T(1024)S(1)} %broadcast_multiply_fusion.4) | copy-start | bytes 12292
  317.4 138.2 %copy-start.41 = (f32[1024]{0:T(1024)}, f32[1024]{0:T(1024)S(1)}, u32[]{:S(2)}) copy-start(f32[1024]{0:T(1024)S(1)} %add_rsqrt_fusion) | copy-start | bytes 12292
  324.2 59.0 %copy-start.45 = (f32[4608]{0:T(1024)S(1)}, f32[4608]{0:T(1024)}, u32[]{:S(2)}) copy-start(f32[4608]{0:T(1024)} %slice.94) | copy-start | bytes 55300
  324.2 59.0 %copy-start.52 = (f32[1152]{0:T(1024)S(1)}, f32[1152]{0:T(1024)}, u32[]{:S(2)}) copy-start(f32[1152]{0:T(1024)} %get-tuple-element.384) | copy-start | bytes 13828
  383.2 22.0 %copy-start.20 = (bf16[1024,1152]{1,0:T(8,128)(2,1)S(1)}, bf16[1024,1152]{1,0:T(8,128)(2,1)}, u32[]{:S(2)}) copy-start(bf16[1024,1152]{1,0:T(8,128)(2,1)} %get-tuple-element.361) | copy-start | bytes 7077892
  383.2 51.4 %slice-start = ((s8[4718592]{0:T(1024)(128)(4,1)}), s8[4194304]{0:T(1024)(128)(4,1)S(1)}, s32[]{:S(2)}) async-start(s8[4718592]{0:T(1024)(128)(4,1)} %bitcast.164), calls=%async_computation.25 | async-start | bytes 8388608
  405.1 29.4 %slice-start.1 = ((s8[4718592]{0:T(1024)(128)(4,1)}), s8[524288]{0:T(1024)(128)(4,1)S(1)}, s32[]{:S(2)}) async-start(s8[4718592]{0:T(1024)(128)(4,1)} %bitcast.164), calls=%async_computation.26 | async-start | bytes 1048576
  734.1 219.3 %reduce-scatter.27.cloned.1.call-start = ((), (), s32[]{:S(2)}) async-start(), calls=%async_computation.20 | async-start | bytes 15925248 | tf_op jit(solution)/shard_map/reduce_scatter | solution.py:305
  754.5 324.5 %reduce-scatter.23.cloned.1.call-start = ((), (), s32[]{:S(2)}) async-start(), calls=%async_computation.18 | async-start | bytes 15925248 | tf_op jit(solution)/shard_map/reduce_scatter | solution.py:302
  771.6 341.4 %reduce-scatter.33.cloned.1.call-start = ((), (), s32[]{:S(2)}) async-start(), calls=%async_computation.23 | async-start | bytes 221184
  774.8 16.6 copy-start.4
  774.8 16.6 copy-start.40
  774.8 16.6 copy-start.44
  796.9 26.7 %slice-start.2 = ((s8[4718592]{0:T(1024)(128)(4,1)}), s8[524288]{0:T(1024)(128)(4,1)S(1)}, s32[]{:S(2)}) async-start(s8[4718592]{0:T(1024)(128)(4,1)} %bitcast.166), calls=%async_computation.27 | async-start | bytes 1048576
  801.8 331.3 %reduce-scatter.21.cloned.1.call-start = ((), (), s32[]{:S(2)}) async-start(), calls=%async_computation.17 | async-start | bytes 3981312 | tf_op jit(solution)/shard_map/reduce_scatter | solution.py:299
  802.4 519.5 %reduce-scatter.35.cloned.1.call-start = ((), (), s32[]{:S(2)}) async-start(), calls=%async_computation.24 | async-start | bytes 16920576
  802.8 20.8 %slice-start.3 = ((s8[4718592]{0:T(1024)(128)(4,1)}), s8[4194304]{0:T(1024)(128)(4,1)S(1)}, s32[]{:S(2)}) async-start(s8[4718592]{0:T(1024)(128)(4,1)} %bitcast.166), calls=%async_computation.28 | async-start | bytes 8388608
  831.6 21.0 %copy-start.32 = (bf16[8,1152]{1,0:T(8,128)(2,1)S(1)}, bf16[8,1152]{1,0:T(8,128)(2,1)}, u32[]{:S(2)}) copy-start(bf16[8,1152]{1,0:T(8,128)(2,1)} %param.30) | copy-start | bytes 55300
  860.3 569.1 %reduce-scatter.29.cloned.1.call-start = ((), (), s32[]{:S(2)}) async-start(), calls=%async_computation.21 | async-start | bytes 8773632
  867.5 694.4 %reduce-scatter.31.cloned.1.call-start = ((), (), s32[]{:S(2)}) async-start(), calls=%async_computation.22 | async-start | bytes 12533760
  962.2 723.8 %reduce-scatter.25.cloned.1.call-start = ((), (), s32[]{:S(2)}) async-start(), calls=%async_computation.19 | async-start | bytes 11280384 | tf_op jit(solution)/shard_map/reduce_scatter | solution.py:315
  1098.6 132.8 %copy-start.58 = (f32[1,216]{1,0:T(1,128)S(1)}, f32[1,216]{1,0:T(1,128)}, u32[]{:S(2)}) copy-start(f32[1,216]{1,0:T(1,128)} %param.51) | copy-start | bytes 2596
  1098.6 132.8 %copy-start.59 = (f32[1,216]{1,0:T(1,128)S(1)}, f32[1,216]{1,0:T(1,128)}, u32[]{:S(2)}) copy-start(f32[1,216]{1,0:T(1,128)} %param.53) | copy-start | bytes 2596
  1098.6 132.8 %copy-start.60 = (f32[1,216]{1,0:T(1,128)S(1)}, f32[1,216]{1,0:T(1,128)}, u32[]{:S(2)}) copy-start(f32[1,216]{1,0:T(1,128)} %param.52) | copy-start | bytes 2596
  1098.6 133.4 %copy-start.51 = (f32[288]{0:T(512)S(1)}, f32[288]{0:T(512)}, u32[]{:S(2)}) copy-start(f32[288]{0:T(512)} %param.45) | copy-start | bytes 3460
  1098.6 133.4 %copy-start.54 = (f32[288]{0:T(512)S(1)}, f32[288]{0:T(512)}, u32[]{:S(2)}) copy-start(f32[288]{0:T(512)} %param.47) | copy-start | bytes 3460
  1098.7 133.4 %copy-start.55 = (f32[288]{0:T(512)S(1)}, f32[288]{0:T(512)}, u32[]{:S(2)}) copy-start(f32[288]{0:T(512)} %param.46) | copy-start | bytes 3460
  1098.7 223.3 %copy-start.8 = (f32[72,3456]{1,0:T(8,128)S(1)}, f32[72,3456]{1,0:T(8,128)}, u32[]{:S(2)}) copy-start(f32[72,3456]{1,0:T(8,128)} %param.48) | copy-start | bytes 2985988
  1431.7 132.6 %copy-start.9 = (f32[288,576]{0,1:T(8,128)S(1)}, f32[288,576]{0,1:T(8,128)}, u32[]{:S(2)}) copy-start(f32[288,576]{0,1:T(8,128)} %copy.126) | copy-start | bytes 1990660
  1564.3 121.7 %copy-start.12 = (f32[72,2304]{1,0:T(8,128)S(1)}, f32[72,2304]{1,0:T(8,128)}, u32[]{:S(2)}) copy-start(f32[72,2304]{1,0:T(8,128)} %param.39) | copy-start | bytes 1990660
  1567.3 118.7 %copy-start.26 = (f32[72,2304]{1,0:T(8,128)S(1)}, f32[72,2304]{1,0:T(8,128)}, u32[]{:S(2)}) copy-start(f32[72,2304]{1,0:T(8,128)} %param.41) | copy-start | bytes 1990660
  1567.3 118.7 %copy-start.27 = (f32[72,2304]{1,0:T(8,128)S(1)}, f32[72,2304]{1,0:T(8,128)}, u32[]{:S(2)}) copy-start(f32[72,2304]{1,0:T(8,128)} %param.40) | copy-start | bytes 1990660
  (39 other events, 220.4 us)
Sparse Core Ops, SparseCore 0:
  10.8 75.2 all-gather.11
  88.8 70.7 all-gather.13
  162.4 41.6 all-gather.15
  206.2 87.3 all-gather.17
  296.3 86.8 all-gather.19
  734.2 92.8 reduce-scatter.18
  829.5 123.8 reduce-scatter.26
  955.7 123.2 reduce-scatter.22
  1081.9 10.4 reduce-scatter.32
  1094.5 38.4 reduce-scatter.20
  1137.7 184.1 reduce-scatter.34
  1326.4 103.0 reduce-scatter.28
  1434.1 127.7 reduce-scatter.30
  1565.9 120.0 reduce-scatter.24
where the time goes:
time: 1700 us
  waiting for transfers between devices  699 us (41%)
  matrix products  467 us (27%)
  blocking collectives  201 us (12%)
  other arithmetic  175 us (10%)
  local copies, waits for them, and re-layouts  129 us (8%)
  between operations  18.1 us (1%)
    unnamed x18, waiting for transfers between devices  314 us
    unnamed x3, blocking collectives  154 us
    reduce_scatter x1, waiting for transfers between devices, body(): lax.psum_scatter(grad_fc1.astype(jnp.bfloat16), 'mod', scatter_dimension=...  117 us
    reduce_scatter x1, waiting for transfers between devices, body(): lax.psum_scatter(halves[2], 'dp', scatter_dimension=0, tiled=True)  111 us
    reduce_scatter x1, waiting for transfers between devices, body(): lax.psum_scatter(grad_fc2.astype(jnp.bfloat16), 'mod', scatter_dimension=...  85.8 us
    unnamed x184, local copies, waits for them, and re-layouts  83.5 us
    dot_general x4, matrix products, masked_scores(): jnp.einsum('qhd,khd->hqk', query_part, key_rows, preferred_element_type=j...  68 us
    convert_element_type x2, other arithmetic, one_block(): score_grad = (softmax * centred).astype(jnp.bfloat16)  55.6 us
  transfers between devices with their start and end apart: 15, of which 10 were waited for; matrix products, arithmetic and copies ran while one was open for 24% of the time, Pallas kernels for 0%

commit v1 on v0

v1 whole, which is shorter than its diff:
```python
from functools import partial

import jax
import jax.numpy as jnp
from jax import lax
from jax.sharding import Mesh
from jax.sharding import PartitionSpec as P

D = 1152
HEADS = 16
FF = 4608


EPS = 1e-06
MOMENTUM = 0.9
DECAY = 0.5


def normalize(values):
    centre = values - jnp.mean(values, axis=-1, keepdims=True)
    inverse = lax.rsqrt(jnp.mean(centre * centre, axis=-1, keepdims=True) + EPS)
    return (centre * inverse, inverse)


def normalize_back(upstream, normed, inverse):
    return inverse * (
        upstream
        - jnp.mean(upstream, axis=-1, keepdims=True)
        - normed * jnp.mean(upstream * normed, axis=-1, keepdims=True)
    )


def step_rates(tokens_all):
    base_rate = tokens_all ** (-0.5)
    return (
        2.5 * D ** (-0.5) * base_rate,
        3.0 * D ** (-0.5) * base_rate,
        3.3 * D ** (-0.5) * base_rate,
        2.8 * FF ** (-0.5) * base_rate,
        0.5 * base_rate,
        2.0 * D ** (-0.5) * base_rate,
        0.3 * base_rate,
    )


def nesterov(weight, moment, average, gradient, rate):
    moment = MOMENTUM * moment + gradient
    weight = weight - rate * (gradient + MOMENTUM * moment)
    average = DECAY * average + (1.0 - DECAY) * weight
    return (weight, moment, average)


def masked_scores(query_part, seg_part, key_rows, segments, scaling):
    scores = (
        jnp.einsum("qhd,khd->hqk", query_part, key_rows, preferred_element_type=jnp.float32)
        * scaling
    )
    allowed = seg_part[:, None] == segments[None, :]
    return jnp.where(allowed[None], scores, -1e30)


def attend_forward(query_rows, key_rows, value_rows, segments, block_rows):
    tokens, head_count, head_width = query_rows.shape
    scaling = head_width ** (-0.5)
    blocks = tokens // block_rows

    def one_block(inputs):
        query_part, seg_part = inputs
        scores = masked_scores(query_part, seg_part, key_rows, segments, scaling)
        largest = jnp.max(scores, axis=-1, keepdims=True)
        weights = jnp.exp(scores - largest)
        totals = jnp.sum(weights, axis=-1, keepdims=True)
        softmax_low = (weights / totals).astype(jnp.bfloat16)
        mixture = jnp.einsum(
            "hqk,khd->qhd", softmax_low, value_rows, preferred_element_type=jnp.float32
        )
        return (mixture.astype(jnp.bfloat16), (largest + jnp.log(totals))[..., 0])

    mixture, log_totals = lax.map(
        one_block,
        (
            query_rows.reshape(blocks, block_rows, head_count, head_width),
            segments.reshape(blocks, block_rows),
        ),
    )
    return (mixture.reshape(tokens, head_count * head_width), log_totals)


def attend_backward(query_rows, key_rows, value_rows, segments, log_totals, upstream, block_rows):
    tokens, head_count, head_width = query_rows.shape
    scaling = head_width ** (-0.5)
    blocks = tokens // block_rows

    def one_block(carried, inputs):
        key_grad, value_grad = carried
        query_part, seg_part, log_part, up_part = inputs
        scores = masked_scores(query_part, seg_part, key_rows, segments, scaling)
        softmax = jnp.exp(scores - log_part[..., None])
        softmax_low = softmax.astype(jnp.bfloat16)
        value_grad = value_grad + jnp.einsum(
            "hqk,qhd->khd", softmax_low, up_part, preferred_element_type=jnp.float32
        )
        prob_grad = jnp.einsum(
            "qhd,khd->hqk", up_part, value_rows, preferred_element_type=jnp.float32
        )
        centred = prob_grad - jnp.sum(softmax * prob_grad, axis=-1, keepdims=True)
        score_grad = (softmax * centred).astype(jnp.bfloat16)
        query_grad = (
            jnp.einsum("hqk,khd->qhd", score_grad, key_rows, preferred_element_type=jnp.float32)
            * scaling
        )
        key_grad = (
            key_grad
            + jnp.einsum("hqk,qhd->khd", score_grad, query_part, preferred_element_type=jnp.float32)
            * scaling
        )
        return ((key_grad, value_grad), query_grad.astype(jnp.bfloat16))

    zeroes = jnp.zeros(key_rows.shape, jnp.float32)
    carried, query_grad = lax.scan(
        one_block,
        (zeroes, zeroes),
        (
            query_rows.reshape(blocks, block_rows, head_count, head_width),
            segments.reshape(blocks, block_rows),
            log_totals,
            upstream.reshape(blocks, block_rows, head_count, head_width),
        ),
    )
    full_width = head_count * head_width
    return (
        query_grad.reshape(tokens, full_width),
        carried[0].reshape(tokens, full_width).astype(jnp.bfloat16),
        carried[1].reshape(tokens, full_width).astype(jnp.bfloat16),
    )


ROWS = ("far", "near", "core")
ALL = ("far", "near", "core", "mod")
LOW = jnp.bfloat16
WIDE = jnp.float32


def swap(values, axis):
    return lax.ppermute(values, axis, [(0, 1), (1, 0)])


def shifted(values, distance, count):
    return lax.ppermute(values, "far", [(i, (i + distance) % count) for i in range(count)])


def collect_far(shard):
    count = lax.axis_size("far")
    if count > 4:
        return lax.all_gather(shard, "far", axis=0)
    here = lax.axis_index("far")
    held = jnp.zeros((count,) + shard.shape, shard.dtype)
    held = lax.dynamic_update_index_in_dim(held, shard, here, 0)
    for distance in range(1, count):
        came = shifted(shard, distance, count)
        held = lax.dynamic_update_index_in_dim(held, came, (here - distance) % count, 0)
    return held


def gather_weight(shard, first):
    near, core, half = lax.axis_index("near"), lax.axis_index("core"), lax.axis_index("mod")
    own = collect_far(shard)
    if first == "near":
        by_near = swap(own, "near")
        by_mod = swap(own, "mod")
        by_both = swap(by_near, "mod")
    else:
        by_mod = swap(own, "mod")
        by_near = swap(own, "near")
        by_both = swap(by_mod, "near")
    count, rows, columns = own.shape
    whole = jnp.zeros((2, count, 2, 2, rows, columns), shard.dtype)
    for piece, n, m in ((own, 0, 0), (by_near, 1, 0), (by_mod, 0, 1), (by_both, 1, 1)):
        other = swap(piece, "core")
        for part, k in ((piece, 0), (other, 1)):
            whole = lax.dynamic_update_slice(
                whole, part[None, :, None, None], (half ^ m, 0, near ^ n, core ^ k, 0, 0)
            )
    return whole.reshape(2, count * 4 * rows, columns)


def scatter_gradient(left, right, first):
    count = lax.axis_size("far")
    here = lax.axis_index("far")
    near, core, half = lax.axis_index("near"), lax.axis_index("core"), lax.axis_index("mod")
    tokens = left.shape[0]
    blocks = left.reshape(tokens, count, 2, 2, -1)

    def piece(n, k, m):
        rows = lax.dynamic_index_in_dim(blocks, near ^ n, 2, False)
        rows = lax.dynamic_index_in_dim(rows, core ^ k, 2, False)
        columns = lax.dynamic_index_in_dim(right, half ^ m, 0, False)
        product = jnp.dot(
            rows.reshape(tokens, -1).T, columns, preferred_element_type=WIDE
        )
        return product.reshape(count, -1, columns.shape[1])

    def chip_sum(n, m):
        came = swap(piece(n, 1, m).astype(LOW), "core")
        return (piece(n, 0, m) + came.astype(WIDE)).astype(LOW)

    def joined(kept, sent, axis):
        return (kept.astype(WIDE) + swap(sent, axis).astype(WIDE)).astype(LOW)

    if first == "mod":
        far_side = chip_sum(1, 1)
        near_side = chip_sum(0, 1)
        sent = joined(chip_sum(1, 0), far_side, "mod")
        kept = joined(chip_sum(0, 0), near_side, "mod")
        total = joined(kept, sent, "near")
    else:
        far_side = chip_sum(1, 1)
        near_side = chip_sum(1, 0)
        sent = joined(chip_sum(0, 1), far_side, "near")
        kept = joined(chip_sum(0, 0), near_side, "near")
        total = joined(kept, sent, "mod")
    if count > 4:
        return lax.psum_scatter(total.astype(WIDE), "far", scatter_dimension=0, tiled=False)
    result = lax.dynamic_index_in_dim(total, here, 0, False).astype(WIDE)
    for distance in range(1, count):
        block = lax.dynamic_index_in_dim(total, (here + distance) % count, 0, False)
        result = result + shifted(block, distance, count).astype(WIDE)
    return result


def times(left, right):
    return jnp.dot(left, right, preferred_element_type=WIDE)


def times_back(left, right):
    return lax.dot_general(left, right, (((1,), (1,)), ((), ())), preferred_element_type=WIDE)


def body(
    x_in,
    cond,
    segments,
    out_grad,
    qkv_weight,
    qkv_moment,
    qkv_average,
    proj_weight,
    proj_moment,
    proj_average,
    fc1_weight,
    fc1_moment,
    fc1_average,
    fc2_weight,
    fc2_moment,
    fc2_average,
    bias_weight,
    bias_moment,
    bias_average,
    ada_weight,
    ada_moment,
    ada_average,
    adab_weight,
    adab_moment,
    adab_average,
):
    tokens, width = x_in.shape
    row_devices = lax.axis_size(ROWS)
    devices = lax.axis_size(ALL)
    row_index = lax.axis_index(ROWS)
    images = cond.shape[0] // 2
    head_width = width // HEADS
    block_rows = min(512, tokens)

    cond_silu, silu_back = jax.vjp(jax.nn.silu, cond.astype(WIDE))
    silu_all = lax.all_gather(cond_silu.astype(LOW), ROWS, axis=0, tiled=True)
    ada_low = ada_weight.astype(LOW)
    ada_columns = lax.all_to_all(ada_low, ROWS, split_axis=1, concat_axis=0, tiled=True)
    adab_low = adab_weight.astype(LOW).astype(WIDE)
    mod_columns = (times(silu_all, ada_columns) + adab_low).astype(LOW)
    mod_rows = lax.all_to_all(mod_columns, ALL, split_axis=0, concat_axis=1, tiled=True)
    modulation = jnp.swapaxes(
        mod_rows.reshape(images, row_devices, 2, -1), 1, 2
    ).reshape(images, -1)

    bias_full = lax.all_gather(bias_weight.astype(LOW), ALL, axis=0, tiled=True).astype(WIDE)
    qkv_low = gather_weight(qkv_weight.astype(LOW), "near")
    proj_low = gather_weight(proj_weight.astype(LOW), "mod")
    fc1_low = gather_weight(fc1_weight.astype(LOW), "near")
    fc2_low = gather_weight(fc2_weight.astype(LOW), "mod")
    hidden_width = fc2_low.shape[1]

    chooser = segments[:, None] == jnp.arange(images, dtype=jnp.int32)[None, :]
    per_token = times(chooser.astype(LOW), modulation)
    shift_attn, scale_attn, gate_attn, shift_mlp, scale_mlp, gate_mlp = [
        per_token[:, group * width : (group + 1) * width] for group in range(6)
    ]
    residual = x_in.astype(WIDE)
    first_norm, first_inverse = normalize(residual)
    attn_input = (first_norm * (1.0 + scale_attn) + shift_attn).astype(LOW)
    joint_proj = jnp.concatenate([times(attn_input, qkv_low[0]), times(attn_input, qkv_low[1])], 1)
    query_rows = (joint_proj[:, 0:width] + bias_full[0:width]).astype(LOW)
    key_rows = joint_proj[:, width : 2 * width].astype(LOW)
    value_rows = (joint_proj[:, 2 * width :] + bias_full[width : 2 * width]).astype(LOW)
    head_shape = (tokens, HEADS, head_width)
    query_heads = query_rows.reshape(head_shape)
    key_heads = key_rows.reshape(head_shape)
    value_heads = value_rows.reshape(head_shape)
    mixture, log_totals = attend_forward(query_heads, key_heads, value_heads, segments, block_rows)
    attn_out = (
        jnp.concatenate([times(mixture, proj_low[0]), times(mixture, proj_low[1])], 1)
        + bias_full[2 * width : 3 * width]
    )
    residual_mid = residual + gate_attn * attn_out
    second_norm, second_inverse = normalize(residual_mid)
    mlp_input = (second_norm * (1.0 + scale_mlp) + shift_mlp).astype(LOW)
    pre_act = (
        jnp.concatenate([times(mlp_input, fc1_low[0]), times(mlp_input, fc1_low[1])], 1)
        + bias_full[3 * width : 3 * width + hidden_width]
    )
    hidden_full, gelu_back = jax.vjp(partial(jax.nn.gelu, approximate=True), pre_act)
    hidden = hidden_full.astype(LOW)
    branch = (
        jnp.concatenate([times(hidden, fc2_low[0]), times(hidden, fc2_low[1])], 1)
        + bias_full[3 * width + hidden_width :]
    )
    block_out = (residual_mid + gate_mlp * branch).astype(LOW)

    def halves(values):
        middle = values.shape[1] // 2
        return jnp.stack([values[:, :middle], values[:, middle:]])

    upstream = out_grad.astype(WIDE)
    branch_grad = (gate_mlp * upstream).astype(LOW)
    gate_mlp_grad = upstream * branch
    branch_halves = halves(branch_grad)
    fc2_shard = scatter_gradient(hidden, branch_halves, "mod")
    hidden_grad = times_back(branch_halves[0], fc2_low[0]) + times_back(branch_halves[1], fc2_low[1])
    pre_grad = gelu_back(hidden_grad)[0].astype(LOW)
    pre_halves = halves(pre_grad)
    fc1_shard = scatter_gradient(mlp_input, pre_halves, "near")
    mlp_grad = times_back(pre_halves[0], fc1_low[0]) + times_back(pre_halves[1], fc1_low[1])
    scale_mlp_grad = mlp_grad * second_norm
    middle_grad = upstream + normalize_back(
        mlp_grad * (1.0 + scale_mlp), second_norm, second_inverse
    )
    attn_grad = (gate_attn * middle_grad).astype(LOW)
    gate_attn_grad = middle_grad * attn_out
    attn_halves = halves(attn_grad)
    proj_shard = scatter_gradient(mixture, attn_halves, "mod")
    mixture_grad = (
        times_back(attn_halves[0], proj_low[0]) + times_back(attn_halves[1], proj_low[1])
    ).astype(LOW)
    query_grad, key_grad, value_grad = attend_backward(
        query_heads,
        key_heads,
        value_heads,
        segments,
        log_totals,
        mixture_grad.reshape(head_shape),
        block_rows,
    )
    joint_grad = jnp.concatenate([query_grad, key_grad, value_grad], axis=1)
    joint_halves = halves(joint_grad)
    qkv_shard = scatter_gradient(attn_input, joint_halves, "near")
    input_grad = times_back(joint_halves[0], qkv_low[0]) + times_back(joint_halves[1], qkv_low[1])
    scale_attn_grad = input_grad * first_norm
    x_grad = middle_grad + normalize_back(
        input_grad * (1.0 + scale_attn), first_norm, first_inverse
    )

    token_mod_grad = jnp.concatenate(
        [input_grad, scale_attn_grad, gate_attn_grad, mlp_grad, scale_mlp_grad, gate_mlp_grad],
        axis=1,
    )
    slot_mod_grad = jnp.einsum(
        "ts,tc->sc", chooser.astype(WIDE), token_mod_grad, precision=lax.Precision.HIGHEST
    ).astype(LOW)
    half_grad = lax.all_to_all(slot_mod_grad, "mod", split_axis=1, concat_axis=0, tiled=True)
    mod_grad_all = lax.all_gather(half_grad, ROWS, axis=0, tiled=True)
    own_rows = ada_weight.shape[0]
    own_silu = lax.dynamic_slice_in_dim(silu_all, row_index * own_rows, own_rows, 1)
    ada_shard = jnp.einsum("ic,io->co", own_silu, mod_grad_all, preferred_element_type=WIDE)
    own_columns = adab_weight.shape[1]
    adab_shard = jnp.sum(
        lax.dynamic_slice_in_dim(mod_grad_all, row_index * own_columns, own_columns, 1).astype(WIDE),
        axis=0,
    )
    silu_part = times_back(mod_grad_all, ada_low)
    silu_part = lax.all_to_all(silu_part, ROWS, split_axis=0, concat_axis=1, tiled=True)
    cond_grad = silu_back(silu_part + swap(silu_part, "mod"))[0]

    grad_bias = jnp.concatenate(
        [
            jnp.sum(part.astype(WIDE), axis=0)
            for part in (query_grad, value_grad, attn_grad, pre_grad, branch_grad)
        ]
    ).reshape(devices, -1)
    bias_shard = jnp.sum(
        lax.all_to_all(grad_bias, ALL, split_axis=0, concat_axis=0, tiled=True), axis=0
    )

    rates = step_rates(tokens * devices)
    states_out = []
    states_out.extend(nesterov(qkv_weight, qkv_moment, qkv_average, qkv_shard, rates[0]))
    states_out.extend(nesterov(proj_weight, proj_moment, proj_average, proj_shard, rates[1]))
    states_out.extend(nesterov(fc1_weight, fc1_moment, fc1_average, fc1_shard, rates[2]))
    states_out.extend(nesterov(fc2_weight, fc2_moment, fc2_average, fc2_shard, rates[3]))
    states_out.extend(nesterov(bias_weight, bias_moment, bias_average, bias_shard, rates[4]))
    states_out.extend(nesterov(ada_weight, ada_moment, ada_average, ada_shard, rates[5]))
    states_out.extend(
        nesterov(adab_weight, adab_moment, adab_average, adab_shard.reshape(1, -1), rates[6])
    )
    return (block_out, x_grad, cond_grad) + tuple(states_out)


def solution(mesh):
    far = mesh.shape["dp"] // 4
    fine = Mesh(mesh.devices.reshape(far, 2, 2, mesh.shape["mod"]), ALL)
    tokens = P(ALL, None)
    images = P(ROWS, None)
    trunk = P(ROWS, "mod")
    bias = P(ALL)
    adab = P("mod", ROWS)
    states = (trunk,) * 12 + (bias,) * 3 + (trunk,) * 3 + (adab,) * 3
    return jax.shard_map(
        body,
        mesh=fine,
        in_specs=(tokens, images, bias, tokens) + states,
        out_specs=(tokens, tokens, images) + states,
        check_vma=False,
    )
```

time: 1700 us -> 1390 us (0.82)
  waiting for transfers between devices: 699 us -> 315 us
  blocking collectives: 201 us -> 88.5 us
  starting transfers between devices: 4.78 us -> 98.6 us
  local copies, waits for them, and re-layouts: 129 us -> 195 us
  other arithmetic: 175 us -> 203 us
    reduce_scatter x5 -> x0, waiting for transfers between devices: 333 us -> none  [the longest x1 117 us: body(): lax.psum_scatter(grad_fc1.astype(jnp.bfloat16), 'mod', scatter_dimension=...]
    unnamed x18 -> x0, waiting for transfers between devices: 314 us -> none
    ppermute x0 -> x81, waiting for transfers between devices: none -> 293 us  [the longest x57 225 us: swap(): return lax.ppermute(values, axis, [(0, 1), (1, 0)])]
    unnamed x3 -> x1, blocking collectives: 154 us -> 41.3 us
    ppermute x0 -> x81, starting transfers between devices: none -> 61.9 us  [the longest x24 36.4 us: shifted(): lax.ppermute(values, 'far', [(i, (i + distance) % count) for i in range(c...]
    unnamed x184 -> x328, local copies, waits for them, and re-layouts: 83.5 us -> 25.2 us
    dynamic_update_slice x0 -> x44, local copies, waits for them, and re-layouts: none -> 56.5 us  [the longest x32 47.6 us: gather_weight(): lax.dynamic_update_slice(whole, part[None, :, None, None], (half ^ m, 0,...]
    all_gather x5 -> x0, waiting for transfers between devices: 49.6 us -> none  [the longest x1 39.4 us: body(): lax.all_gather(halves_low[3], 'dp', axis=0, tiled=True)]
  transfers between devices with their start and end apart: 15 -> 86, of which waited for: 10 -> 29; matrix products, arithmetic and copies ran while one was open for 24% -> 32% of each run, Pallas kernels for 0% -> 0%
where the time goes in v1:
time: 1390 us; the launch traced here: 1380 us
  matrix products  479 us (34%)
  waiting for transfers between devices  315 us (23%)
  other arithmetic  203 us (15%)
  local copies, waits for them, and re-layouts  195 us (14%)
  starting transfers between devices  98.6 us (7%)
  blocking collectives  88.5 us (6%)
    ppermute x57, waiting for transfers between devices, swap(): return lax.ppermute(values, axis, [(0, 1), (1, 0)])  225 us
    dot_general x9, matrix products, times_back(): lax.dot_general(left, right, (((1,), (1,)), ((), ())), preferred_element_...  89 us
    dot_general x32, matrix products, piece(): jnp.dot(rows.reshape(tokens, -1).T, columns, preferred_element_type=WIDE)  76.9 us
    dot_general x10, matrix products, times(): return jnp.dot(left, right, preferred_element_type=WIDE)  71.7 us
    ppermute x24, waiting for transfers between devices, shifted(): lax.ppermute(values, 'far', [(i, (i + distance) % count) for i in range(c...  67.4 us
    dot_general x4, matrix products, masked_scores(): jnp.einsum('qhd,khd->hqk', query_part, key_rows, preferred_element_type=j...  67.4 us
    convert_element_type x2, other arithmetic, one_block(): score_grad = (softmax * centred).astype(jnp.bfloat16)  55.5 us
    dot_general x2, matrix products, one_block(): jnp.einsum('qhd,khd->hqk', up_part, value_rows, preferred_element_type=jn...  52.6 us
  transfers between devices with their start and end apart: 86, of which 29 were waited for; matrix products, arithmetic and copies ran while one was open for 32% of the time, Pallas kernels for 0%

profile of v1, /device:TPU:0, one launch (start us, length us, event | category | flops | bytes accessed | tf_op | source)
XLA Modules:
  0.0 1384.0 jit_solution(12568528321172422887)
XLA Ops:
  25.5 41.3 %all-reduce = bf16[9216]{0:T(1024)(128)(2,1)S(1)} all-reduce(bf16[9216]{0:T(1024)(128)(2,1)} %dynamic-update-slice), channel_id=1, replica_groups=mesh['far'=4,'near'=2,'core'=2,'mod'=2] {'far','near','core','mod'}, use_global_device_ids=true, to_apply=%add | all-reduce | flops 9216 | bytes 36864
  75.0 23.1 %all_gather.9 = bf16[128,1152]{1,0:T(8,128)(2,1)} all-gather(bf16[8,1152]{1,0:T(8,128)(2,1)S(1)} %copy-done.95), channel_id=1, replica_groups=mesh['far'=4,'near'=2,'core'=2,'mod'=2] {'far','near','core'}, dimensions={0}, use_global_device_ids=true | all-gather | bytes 313344 | tf_op jit(solution)/shard_map/all_gather | solution.py:275
  126.2 16.6 %collective-permute-done.21 = bf16[72,2304]{1,0:T(8,128)(2,1)S(1)} collective-permute-done((bf16[72,2304]{1,0:T(8,128)(2,1)S(1)}, bf16[72,2304]{1,0:T(8,128)(2,1)S(1)}, u32[]{:S(2)}, u32[]{:S(2)}) %collective-permute-start.21) | collective-permute-done | bytes 331808 | tf_op jit(solution)/shard_map/ppermute | solution.py:149
  172.0 19.4 %collective-permute-done.18 = bf16[4,72,576]{2,1,0:T(8,128)(2,1)} collective-permute-done((bf16[4,72,576]{2,1,0:T(8,128)(2,1)S(1)}, bf16[4,72,576]{2,1,0:T(8,128)(2,1)}, u32[]{:S(2)}, u32[]{:S(2)}) %collective-permute-start.18) | collective-permute-done | bytes 331808 | tf_op jit(solution)/shard_map/ppermute | solution.py:145
  195.1 12.1 all-to-all-start.1
  208.9 13.0 all-to-all-done.1
  222.1 11.5 fusion.201
  256.7 24.4 %collective-permute-done.24 = bf16[4,72,2304]{2,1,0:T(8,128)(2,1)S(1)} collective-permute-done((bf16[4,72,2304]{2,1,0:T(8,128)(2,1)}, bf16[4,72,2304]{2,1,0:T(8,128)(2,1)S(1)}, u32[]{:S(2)}, u32[]{:S(2)}) %collective-permute-start.24) | collective-permute-done | bytes 1327136 | tf_op jit(solution)/shard_map/ppermute | solution.py:145
  285.6 26.6 %collective-permute-done.34 = bf16[4,288,576]{2,1,0:T(8,128)(2,1)S(1)} collective-permute-done((bf16[4,288,576]{2,1,0:T(8,128)(2,1)S(1)}, bf16[4,288,576]{2,1,0:T(8,128)(2,1)S(1)}, u32[]{:S(2)}, u32[]{:S(2)}) %collective-permute-start.34) | collective-permute-done | bytes 1327136 | tf_op jit(solution)/shard_map/ppermute | solution.py:145
  317.7 21.8 %collective-permute-done.8 = bf16[4,72,1728]{2,1,0:T(8,128)(2,1)S(1)} collective-permute-done((bf16[4,72,1728]{2,1,0:T(8,128)(2,1)}, bf16[4,72,1728]{2,1,0:T(8,128)(2,1)S(1)}, u32[]{:S(2)}, u32[]{:S(2)}) %collective-permute-start.8) | collective-permute-done | bytes 995360 | tf_op jit(solution)/shard_map/ppermute | solution.py:145
  345.2 22.4 %collective-permute-done.28 = bf16[4,72,2304]{2,1,0:T(8,128)(2,1)} collective-permute-done((bf16[4,72,2304]{2,1,0:T(8,128)(2,1)S(1)}, bf16[4,72,2304]{2,1,0:T(8,128)(2,1)}, u32[]{:S(2)}, u32[]{:S(2)}) %collective-permute-start.28) | collective-permute-done | bytes 1327136 | tf_op jit(solution)/shard_map/ppermute | solution.py:145
  416.9 94.8 %while.27 = (s32[]{:T(128)}, bf16[2,512,16,72]{1,3,2,0:T(8,128)(2,1)S(1)}, f32[2,16,512]{2,1,0:T(8,128)}, s32[2,512]{1,0:T(2,128)S(1)}, s32[1024]{0:T(1024)S(1)}...) while((s32[]{:T(128)}, ...), condition=%wide.region_5.6_spmd, body=%wide.region_2.5_spmd.sunk | while | flops 2517688320 | bytes 110110832 | solution.py:79
  417.3 16.0 %fusion.380 = (f32[16,512]{1,0:T(8,128)S(1)}, f32[16,512,1024]{2,1,0:T(8,128)}) fusion(pred[512,1024]{1,0:T(8,128)(4,1)S(1)} %broadcast_compare_fusion.4, bf16[1024,16,72]{0,2,1:T(8,128)(2,1)} %get-tuple-element.549, bf16[2,512,16,72]{1,3,2,0:T(8,128)(2,1)} %get-tuple-element.548, s32[]{:T(128)S(6)} %copy.300), kind=kOutput, calls=%fused_computation.3.clone.1 | convolution fusion | flops 1233117184 | bytes 37650436 | tf_op jit(solution)/shard_map/while/body/eval_jaxpr/qhd,khd->hqk/dot_general | solution.py:55
  433.4 15.0 %fusion.381 = f32[16,512]{1,0:T(8,128)S(1)} fusion(f32[16,512,1024]{2,1,0:T(8,128)} %get-tuple-element.510, f32[16,512]{1,0:T(8,128)S(1)} %get-tuple-element.511, pred[512,1024]{1,0:T(8,128)(4,1)S(1)} %broadcast_compare_fusion.4), kind=kLoop, calls=%fused_computation.4.clone.1 | loop fusion | flops 33546240 | bytes 34144256 | tf_op jit(solution)/shard_map/while/body/eval_jaxpr/reduce_sum | solution.py:72
  448.4 15.2 %fusion.382 = bf16[2,512,16,72]{1,3,2,0:T(8,128)(2,1)S(1)} fusion(bf16[2,512,16,72]{1,3,2,0:T(8,128)(2,1)S(1)} %get-tuple-element.535, s32[]{:T(128)S(6)} %copy.300, bf16[1024,16,72]{0,2,1:T(8,128)(2,1)} %get-tuple-element.550, f32[16,512,1024]{2,1,0:T(8,128)} %get-tuple-element.510, f32[16,512]{1,0:T(8,128)S(1)} %fusion.381, ...), kind=kOutput, calls=%fused_computation.8.clone.1 | convolution fusion | flops 1250492416 | bytes 37683204 | tf_op jit(solution)/shard_map/while/body/eval_jaxpr/hqk,khd->qhd/dot_general | solution.py:74
  464.6 16.0 %fusion.380 = (f32[16,512]{1,0:T(8,128)S(1)}, f32[16,512,1024]{2,1,0:T(8,128)}) fusion(pred[512,1024]{1,0:T(8,128)(4,1)S(1)} %broadcast_compare_fusion.4, bf16[1024,16,72]{0,2,1:T(8,128)(2,1)} %get-tuple-element.549, bf16[2,512,16,72]{1,3,2,0:T(8,128)(2,1)} %get-tuple-element.548, s32[]{:T(128)S(6)} %copy.300), kind=kOutput, calls=%fused_computation.3.clone.1 | convolution fusion | flops 1233117184 | bytes 37650436 | tf_op jit(solution)/shard_map/while/body/eval_jaxpr/qhd,khd->hqk/dot_general | solution.py:55
  480.7 15.0 %fusion.381 = f32[16,512]{1,0:T(8,128)S(1)} fusion(f32[16,512,1024]{2,1,0:T(8,128)} %get-tuple-element.510, f32[16,512]{1,0:T(8,128)S(1)} %get-tuple-element.511, pred[512,1024]{1,0:T(8,128)(4,1)S(1)} %broadcast_compare_fusion.4), kind=kLoop, calls=%fused_computation.4.clone.1 | loop fusion | flops 33546240 | bytes 34144256 | tf_op jit(solution)/shard_map/while/body/eval_jaxpr/reduce_sum | solution.py:72
  495.7 15.2 %fusion.382 = bf16[2,512,16,72]{1,3,2,0:T(8,128)(2,1)S(1)} fusion(bf16[2,512,16,72]{1,3,2,0:T(8,128)(2,1)S(1)} %get-tuple-element.535, s32[]{:T(128)S(6)} %copy.300, bf16[1024,16,72]{0,2,1:T(8,128)(2,1)} %get-tuple-element.550, f32[16,512,1024]{2,1,0:T(8,128)} %get-tuple-element.510, f32[16,512]{1,0:T(8,128)S(1)} %fusion.381, ...), kind=kOutput, calls=%fused_computation.8.clone.1 | convolution fusion | flops 1250492416 | bytes 37683204 | tf_op jit(solution)/shard_map/while/body/eval_jaxpr/hqk,khd->qhd/dot_general | solution.py:74
  564.1 11.7 fusion.289
  603.7 10.9 fusion.50
  646.1 13.9 %fusion.141 = f32[1024,4608]{1,0:T(8,128)} fusion(bf16[4608,576]{1,0:T(8,128)(2,1)} %bitcast.672, bf16[1024,1152]{1,0:T(8,128)(2,1)S(1)} %copy-done.12), kind=kOutput, calls=%fused_computation.245 | convolution fusion | flops 5435817984 | bytes 25493504 | tf_op jit(solution)/shard_map/dot_general | solution.py:236
  660.1 11.8 fusion.291
  680.7 25.5 %convert_reduce_fusion = (f32[4608]{0:T(1024)}, bf16[1024,4608]{1,0:T(8,128)(2,1)}) fusion(f32[4608]{0:T(1024)S(1)} %copy-done.82, f32[1024,2304]{1,0:T(8,128)} %fusion.289, f32[1024,2304]{1,0:T(8,128)} %fusion.288, f32[1024,4608]{1,0:T(8,128)} %fusion.141, bf16[4608,576]{1,0:T(8,128)(2,1)} %bitcast.670, bf16[1024,1152]{1,0:T(8,128)(2,1)S(1)} %copy-done.12), kind=kOutput, calls=%fused_computation.68 | convolution fusion | flops 5553778176 | bytes 53843968 | tf_op jit(solution)/shard_map/dot_general | solution.py:236
  706.2 11.3 fusion.76
  717.5 13.1 fusion.275
  730.6 13.9 %convert_reduce_fusion.3 = (f32[1152]{0:T(1024)}, bf16[1024,1152]{1,0:T(8,128)(2,1)S(1)}, f32[1024,1152]{1,0:T(8,128)}, bf16[1024,1152]{1,0:T(8,128)(2,1)}) fusion(f32[1024,6912]{1,0:T(8,128)} %fusion.201, f32[1024]{0:T(1024)S(1)} %broadcast_multiply_fusion.2, f32[1024,1152]{1,0:T(8,128)S(1)} %bitcast.642, f32[1024]{0:T(1024)S(1)} %copy-done.90, ...), kind=kLoop, calls=%fused_computation.116 | loop fusion | flops 22412160 | bytes 40133632 | tf_op jit(solution)/shard_map/reduce_sum | solution.py:394
  773.9 220.2 %while.28 = (s32[]{:T(128)}, f32[1024,16,72]{0,2,1:T(8,128)}, f32[1024,16,72]{0,2,1:T(8,128)}, bf16[2,512,16,72]{1,3,2,0:T(8,128)(2,1)}, bf16[2,512,16,72]{1,3,2...) while((s32[]{:T(128)}, f32[1024,16,72]{0,2,1:T(8,128)}, ...), condition=%wide.region_12.13_spmd.clone, body=%wide.region_10.12_spmd.clone.sunk | while | flops 6173220864 | bytes 352954528 | solution.py:120
  774.7 17.7 %fusion.392 = f32[16,512,1024]{2,1,0:T(8,128)} fusion(bf16[1024,16,72]{0,2,1:T(8,128)(2,1)} %get-tuple-element.585, bf16[2,512,16,72]{1,3,2,0:T(8,128)(2,1)} %get-tuple-element.582, s32[]{:T(128)S(6)} %copy.346), kind=kOutput, calls=%fused_computation.33.clone.1 | convolution fusion | flops 1207959552 | bytes 37093380 | tf_op jit(solution)/shard_map/while/body/eval_jaxpr/qhd,khd->hqk/dot_general | solution.py:55
  792.4 17.9 %bitcast_add_fusion.5 = f32[1024,16,72]{0,2,1:T(8,128)} fusion(f32[1024,16,72]{0,2,1:T(8,128)} %get-tuple-element.567, pred[]{:T(512)S(6)} %compare.9, f32[16,512,1024]{2,1,0:T(8,128)} %fusion.392, f32[16,512]{1,0:T(8,128)S(1)} %dynamic-slice_bitcast_fusion.14, pred[512,1024]{1,0:T(8,128)(4,1)S(1)} %broadcast_compare_fusion.5, ...), kind=kOutput, calls=%fused_computation.24.clone.1 | convolution fusion | flops 1243873280 | bytes 44728324 | tf_op jit(solution)/shard_map/while/body/eval_jaxpr/hqk,qhd->khd/dot_general | solution.py:100
  810.3 26.3 %multiply_reduce_fusion.4 = (f32[16,512]{1,0:T(8,128)S(1)}, f32[16,512,1024]{2,1,0:T(8,128)}) fusion(f32[16,512,1024]{2,1,0:T(8,128)} %fusion.392, f32[16,512]{1,0:T(8,128)S(1)} %dynamic-slice_bitcast_fusion.14, pred[512,1024]{1,0:T(8,128)(4,1)S(1)} %broadcast_compare_fusion.5, bf16[1024,16,72]{0,2,1:T(8,128)(2,1)} %get-tuple-element.588, ...), kind=kOutput, calls=%fused_computation.19.clone.1 | convolution fusion | flops 1249894400 | bytes 71237632 | tf_op jit(solution)/shard_map/while/body/eval_jaxpr/qhd,khd->hqk/dot_general | solution.py:103
  836.6 27.8 %multiply_convert_fusion.6 = bf16[16,512,1024]{2,1,0:T(8,128)(2,1)} fusion(f32[16,512,1024]{2,1,0:T(8,128)} %get-tuple-element.523, f32[16,512,1024]{2,1,0:T(8,128)} %fusion.392, f32[16,512]{1,0:T(8,128)S(1)} %get-tuple-element.524, f32[16,512]{1,0:T(8,128)S(1)} %dynamic-slice_bitcast_fusion.14, pred[512,1024]{1,0:T(8,128)(4,1)S(1)} %broadcast_compare_fusion.5), kind=kLoop, calls=%fused_computation.18.clone.1 | loop fusion | flops 50331648 | bytes 84475904 | tf_op jit(solution)/shard_map/while/body/eval_jaxpr/convert_element_type | solution.py:107
  864.3 10.4 fusion.393
  883.1 17.7 %fusion.392 = f32[16,512,1024]{2,1,0:T(8,128)} fusion(bf16[1024,16,72]{0,2,1:T(8,128)(2,1)} %get-tuple-element.585, bf16[2,512,16,72]{1,3,2,0:T(8,128)(2,1)} %get-tuple-element.582, s32[]{:T(128)S(6)} %copy.346), kind=kOutput, calls=%fused_computation.33.clone.1 | convolution fusion | flops 1207959552 | bytes 37093380 | tf_op jit(solution)/shard_map/while/body/eval_jaxpr/qhd,khd->hqk/dot_general | solution.py:55
  900.8 19.2 %bitcast_add_fusion.5 = f32[1024,16,72]{0,2,1:T(8,128)} fusion(f32[1024,16,72]{0,2,1:T(8,128)} %get-tuple-element.567, pred[]{:T(512)S(6)} %compare.9, f32[16,512,1024]{2,1,0:T(8,128)} %fusion.392, f32[16,512]{1,0:T(8,128)S(1)} %dynamic-slice_bitcast_fusion.14, pred[512,1024]{1,0:T(8,128)(4,1)S(1)} %broadcast_compare_fusion.5, ...), kind=kOutput, calls=%fused_computation.24.clone.1 | convolution fusion | flops 1243873280 | bytes 44728324 | tf_op jit(solution)/shard_map/while/body/eval_jaxpr/hqk,qhd->khd/dot_general | solution.py:100
  920.0 26.3 %multiply_reduce_fusion.4 = (f32[16,512]{1,0:T(8,128)S(1)}, f32[16,512,1024]{2,1,0:T(8,128)}) fusion(f32[16,512,1024]{2,1,0:T(8,128)} %fusion.392, f32[16,512]{1,0:T(8,128)S(1)} %dynamic-slice_bitcast_fusion.14, pred[512,1024]{1,0:T(8,128)(4,1)S(1)} %broadcast_compare_fusion.5, bf16[1024,16,72]{0,2,1:T(8,128)(2,1)} %get-tuple-element.588, ...), kind=kOutput, calls=%fused_computation.19.clone.1 | convolution fusion | flops 1249894400 | bytes 71237632 | tf_op jit(solution)/shard_map/while/body/eval_jaxpr/qhd,khd->hqk/dot_general | solution.py:103
  946.3 27.8 %multiply_convert_fusion.6 = bf16[16,512,1024]{2,1,0:T(8,128)(2,1)} fusion(f32[16,512,1024]{2,1,0:T(8,128)} %get-tuple-element.523, f32[16,512,1024]{2,1,0:T(8,128)} %fusion.392, f32[16,512]{1,0:T(8,128)S(1)} %get-tuple-element.524, f32[16,512]{1,0:T(8,128)S(1)} %dynamic-slice_bitcast_fusion.14, pred[512,1024]{1,0:T(8,128)(4,1)S(1)} %broadcast_compare_fusion.5), kind=kLoop, calls=%fused_computation.18.clone.1 | loop fusion | flops 50331648 | bytes 84475904 | tf_op jit(solution)/shard_map/while/body/eval_jaxpr/convert_element_type | solution.py:107
  974.1 10.4 fusion.393
  1055.9 13.2 constant_dynamic-update-slice_fusion.1
  1096.0 14.3 %convolution_convert_fusion = bf16[4,6912]{1,0:T(4,128)(2,1)} fusion(f32[1024,6912]{1,0:T(8,128)} %fusion.66, s32[1024]{0:T(1024)S(1)} %get-tuple-element.625), kind=kOutput, calls=%fused_computation.78 | convolution fusion | flops 339770368 | bytes 28370944 | tf_op jit(solution)/shard_map/ts,tc->sc/dot_general | solution.py:375
  1117.6 11.7 all-to-all-start.4
  1129.3 24.1 %all_gather.11 = bf16[128,3456]{1,0:T(8,128)(2,1)S(1)} all-gather(bf16[8,3456]{1,0:T(8,128)(2,1)S(1)} %all_to_all.70), channel_id=1, replica_groups=mesh['far'=4,'near'=2,'core'=2,'mod'=2] {'far','near','core'}, dimensions={0}, use_global_device_ids=true | all-gather | bytes 940032 | tf_op jit(solution)/shard_map/all_gather | solution.py:379
  1216.8 16.9 %collective-permute-done.46 = bf16[4,72,1728]{2,1,0:T(8,128)(2,1)S(1)} collective-permute-done((bf16[4,72,1728]{2,1,0:T(8,128)(2,1)S(1)}, bf16[4,72,1728]{2,1,0:T(8,128)(2,1)S(1)}, u32[]{:S(2)}, u32[]{:S(2)}) %collective-permute-start.46) | collective-permute-done | bytes 995360 | tf_op jit(solution)/shard_map/ppermute | solution.py:145
  1237.9 11.4 collective-permute-done.76
  1260.3 11.1 collective-permute-done.47
  1289.1 10.8 collective-permute-done.49
  1304.2 15.2 %collective-permute-done.77 = bf16[4,288,576]{2,1,0:T(8,128)(2,1)S(1)} collective-permute-done((bf16[4,288,576]{2,1,0:T(8,128)(2,1)S(1)}, bf16[4,288,576]{2,1,0:T(8,128)(2,1)S(1)}, u32[]{:S(2)}, u32[]{:S(2)}) %collective-permute-start.77) | collective-permute-done | bytes 1327136 | tf_op jit(solution)/shard_map/ppermute | solution.py:145
  1324.1 22.5 %collective-permute-done.63 = bf16[4,72,2304]{2,1,0:T(8,128)(2,1)S(1)} collective-permute-done((bf16[4,72,2304]{2,1,0:T(8,128)(2,1)S(1)}, bf16[4,72,2304]{2,1,0:T(8,128)(2,1)S(1)}, u32[]{:S(2)}, u32[]{:S(2)}) %collective-permute-start.63) | collective-permute-done | bytes 1327136 | tf_op jit(solution)/shard_map/ppermute | solution.py:145
  1367.7 14.3 %collective-permute-done.69 = bf16[72,2304]{1,0:T(8,128)(2,1)S(1)} collective-permute-done((bf16[72,2304]{1,0:T(8,128)(2,1)S(1)}, bf16[72,2304]{1,0:T(8,128)(2,1)S(1)}, u32[]{:S(2)}, u32[]{:S(2)}) %collective-permute-start.69) | collective-permute-done | bytes 331808 | tf_op jit(solution)/shard_map/ppermute | solution.py:149
  (709 shorter events, 575.9 us)
Async XLA Ops:
  2.3 97.4 %collective-permute-start.11 = (bf16[72,576]{1,0:T(8,128)(2,1)}, bf16[72,576]{1,0:T(8,128)(2,1)}, u32[]{:S(2)}, u32[]{:S(2)}) collective-permute-start(bf16[72,576]{1,0:T(8,128)(2,1)} %get-tuple-element.339), channel_id=1, source_target_pairs={{0,16},{8,24},{16,0},{24,8},{1,17},{9,25},{17,1},{25,9},{2,18},{10... | collective-permute-start | bytes 248840 | tf_op jit(solution)/shard_map/ppermute | solution.py:149
  6.4 91.8 %collective-permute-start.10 = (bf16[72,576]{1,0:T(8,128)(2,1)}, bf16[72,576]{1,0:T(8,128)(2,1)}, u32[]{:S(2)}, u32[]{:S(2)}) collective-permute-start(bf16[72,576]{1,0:T(8,128)(2,1)} %get-tuple-element.339), channel_id=1, source_target_pairs={{0,8},{8,16},{16,24},{24,0},{1,9},{9,17},{17,25},{25,1},{2,10},{10... | collective-permute-start | bytes 248840 | tf_op jit(solution)/shard_map/ppermute | solution.py:149
  8.0 93.5 %collective-permute-start.12 = (bf16[72,576]{1,0:T(8,128)(2,1)}, bf16[72,576]{1,0:T(8,128)(2,1)}, u32[]{:S(2)}, u32[]{:S(2)}) collective-permute-start(bf16[72,576]{1,0:T(8,128)(2,1)} %get-tuple-element.339), channel_id=1, source_target_pairs={{0,24},{8,0},{16,8},{24,16},{1,25},{9,1},{17,9},{25,17},{2,26},{10... | collective-permute-start | bytes 248840 | tf_op jit(solution)/shard_map/ppermute | solution.py:149
  12.1 99.7 %collective-permute-start.1 = (bf16[72,1728]{1,0:T(8,128)(2,1)}, bf16[72,1728]{1,0:T(8,128)(2,1)}, u32[]{:S(2)}, u32[]{:S(2)}) collective-permute-start(bf16[72,1728]{1,0:T(8,128)(2,1)} %get-tuple-element.341), channel_id=1, source_target_pairs={{0,16},{8,24},{16,0},{24,8},{1,17},{9,25},{17,1},{25,9},{2,18},{10... | collective-permute-start | bytes 746504 | tf_op jit(solution)/shard_map/ppermute | solution.py:149
  13.1 95.4 %collective-permute-start = (bf16[72,1728]{1,0:T(8,128)(2,1)}, bf16[72,1728]{1,0:T(8,128)(2,1)}, u32[]{:S(2)}, u32[]{:S(2)}) collective-permute-start(bf16[72,1728]{1,0:T(8,128)(2,1)} %get-tuple-element.341), channel_id=1, source_target_pairs={{0,8},{8,16},{16,24},{24,0},{1,9},{9,17},{17,25},{25,1},{2,10},{10... | collective-permute-start | bytes 746504 | tf_op jit(solution)/shard_map/ppermute | solution.py:149
  17.1 175.7 %all-to-all-start = ((bf16[72,16,216]{2,0,1:T(8,128)(2,1)}), bf16[72,16,216]{2,0,1:T(8,128)(2,1)}, u32[]{:S(2)}, u32[]{:S(2)}) async-start(bf16[72,16,216]{2,0,1:T(8,128)(2,1)} %copy.215), calls=%async_computation | async-start | bytes 1179648 | tf_op jit(solution)/shard_map/all_to_all | solution.py:277
  99.7 43.1 %collective-permute-start.21 = (bf16[72,2304]{1,0:T(8,128)(2,1)S(1)}, bf16[72,2304]{1,0:T(8,128)(2,1)S(1)}, u32[]{:S(2)}, u32[]{:S(2)}) collective-permute-start(bf16[72,2304]{1,0:T(8,128)(2,1)S(1)} %get-tuple-element.335), channel_id=1, source_target_pairs={{0,16},{8,24},{16,0},{24,8},{1,17},{9,25},{17,1},{25,9},{2,18},{10... | collective-permute-start | bytes 995336 | tf_op jit(solution)/shard_map/ppermute | solution.py:149
  108.4 35.7 %collective-permute-start.22 = (bf16[72,2304]{1,0:T(8,128)(2,1)S(1)}, bf16[72,2304]{1,0:T(8,128)(2,1)S(1)}, u32[]{:S(2)}, u32[]{:S(2)}) collective-permute-start(bf16[72,2304]{1,0:T(8,128)(2,1)S(1)} %get-tuple-element.335), channel_id=1, source_target_pairs={{0,24},{8,0},{16,8},{24,16},{1,25},{9,1},{17,9},{25,17},{2,26},{10... | collective-permute-start | bytes 995336 | tf_op jit(solution)/shard_map/ppermute | solution.py:149
  111.8 46.1 %collective-permute-start.31 = (bf16[288,576]{1,0:T(8,128)(2,1)S(1)}, bf16[288,576]{1,0:T(8,128)(2,1)S(1)}, u32[]{:S(2)}, u32[]{:S(2)}) collective-permute-start(bf16[288,576]{1,0:T(8,128)(2,1)S(1)} %get-tuple-element.333), channel_id=1, source_target_pairs={{0,16},{8,24},{16,0},{24,8},{1,17},{9,25},{17,1},{25,9},{2,18},{10... | collective-permute-start | bytes 995336 | tf_op jit(solution)/shard_map/ppermute | solution.py:149
  113.4 38.8 %collective-permute-start.30 = (bf16[288,576]{1,0:T(8,128)(2,1)S(1)}, bf16[288,576]{1,0:T(8,128)(2,1)S(1)}, u32[]{:S(2)}, u32[]{:S(2)}) collective-permute-start(bf16[288,576]{1,0:T(8,128)(2,1)S(1)} %get-tuple-element.333), channel_id=1, source_target_pairs={{0,8},{8,16},{16,24},{24,0},{1,9},{9,17},{17,25},{25,1},{2,10},{10... | collective-permute-start | bytes 995336 | tf_op jit(solution)/shard_map/ppermute | solution.py:149
  125.4 33.8 %collective-permute-start.32 = (bf16[288,576]{1,0:T(8,128)(2,1)S(1)}, bf16[288,576]{1,0:T(8,128)(2,1)S(1)}, u32[]{:S(2)}, u32[]{:S(2)}) collective-permute-start(bf16[288,576]{1,0:T(8,128)(2,1)S(1)} %get-tuple-element.333), channel_id=1, source_target_pairs={{0,24},{8,0},{16,8},{24,16},{1,25},{9,1},{17,9},{25,17},{2,26},{10... | collective-permute-start | bytes 995336 | tf_op jit(solution)/shard_map/ppermute | solution.py:149
  157.8 126.1 %collective-permute-start.6 = (bf16[4,72,1728]{2,1,0:T(8,128)(2,1)S(1)}, bf16[4,72,1728]{2,1,0:T(8,128)(2,1)}, u32[]{:S(2)}, u32[]{:S(2)}) collective-permute-start(bf16[4,72,1728]{2,1,0:T(8,128)(2,1)S(1)} %bitcast_dynamic-update-slice_fusion.41), channel_id=1, source_target_pairs={{0,1},{1,0},{2,3},{3,2},{4,5},{5,4},{6,7},{7,6},{8,9},{9,8},{10,11... | collective-permute-start | bytes 2985992 | tf_op jit(solution)/shard_map/ppermute | solution.py:145
  159.2 92.7 %collective-permute-start.4 = (bf16[4,72,1728]{2,1,0:T(8,128)(2,1)S(1)}, bf16[4,72,1728]{2,1,0:T(8,128)(2,1)}, u32[]{:S(2)}, u32[]{:S(2)}) collective-permute-start(bf16[4,72,1728]{2,1,0:T(8,128)(2,1)S(1)} %bitcast_dynamic-update-slice_fusion.41), channel_id=1, source_target_pairs={{0,4},{4,0},{1,5},{5,1},{2,6},{6,2},{3,7},{7,3},{8,12},{12,8},{9,1... | collective-permute-start | bytes 2985992 | tf_op jit(solution)/shard_map/ppermute | solution.py:145
  166.3 82.6 %collective-permute-start.3 = (bf16[4,72,1728]{2,1,0:T(8,128)(2,1)S(1)}, bf16[4,72,1728]{2,1,0:T(8,128)(2,1)}, u32[]{:S(2)}, u32[]{:S(2)}) collective-permute-start(bf16[4,72,1728]{2,1,0:T(8,128)(2,1)S(1)} %bitcast_dynamic-update-slice_fusion.41), channel_id=1, source_target_pairs={{0,2},{2,0},{1,3},{3,1},{4,6},{6,4},{5,7},{7,5},{8,10},{10,8},{9,1... | collective-permute-start | bytes 2985992 | tf_op jit(solution)/shard_map/ppermute | solution.py:145
  191.4 150.9 %collective-permute-start.26 = (bf16[4,72,2304]{2,1,0:T(8,128)(2,1)}, bf16[4,72,2304]{2,1,0:T(8,128)(2,1)}, u32[]{:S(2)}, u32[]{:S(2)}) collective-permute-start(bf16[4,72,2304]{2,1,0:T(8,128)(2,1)} %bitcast_dynamic-update-slice_fusion.37), channel_id=1, source_target_pairs={{0,1},{1,0},{2,3},{3,2},{4,5},{5,4},{6,7},{7,6},{8,9},{9,8},{10,11... | collective-permute-start | bytes 3981320 | tf_op jit(solution)/shard_map/ppermute | solution.py:145
  192.0 51.4 %collective-permute-start.19 = (bf16[4,72,576]{2,1,0:T(8,128)(2,1)}, bf16[4,72,576]{2,1,0:T(8,128)(2,1)}, u32[]{:S(2)}, u32[]{:S(2)}) collective-permute-start(bf16[4,72,576]{2,1,0:T(8,128)(2,1)} %collective-permute-done.18), channel_id=1, source_target_pairs={{0,2},{2,0},{1,3},{3,1},{4,6},{6,4},{5,7},{7,5},{8,10},{10,8},{9,1... | collective-permute-start | bytes 995336 | tf_op jit(solution)/shard_map/ppermute | solution.py:145
  249.0 32.1 %collective-permute-start.24 = (bf16[4,72,2304]{2,1,0:T(8,128)(2,1)}, bf16[4,72,2304]{2,1,0:T(8,128)(2,1)S(1)}, u32[]{:S(2)}, u32[]{:S(2)}) collective-permute-start(bf16[4,72,2304]{2,1,0:T(8,128)(2,1)} %bitcast_dynamic-update-slice_fusion.37), channel_id=1, source_target_pairs={{0,4},{4,0},{1,5},{5,1},{2,6},{6,2},{3,7},{7,3},{8,12},{12,8},{9,1... | collective-permute-start | bytes 3981320 | tf_op jit(solution)/shard_map/ppermute | solution.py:145
  251.9 60.3 %collective-permute-start.34 = (bf16[4,288,576]{2,1,0:T(8,128)(2,1)S(1)}, bf16[4,288,576]{2,1,0:T(8,128)(2,1)S(1)}, u32[]{:S(2)}, u32[]{:S(2)}) collective-permute-start(bf16[4,288,576]{2,1,0:T(8,128)(2,1)S(1)} %copy-done.27), channel_id=1, source_target_pairs={{0,4},{4,0},{1,5},{5,1},{2,6},{6,2},{3,7},{7,3},{8,12},{12,8},{9,1... | collective-permute-start | bytes 3981320 | tf_op jit(solution)/shard_map/ppermute | solution.py:145
  281.1 32.4 %collective-permute-start.5 = (bf16[4,72,1728]{2,1,0:T(8,128)(2,1)}, bf16[4,72,1728]{2,1,0:T(8,128)(2,1)S(1)}, u32[]{:S(2)}, u32[]{:S(2)}) collective-permute-start(bf16[4,72,1728]{2,1,0:T(8,128)(2,1)} %collective-permute-done.4), channel_id=1, source_target_pairs={{0,2},{2,0},{1,3},{3,1},{4,6},{6,4},{5,7},{7,5},{8,10},{10,8},{9,1... | collective-permute-start | bytes 2985992 | tf_op jit(solution)/shard_map/ppermute | solution.py:145
  282.3 35.1 %collective-permute-start.36 = (bf16[4,288,576]{2,1,0:T(8,128)(2,1)S(1)}, bf16[4,288,576]{2,1,0:T(8,128)(2,1)S(1)}, u32[]{:S(2)}, u32[]{:S(2)}) collective-permute-start(bf16[4,288,576]{2,1,0:T(8,128)(2,1)S(1)} %copy-done.27), channel_id=1, source_target_pairs={{0,1},{1,0},{2,3},{3,2},{4,5},{5,4},{6,7},{7,6},{8,9},{9,8},{10,11... | collective-permute-start | bytes 3981320 | tf_op jit(solution)/shard_map/ppermute | solution.py:145
  283.9 55.6 %collective-permute-start.8 = (bf16[4,72,1728]{2,1,0:T(8,128)(2,1)}, bf16[4,72,1728]{2,1,0:T(8,128)(2,1)S(1)}, u32[]{:S(2)}, u32[]{:S(2)}) collective-permute-start(bf16[4,72,1728]{2,1,0:T(8,128)(2,1)} %collective-permute-done.4), channel_id=1, source_target_pairs={{0,1},{1,0},{2,3},{3,2},{4,5},{5,4},{6,7},{7,6},{8,9},{9,8},{10,11... | collective-permute-start | bytes 2985992 | tf_op jit(solution)/shard_map/ppermute | solution.py:145
  317.4 50.2 %collective-permute-start.28 = (bf16[4,72,2304]{2,1,0:T(8,128)(2,1)S(1)}, bf16[4,72,2304]{2,1,0:T(8,128)(2,1)}, u32[]{:S(2)}, u32[]{:S(2)}) collective-permute-start(bf16[4,72,2304]{2,1,0:T(8,128)(2,1)S(1)} %collective-permute-done.24), channel_id=1, source_target_pairs={{0,1},{1,0},{2,3},{3,2},{4,5},{5,4},{6,7},{7,6},{8,9},{9,8},{10,11... | collective-permute-start | bytes 3981320 | tf_op jit(solution)/shard_map/ppermute | solution.py:145
  317.7 49.9 %collective-permute-start.25 = (bf16[4,72,2304]{2,1,0:T(8,128)(2,1)S(1)}, bf16[4,72,2304]{2,1,0:T(8,128)(2,1)S(1)}, u32[]{:S(2)}, u32[]{:S(2)}) collective-permute-start(bf16[4,72,2304]{2,1,0:T(8,128)(2,1)S(1)} %collective-permute-done.24), channel_id=1, source_target_pairs={{0,2},{2,0},{1,3},{3,1},{4,6},{6,4},{5,7},{7,5},{8,10},{10,8},{9,1... | collective-permute-start | bytes 3981320 | tf_op jit(solution)/shard_map/ppermute | solution.py:145
  339.5 33.5 %collective-permute-start.38 = (bf16[4,288,576]{2,1,0:T(8,128)(2,1)S(1)}, bf16[4,288,576]{2,1,0:T(8,128)(2,1)}, u32[]{:S(2)}, u32[]{:S(2)}) collective-permute-start(bf16[4,288,576]{2,1,0:T(8,128)(2,1)S(1)} %collective-permute-done.36), channel_id=1, source_target_pairs={{0,4},{4,0},{1,5},{5,1},{2,6},{6,2},{3,7},{7,3},{8,12},{12,8},{9,1... | collective-permute-start | bytes 3981320 | tf_op jit(solution)/shard_map/ppermute | solution.py:145
  342.3 35.6 %collective-permute-start.37 = (bf16[4,288,576]{2,1,0:T(8,128)(2,1)S(1)}, bf16[4,288,576]{2,1,0:T(8,128)(2,1)S(1)}, u32[]{:S(2)}, u32[]{:S(2)}) collective-permute-start(bf16[4,288,576]{2,1,0:T(8,128)(2,1)S(1)} %collective-permute-done.36), channel_id=1, source_target_pairs={{0,2},{2,0},{1,3},{3,1},{4,6},{6,4},{5,7},{7,5},{8,10},{10,8},{9,1... | collective-permute-start | bytes 3981320 | tf_op jit(solution)/shard_map/ppermute | solution.py:145
  342.3 34.4 %collective-permute-start.27 = (bf16[4,72,2304]{2,1,0:T(8,128)(2,1)}, bf16[4,72,2304]{2,1,0:T(8,128)(2,1)S(1)}, u32[]{:S(2)}, u32[]{:S(2)}) collective-permute-start(bf16[4,72,2304]{2,1,0:T(8,128)(2,1)} %collective-permute-done.26), channel_id=1, source_target_pairs={{0,2},{2,0},{1,3},{3,1},{4,6},{6,4},{5,7},{7,5},{8,10},{10,8},{9,1... | collective-permute-start | bytes 3981320 | tf_op jit(solution)/shard_map/ppermute | solution.py:145
  367.6 185.3 %collective-permute-start.29 = (bf16[4,72,2304]{2,1,0:T(8,128)(2,1)}, bf16[4,72,2304]{2,1,0:T(8,128)(2,1)}, u32[]{:S(2)}, u32[]{:S(2)}) collective-permute-start(bf16[4,72,2304]{2,1,0:T(8,128)(2,1)} %collective-permute-done.28), channel_id=1, source_target_pairs={{0,2},{2,0},{1,3},{3,1},{4,6},{6,4},{5,7},{7,5},{8,10},{10,8},{9,1... | collective-permute-start | bytes 3981320 | tf_op jit(solution)/shard_map/ppermute | solution.py:145
  373.0 265.2 %collective-permute-start.39 = (bf16[4,288,576]{2,1,0:T(8,128)(2,1)}, bf16[4,288,576]{2,1,0:T(8,128)(2,1)}, u32[]{:S(2)}, u32[]{:S(2)}) collective-permute-start(bf16[4,288,576]{2,1,0:T(8,128)(2,1)} %collective-permute-done.38), channel_id=1, source_target_pairs={{0,2},{2,0},{1,3},{3,1},{4,6},{6,4},{5,7},{7,5},{8,10},{10,8},{9,1... | collective-permute-start | bytes 3981320 | tf_op jit(solution)/shard_map/ppermute | solution.py:145
  1054.1 156.3 %collective-permute-start.75 = (bf16[4,288,576]{2,1,0:T(8,128)(2,1)}, bf16[4,288,576]{2,1,0:T(8,128)(2,1)}, u32[]{:S(2)}, u32[]{:S(2)}) collective-permute-start(bf16[4,288,576]{2,1,0:T(8,128)(2,1)} %fusion.119), channel_id=1, source_target_pairs={{0,2},{2,0},{1,3},{3,1},{4,6},{6,4},{5,7},{7,5},{8,10},{10,8},{9,1... | collective-permute-start | bytes 3981320 | tf_op jit(solution)/shard_map/ppermute | solution.py:145
  1054.6 117.2 %collective-permute-start.52 = (bf16[4,72,576]{2,1,0:T(8,128)(2,1)}, bf16[4,72,576]{2,1,0:T(8,128)(2,1)}, u32[]{:S(2)}, u32[]{:S(2)}) collective-permute-start(bf16[4,72,576]{2,1,0:T(8,128)(2,1)} %convolution_convert_fusion.11), channel_id=1, source_target_pairs={{0,2},{2,0},{1,3},{3,1},{4,6},{6,4},{5,7},{7,5},{8,10},{10,8},{9,1... | collective-permute-start | bytes 995336 | tf_op jit(solution)/shard_map/ppermute | solution.py:145
  1054.6 115.0 %collective-permute-start.55 = (bf16[4,72,576]{2,1,0:T(8,128)(2,1)}, bf16[4,72,576]{2,1,0:T(8,128)(2,1)}, u32[]{:S(2)}, u32[]{:S(2)}) collective-permute-start(bf16[4,72,576]{2,1,0:T(8,128)(2,1)} %convolution_convert_fusion.9), channel_id=1, source_target_pairs={{0,2},{2,0},{1,3},{3,1},{4,6},{6,4},{5,7},{7,5},{8,10},{10,8},{9,1... | collective-permute-start | bytes 995336 | tf_op jit(solution)/shard_map/ppermute | solution.py:145
  1055.1 130.5 %collective-permute-start.51 = (bf16[4,72,576]{2,1,0:T(8,128)(2,1)}, bf16[4,72,576]{2,1,0:T(8,128)(2,1)}, u32[]{:S(2)}, u32[]{:S(2)}) collective-permute-start(bf16[4,72,576]{2,1,0:T(8,128)(2,1)} %convolution_convert_fusion.12), channel_id=1, source_target_pairs={{0,2},{2,0},{1,3},{3,1},{4,6},{6,4},{5,7},{7,5},{8,10},{10,8},{9,1... | collective-permute-start | bytes 995336 | tf_op jit(solution)/shard_map/ppermute | solution.py:145
  1055.2 120.3 %collective-permute-start.54 = (bf16[4,72,576]{2,1,0:T(8,128)(2,1)}, bf16[4,72,576]{2,1,0:T(8,128)(2,1)}, u32[]{:S(2)}, u32[]{:S(2)}) collective-permute-start(bf16[4,72,576]{2,1,0:T(8,128)(2,1)} %convolution_convert_fusion.10), channel_id=1, source_target_pairs={{0,2},{2,0},{1,3},{3,1},{4,6},{6,4},{5,7},{7,5},{8,10},{10,8},{9,1... | collective-permute-start | bytes 995336 | tf_op jit(solution)/shard_map/ppermute | solution.py:145
  1117.6 41.5 %all-to-all-start.4 = ((f32[32,1,288]{2,1,0:T(1,128)}), f32[32,1,288]{2,1,0:T(1,128)S(1)}, u32[]{:S(2)}, u32[]{:S(2)}) async-start(f32[32,1,288]{2,1,0:T(1,128)} %all_to_all.75), calls=%async_computation.4 | async-start | bytes 98304 | tf_op jit(solution)/shard_map/all_to_all | solution.py:399
  1214.1 35.2 %collective-permute-start.76 = (bf16[4,288,576]{2,1,0:T(8,128)(2,1)S(1)}, bf16[4,288,576]{2,1,0:T(8,128)(2,1)S(1)}, u32[]{:S(2)}, u32[]{:S(2)}) collective-permute-start(bf16[4,288,576]{2,1,0:T(8,128)(2,1)S(1)} %add_convert_fusion.4), channel_id=1, source_target_pairs={{0,1},{1,0},{2,3},{3,2},{4,5},{5,4},{6,7},{7,6},{8,9},{9,8},{10,11... | collective-permute-start | bytes 3981320 | tf_op jit(solution)/shard_map/ppermute | solution.py:145
  1234.3 37.1 %collective-permute-start.47 = (bf16[4,72,1728]{2,1,0:T(8,128)(2,1)S(1)}, bf16[4,72,1728]{2,1,0:T(8,128)(2,1)S(1)}, u32[]{:S(2)}, u32[]{:S(2)}) collective-permute-start(bf16[4,72,1728]{2,1,0:T(8,128)(2,1)S(1)} %add_convert_fusion.17), channel_id=1, source_target_pairs={{0,1},{1,0},{2,3},{3,2},{4,5},{5,4},{6,7},{7,6},{8,9},{9,8},{10,11... | collective-permute-start | bytes 2985992 | tf_op jit(solution)/shard_map/ppermute | solution.py:145
  1237.3 36.4 %collective-permute-start.71 = (bf16[4,288,576]{2,1,0:T(8,128)(2,1)S(1)}, bf16[4,288,576]{2,1,0:T(8,128)(2,1)S(1)}, u32[]{:S(2)}, u32[]{:S(2)}) collective-permute-start(bf16[4,288,576]{2,1,0:T(8,128)(2,1)S(1)} %copy-done.120), channel_id=1, source_target_pairs={{0,2},{2,0},{1,3},{3,1},{4,6},{6,4},{5,7},{7,5},{8,10},{10,8},{9,1... | collective-permute-start | bytes 3981320 | tf_op jit(solution)/shard_map/ppermute | solution.py:145
  1237.4 36.6 %collective-permute-start.64 = (bf16[4,72,2304]{2,1,0:T(8,128)(2,1)S(1)}, bf16[4,72,2304]{2,1,0:T(8,128)(2,1)S(1)}, u32[]{:S(2)}, u32[]{:S(2)}) collective-permute-start(bf16[4,72,2304]{2,1,0:T(8,128)(2,1)S(1)} %copy-done.124), channel_id=1, source_target_pairs={{0,2},{2,0},{1,3},{3,1},{4,6},{6,4},{5,7},{7,5},{8,10},{10,8},{9,1... | collective-permute-start | bytes 3981320 | tf_op jit(solution)/shard_map/ppermute | solution.py:145
  1249.3 38.5 %collective-permute-start.66 = (bf16[4,72,2304]{2,1,0:T(8,128)(2,1)S(1)}, bf16[4,72,2304]{2,1,0:T(8,128)(2,1)S(1)}, u32[]{:S(2)}, u32[]{:S(2)}) collective-permute-start(bf16[4,72,2304]{2,1,0:T(8,128)(2,1)S(1)} %add_convert_fusion.11), channel_id=1, source_target_pairs={{0,4},{4,0},{1,5},{5,1},{2,6},{6,2},{3,7},{7,3},{8,12},{12,8},{9,1... | collective-permute-start | bytes 3981320 | tf_op jit(solution)/shard_map/ppermute | solution.py:145
  1259.4 44.8 %collective-permute-start.73 = (bf16[4,288,576]{2,1,0:T(8,128)(2,1)S(1)}, bf16[4,288,576]{2,1,0:T(8,128)(2,1)S(1)}, u32[]{:S(2)}, u32[]{:S(2)}) collective-permute-start(bf16[4,288,576]{2,1,0:T(8,128)(2,1)S(1)} %add_convert_fusion.7), channel_id=1, source_target_pairs={{0,1},{1,0},{2,3},{3,2},{4,5},{5,4},{6,7},{7,6},{8,9},{9,8},{10,11... | collective-permute-start | bytes 3981320 | tf_op jit(solution)/shard_map/ppermute | solution.py:145
  1271.4 48.0 %collective-permute-start.77 = (bf16[4,288,576]{2,1,0:T(8,128)(2,1)S(1)}, bf16[4,288,576]{2,1,0:T(8,128)(2,1)S(1)}, u32[]{:S(2)}, u32[]{:S(2)}) collective-permute-start(bf16[4,288,576]{2,1,0:T(8,128)(2,1)S(1)} %add_convert_fusion.3), channel_id=1, source_target_pairs={{0,4},{4,0},{1,5},{5,1},{2,6},{6,2},{3,7},{7,3},{8,12},{12,8},{9,1... | collective-permute-start | bytes 3981320 | tf_op jit(solution)/shard_map/ppermute | solution.py:145
  1288.6 35.4 %collective-permute-start.61 = (bf16[4,72,2304]{2,1,0:T(8,128)(2,1)S(1)}, bf16[4,72,2304]{2,1,0:T(8,128)(2,1)S(1)}, u32[]{:S(2)}, u32[]{:S(2)}) collective-permute-start(bf16[4,72,2304]{2,1,0:T(8,128)(2,1)S(1)} %copy-done.123), channel_id=1, source_target_pairs={{0,2},{2,0},{1,3},{3,1},{4,6},{6,4},{5,7},{7,5},{8,10},{10,8},{9,1... | collective-permute-start | bytes 3981320 | tf_op jit(solution)/shard_map/ppermute | solution.py:145
  1288.7 57.8 %collective-permute-start.63 = (bf16[4,72,2304]{2,1,0:T(8,128)(2,1)S(1)}, bf16[4,72,2304]{2,1,0:T(8,128)(2,1)S(1)}, u32[]{:S(2)}, u32[]{:S(2)}) collective-permute-start(bf16[4,72,2304]{2,1,0:T(8,128)(2,1)S(1)} %add_convert_fusion.14), channel_id=1, source_target_pairs={{0,4},{4,0},{1,5},{5,1},{2,6},{6,2},{3,7},{7,3},{8,12},{12,8},{9,1... | collective-permute-start | bytes 3981320 | tf_op jit(solution)/shard_map/ppermute | solution.py:145
  1299.9 46.7 %collective-permute-start.67 = (bf16[4,72,2304]{2,1,0:T(8,128)(2,1)S(1)}, bf16[4,72,2304]{2,1,0:T(8,128)(2,1)S(1)}, u32[]{:S(2)}, u32[]{:S(2)}) collective-permute-start(bf16[4,72,2304]{2,1,0:T(8,128)(2,1)S(1)} %add_convert_fusion.10), channel_id=1, source_target_pairs={{0,1},{1,0},{2,3},{3,2},{4,5},{5,4},{6,7},{7,6},{8,9},{9,8},{10,11... | collective-permute-start | bytes 3981320 | tf_op jit(solution)/shard_map/ppermute | solution.py:145
  1320.1 31.0 %collective-permute-start.78 = (bf16[288,576]{1,0:T(8,128)(2,1)S(1)}, bf16[288,576]{1,0:T(8,128)(2,1)S(1)}, u32[]{:S(2)}, u32[]{:S(2)}) collective-permute-start(bf16[288,576]{1,0:T(8,128)(2,1)S(1)} %get-tuple-element.374), channel_id=1, source_target_pairs={{0,8},{8,16},{16,24},{24,0},{1,9},{9,17},{17,25},{25,1},{2,10},{10... | collective-permute-start | bytes 995336 | tf_op jit(solution)/shard_map/ppermute | solution.py:149
  1320.4 30.8 %collective-permute-start.80 = (bf16[288,576]{1,0:T(8,128)(2,1)S(1)}, bf16[288,576]{1,0:T(8,128)(2,1)S(1)}, u32[]{:S(2)}, u32[]{:S(2)}) collective-permute-start(bf16[288,576]{1,0:T(8,128)(2,1)S(1)} %get-tuple-element.375), channel_id=1, source_target_pairs={{0,24},{8,0},{16,8},{24,16},{1,25},{9,1},{17,9},{25,17},{2,26},{10... | collective-permute-start | bytes 995336 | tf_op jit(solution)/shard_map/ppermute | solution.py:149
  1324.0 37.0 %collective-permute-start.79 = (bf16[288,576]{1,0:T(8,128)(2,1)S(1)}, bf16[288,576]{1,0:T(8,128)(2,1)S(1)}, u32[]{:S(2)}, u32[]{:S(2)}) collective-permute-start(bf16[288,576]{1,0:T(8,128)(2,1)S(1)} %get-tuple-element.376), channel_id=1, source_target_pairs={{0,16},{8,24},{16,0},{24,8},{1,17},{9,25},{17,1},{25,9},{2,18},{10... | collective-permute-start | bytes 995336 | tf_op jit(solution)/shard_map/ppermute | solution.py:149
  1351.2 30.7 %collective-permute-start.69 = (bf16[72,2304]{1,0:T(8,128)(2,1)S(1)}, bf16[72,2304]{1,0:T(8,128)(2,1)S(1)}, u32[]{:S(2)}, u32[]{:S(2)}) collective-permute-start(bf16[72,2304]{1,0:T(8,128)(2,1)S(1)} %get-tuple-element.379), channel_id=1, source_target_pairs={{0,16},{8,24},{16,0},{24,8},{1,17},{9,25},{17,1},{25,9},{2,18},{10... | collective-permute-start | bytes 995336 | tf_op jit(solution)/shard_map/ppermute | solution.py:149
  (199 other events, 3004.7 us)

commit v2 on v1

--- a/solution.py
+++ b/solution.py
@@ -3,13 +3,27 @@
 import jax
 import jax.numpy as jnp
 from jax import lax
+from jax.experimental import pallas as pl
+from jax.experimental.pallas import tpu as pltpu
 from jax.sharding import Mesh
 from jax.sharding import PartitionSpec as P
 
 D = 1152
 HEADS = 16
+HEAD = 72
 FF = 4608
-
+LANES = 128
+CHUNK = 256
+
+ROWS = ("far", "near", "core")
+ALL = ("far", "near", "core", "mod")
+LOW = jnp.bfloat16
+WIDE = jnp.float32
+LOG2E = 1.4426950408889634
+NEG = -1e30
+MESH = pl.DeviceIdType.MESH
+VMEM = pl.BlockSpec(memory_space=pltpu.VMEM)
+ANY = pl.BlockSpec(memory_space=pl.ANY)
 
 EPS = 1e-06
 MOMENTUM = 0.9
@@ -50,95 +64,349 @@
     return (weight, moment, average)
 
 
-def masked_scores(query_part, seg_part, key_rows, segments, scaling):
-    scores = (
-        jnp.einsum("qhd,khd->hqk", query_part, key_rows, preferred_element_type=jnp.float32)
-        * scaling
-    )
-    allowed = seg_part[:, None] == segments[None, :]
-    return jnp.where(allowed[None], scores, -1e30)
-
-
-def attend_forward(query_rows, key_rows, value_rows, segments, block_rows):
-    tokens, head_count, head_width = query_rows.shape
-    scaling = head_width ** (-0.5)
-    blocks = tokens // block_rows
-
-    def one_block(inputs):
-        query_part, seg_part = inputs
-        scores = masked_scores(query_part, seg_part, key_rows, segments, scaling)
-        largest = jnp.max(scores, axis=-1, keepdims=True)
-        weights = jnp.exp(scores - largest)
-        totals = jnp.sum(weights, axis=-1, keepdims=True)
-        softmax_low = (weights / totals).astype(jnp.bfloat16)
-        mixture = jnp.einsum(
-            "hqk,khd->qhd", softmax_low, value_rows, preferred_element_type=jnp.float32
+def places():
+    return {name: lax.axis_index(name) for name in ALL}
+
+
+def greet():
+    here = places()
+    count = lax.axis_size("far")
+    others = [dict(far=lax.rem(here["far"] + d, count)) for d in range(1, count)]
+    others += [{name: 1 - here[name]} for name in ("near", "core", "mod")]
+    barrier = pltpu.get_barrier_semaphore()
+    for other in others:
+        pl.semaphore_signal(barrier, inc=1, device_id=other, device_id_type=MESH)
+    pl.semaphore_wait(barrier, len(others))
+
+
+def remote(source, target, sends, receives, slot, other):
+    return pltpu.make_async_remote_copy(
+        src_ref=source,
+        dst_ref=target,
+        send_sem=sends.at[slot],
+        recv_sem=receives.at[slot],
+        device_id=other,
+        device_id_type=MESH,
+    )
+
+
+def messages(count):
+    return count - 1 + 8
+
+
+class Gather:
+    def __init__(self, whole, sends, receives):
+        self.whole, self.sends, self.receives = whole, sends, receives
+        self.here = places()
+        self.count = lax.axis_size("far")
+        rows = whole.shape[4]
+        self.rows = rows
+        self.split = rows if rows % 16 else 8 * ((rows // 8 + 1) // 2)
+
+    def _block(self, far):
+        return self.whole.at[self.here["mod"], far, self.here["near"], self.here["core"]]
+
+    def _far(self, shard, distance):
+        far = self.here["far"]
+        other = dict(far=lax.rem(far + distance, self.count))
+        return remote(shard, self._block(far), self.sends, self.receives, distance - 1, other)
+
+    def _far_came(self, shard, distance):
+        origin = lax.rem(self.here["far"] + self.count - distance, self.count)
+        return remote(
+            shard, self._block(origin), self.sends, self.receives, distance - 1, dict(far=origin)
         )
-        return (mixture.astype(jnp.bfloat16), (largest + jnp.log(totals))[..., 0])
-
-    mixture, log_totals = lax.map(
-        one_block,
-        (
-            query_rows.reshape(blocks, block_rows, head_count, head_width),
-            segments.reshape(blocks, block_rows),
+
+    def start_far(self, shard, local):
+        pltpu.make_async_copy(shard, self._block(self.here["far"]), local).start()
+        for distance in range(1, self.count):
+            self._far(shard, distance).start()
+
+    def finish_far(self, shard, local):
+        pltpu.make_async_copy(shard, self._block(self.here["far"]), local).wait()
+        for distance in range(1, self.count):
+            self._far(shard, distance).wait_send()
+            self._far_came(shard, distance).wait_recv()
+
+    def _quad(self, flips, first, size):
+        near, core, mod = (
+            1 - self.here[name] if name in flips else self.here[name] for name in ("near", "core", "mod")
+        )
+        return self.whole.at[mod, :, near, core, pl.ds(first, size)]
+
+    def _step(self, name):
+        head, rest = (0, self.split), (self.split, self.rows - self.split)
+        full = (0, self.rows)
+        return {
+            "near": ((), "near", full, 0),
+            "mod": ((), "mod", full, 1),
+            "near_mod": (("near",), "mod", head, 2),
+            "mod_near": (("mod",), "near", rest, 3),
+            "core": ((), "core", full, 4),
+            "near_core": (("near",), "core", full, 5),
+            "mod_core": (("mod",), "core", full, 6),
+            "both_core": (("near", "mod"), "core", full, 7),
+        }[name]
+
+    def _copy(self, name, incoming):
+        flips, axis, span, slot = self._step(name)
+        if span[1] == 0:
+            return None
+        quad = self._quad(flips + (axis,) if incoming else flips, *span)
+        other = {axis: 1 - self.here[axis]}
+        return remote(quad, quad, self.sends, self.receives, self.count - 1 + slot, other)
+
+    def start(self, *names):
+        for name in names:
+            copy = self._copy(name, False)
+            if copy is not None:
+                copy.start()
+
+    def receive(self, *names):
+        for name in names:
+            copy = self._copy(name, True)
+            if copy is not None:
+                copy.wait_recv()
+
+    def spread(self):
+        self.start("near", "mod", "core")
+
+    def cross(self):
+        self.receive("near")
+        self.start("near_mod", "near_core")
+        self.receive("mod")
+        self.start("mod_near", "mod_core")
+
+    def close(self):
+        self.receive("near_mod", "mod_near")
+        self.start("both_core")
+
+    def end(self):
+        self.receive("core", "near_core", "mod_core", "both_core")
+        for name in (
+            "near", "mod", "near_mod", "mod_near", "core", "near_core", "mod_core", "both_core",
+        ):
+            copy = self._copy(name, False)
+            if copy is not None:
+                copy.wait_send()
+
+
+def gather_scratch(weights, locals_):
+    count = lax.axis_size("far")
+    shapes = [pltpu.SemaphoreType.DMA((messages(count),))] * (2 * weights)
+    return shapes + [pltpu.SemaphoreType.DMA((locals_,))]
+
+
+def whole_shape(shard):
+    return jax.ShapeDtypeStruct((2, lax.axis_size("far"), 2, 2) + shard.shape, LOW)
+
+
+def first_kernel(*refs):
+    qkv_s, proj_s, fc1_s, qkv_w, proj_w, fc1_w = refs[:6]
+    *sems, local = refs[6:]
+    qkv, proj, fc1 = (
+        Gather(w, s, r) for w, s, r in zip((qkv_w, proj_w, fc1_w), sems[0::2], sems[1::2])
+    )
+    greet()
+    qkv.start_far(qkv_s, local.at[0])
+    proj.start_far(proj_s, local.at[1])
+    fc1.start_far(fc1_s, local.at[2])
+    qkv.finish_far(qkv_s, local.at[0])
+    qkv.spread()
+    qkv.cross()
+    qkv.close()
+    qkv.end()
+    proj.finish_far(proj_s, local.at[1])
+    fc1.finish_far(fc1_s, local.at[2])
+
+
+def first_gather(qkv_s, proj_s, fc1_s):
+    shards = (qkv_s, proj_s, fc1_s)
+    return pl.pallas_call(
+        first_kernel,
+        out_shape=tuple(whole_shape(shard) for shard in shards),
+        in_specs=[VMEM] * 3,
+        out_specs=(ANY,) * 3,
+        scratch_shapes=gather_scratch(3, 3),
+        compiler_params=pltpu.CompilerParams(collective_id=0, has_side_effects=True),
+        name="first_gather",
+    )(*shards)
+
+
+def lanes(shape): return lax.broadcasted_iota(jnp.int32, shape, 1)
+
+def seg_codes(seg, n):
+    lane = lanes((n, LANES))
+    code = lane - HEAD
+    inside = jnp.logical_and(code >= 0, code < 4)
+    same = code == seg
+    q = jnp.where(jnp.logical_and(inside, same), 1.0, 0.0)
+    k = jnp.where(jnp.logical_and(inside, jnp.logical_not(same)), NEG, 0.0)
+    return q, k
+
+def head_of(wide_rows, start):
+    return wide_rows[:, start:start+HEAD]
+
+def pad_head(part, aug):
+    n = part.shape[0]
+    full = jnp.concatenate([part, jnp.zeros((n, LANES-HEAD), part.dtype)], axis=1)
+    return jnp.where(lanes((n,LANES)) < HEAD, full, aug)
+
+def attend_kernel(*refs):
+    qkv_ref, seg_ref, fc2_s = refs[:3]
+    mixed_ref, lse_ref, proj_w, fc1_w, fc2_w = refs[5:10]
+    qh, kh, vh = refs[10:13]
+    *sems, local = refs[13:]
+    proj, fc1, fc2 = (
+        Gather(w, s, r) for w, s, r in zip((proj_w, fc1_w, fc2_w), sems[0::2], sems[1::2])
+    )
+    greet()
+    fc2.start_far(fc2_s, local.at[0])
+    proj.spread()
+    fc1.spread()
+
+    T = qkv_ref.shape[0]
+    D = HEADS*HEAD
+    def fill(i, carry):
+        rows = pl.ds(pl.multiple_of(i*CHUNK, CHUNK), CHUNK)
+        lane = lanes((CHUNK, LANES))
+        qc, kc = seg_codes(seg_ref[rows, :], CHUNK)
+        qc = qc.astype(LOW); kc = kc.astype(LOW)
+        ones = jnp.where(jnp.logical_and(lane >= HEAD, lane < HEAD+3), 1.0, 0.0).astype(LOW)
+        for h in range(HEADS):
+            qh[h, rows, :] = pad_head(qkv_ref[rows, h*HEAD:(h+1)*HEAD], qc)
+            kh[h, rows, :] = pad_head(qkv_ref[rows, D+h*HEAD:D+(h+1)*HEAD], kc)
+            vh[h, rows, :] = pad_head(qkv_ref[rows, 2*D+h*HEAD:2*D+(h+1)*HEAD], ones)
+        return carry
+    lax.fori_loop(0, T//CHUNK, fill, 0)
+    lse_ref[...] = jnp.zeros_like(lse_ref)
+    def head(h, carry):
+        k = kh[h]; v = vh[h]
+        for i in range(T//CHUNK):
+            rows = pl.ds(i*CHUNK, CHUNK)
+            q = qh[h, rows, :]
+            s = lax.dot_general(q, k, (((1,),(1,)),((),())), preferred_element_type=WIDE)
+            m = jnp.max(s, axis=1, keepdims=True)
+            p = jnp.exp2((s - m)*(HEAD**-0.5*LOG2E)).astype(LOW)
+            o = jnp.dot(p, v, preferred_element_type=WIDE)
+            l = o[:, HEAD:HEAD+1]
+            qh[h, rows, :] = (o / l).astype(LOW)
+            col = m*HEAD**-0.5 + jnp.log(l)
+            lse_ref[rows, :] = jnp.where(lanes((CHUNK,LANES)) == h, col, lse_ref[rows, :])
+        tasks = {
+            2: proj.cross,
+            5: proj.close,
+            7: proj.end,
+            9: lambda: fc2.finish_far(fc2_s, local.at[0]),
+            10: fc2.spread,
+            11: fc1.cross,
+        }
+        for at, task in tasks.items():
+            pl.when(h == at)(task)
+        return carry
+    lax.fori_loop(0, HEADS, head, 0)
+    def drain(i, carry):
+        rows = pl.ds(pl.multiple_of(i*CHUNK, CHUNK), CHUNK)
+        mixed_ref[rows, :] = jnp.concatenate([qh[h, rows, :][:, :HEAD] for h in range(HEADS)], axis=1)
+        return carry
+    lax.fori_loop(0, T//CHUNK, drain, 0)
+    fc1.close()
+    fc2.cross()
+    fc1.end()
+    fc2.close()
+    fc2.end()
+
+
+def attend(qkv, segments, fc2_s, proj_w, fc1_w):
+    tokens = qkv.shape[0]
+    return pl.pallas_call(
+        attend_kernel,
+        out_shape=(
+            jax.ShapeDtypeStruct((tokens, HEADS * HEAD), LOW),
+            jax.ShapeDtypeStruct((tokens, LANES), WIDE),
+            jax.ShapeDtypeStruct(proj_w.shape, LOW),
+            jax.ShapeDtypeStruct(fc1_w.shape, LOW),
+            whole_shape(fc2_s),
         ),
-    )
-    return (mixture.reshape(tokens, head_count * head_width), log_totals)
-
-
-def attend_backward(query_rows, key_rows, value_rows, segments, log_totals, upstream, block_rows):
-    tokens, head_count, head_width = query_rows.shape
-    scaling = head_width ** (-0.5)
-    blocks = tokens // block_rows
-
-    def one_block(carried, inputs):
-        key_grad, value_grad = carried
-        query_part, seg_part, log_part, up_part = inputs
-        scores = masked_scores(query_part, seg_part, key_rows, segments, scaling)
-        softmax = jnp.exp(scores - log_part[..., None])
-        softmax_low = softmax.astype(jnp.bfloat16)
-        value_grad = value_grad + jnp.einsum(
-            "hqk,qhd->khd", softmax_low, up_part, preferred_element_type=jnp.float32
-        )
-        prob_grad = jnp.einsum(
-            "qhd,khd->hqk", up_part, value_rows, preferred_element_type=jnp.float32
-        )
-        centred = prob_grad - jnp.sum(softmax * prob_grad, axis=-1, keepdims=True)
-        score_grad = (softmax * centred).astype(jnp.bfloat16)
-        query_grad = (
-            jnp.einsum("hqk,khd->qhd", score_grad, key_rows, preferred_element_type=jnp.float32)
-            * scaling
-        )
-        key_grad = (
-            key_grad
-            + jnp.einsum("hqk,qhd->khd", score_grad, query_part, preferred_element_type=jnp.float32)
-            * scaling
-        )
-        return ((key_grad, value_grad), query_grad.astype(jnp.bfloat16))
-
-    zeroes = jnp.zeros(key_rows.shape, jnp.float32)
-    carried, query_grad = lax.scan(
-        one_block,
-        (zeroes, zeroes),
-        (
-            query_rows.reshape(blocks, block_rows, head_count, head_width),
-            segments.reshape(blocks, block_rows),
-            log_totals,
-            upstream.reshape(blocks, block_rows, head_count, head_width),
+        in_specs=[VMEM] * 3 + [ANY] * 2,
+        out_specs=(VMEM,) * 2 + (ANY,) * 3,
+        scratch_shapes=[pltpu.VMEM((HEADS, tokens, LANES), LOW)] * 3 + gather_scratch(3, 1),
+        input_output_aliases={3: 2, 4: 3},
+        compiler_params=pltpu.CompilerParams(
+            collective_id=1, has_side_effects=True, vmem_limit_bytes=50 * 2**20
         ),
-    )
-    full_width = head_count * head_width
-    return (
-        query_grad.reshape(tokens, full_width),
-        carried[0].reshape(tokens, full_width).astype(jnp.bfloat16),
-        carried[1].reshape(tokens, full_width).astype(jnp.bfloat16),
-    )
-
-
-ROWS = ("far", "near", "core")
-ALL = ("far", "near", "core", "mod")
-LOW = jnp.bfloat16
-WIDE = jnp.float32
+        name="attend",
+    )(qkv, segments.reshape(tokens, 1), fc2_s, proj_w, fc1_w)
+
+
+def split3(v):
+    hi = v.astype(LOW).astype(WIDE)
+    mid = (v-hi).astype(LOW).astype(WIDE)
+    lo = (v-hi-mid)
+    return hi, mid, lo
+
+def attend_back_kernel(qkv_ref, seg_ref, mixed_ref, lse_ref, up_ref, out_ref, qh, kh, vh, uh):
+    T = qkv_ref.shape[0]
+    D = HEADS*HEAD
+    def fill(i, carry):
+        rows = pl.ds(pl.multiple_of(i*CHUNK, CHUNK), CHUNK)
+        lane = lanes((CHUNK, LANES))
+        qc, kc = seg_codes(seg_ref[rows, :], CHUNK)
+        kc = jnp.where(jnp.logical_and(lane >= HEAD+4, lane < HEAD+7), 1.0, kc).astype(LOW)
+        ones = jnp.where(jnp.logical_and(lane >= HEAD, lane < HEAD+3), 1.0, 0.0).astype(LOW)
+        def spread(v, at, base):
+            hi, mid, lo = split3(v)
+            return jnp.where(lane == at, hi, jnp.where(lane == at+1, mid, jnp.where(lane == at+2, lo, base)))
+        for h in range(HEADS):
+            a, b = h*HEAD, (h+1)*HEAD
+            qa = spread(-lse_ref[rows, h:h+1]*(1.0/HEAD**-0.5), HEAD+4, qc).astype(LOW)
+            qh[h, rows, :] = pad_head(qkv_ref[rows, a:b], qa)
+            kh[h, rows, :] = pad_head(qkv_ref[rows, D+a:D+b], kc)
+            vh[h, rows, :] = pad_head(qkv_ref[rows, 2*D+a:2*D+b], ones)
+            u = up_ref[rows, a:b]
+            delta = jnp.sum(u.astype(WIDE)*mixed_ref[rows, a:b].astype(WIDE), axis=1, keepdims=True)
+            ua = spread(-delta, HEAD, jnp.zeros((CHUNK,LANES),WIDE)).astype(LOW)
+            uh[h, rows, :] = pad_head(u, ua)
+        return carry
+    lax.fori_loop(0, T//CHUNK, fill, 0)
+    NT = (((1,),(1,)),((),()))
+    def head(h, carry):
+        k = kh[h]; v = vh[h]
+        kt = k.T
+        dk = jnp.zeros((T, LANES), WIDE); dv = jnp.zeros((T, LANES), WIDE)
+        for i in range(T//CHUNK):
+            rows = pl.ds(i*CHUNK, CHUNK)
+            q = qh[h, rows, :]; u = uh[h, rows, :]
+            s = lax.dot_general(k, q, NT, preferred_element_type=WIDE)
+            p = jnp.exp2(s*(HEAD**-0.5*LOG2E))
+            dp = lax.dot_general(v, u, NT, preferred_element_type=WIDE)
+            ds = (p*dp).astype(LOW)
+            dv = dv + jnp.dot(p.astype(LOW), u, preferred_element_type=WIDE)
+            dk = dk + jnp.dot(ds, q, preferred_element_type=WIDE)
+            dqt = jnp.dot(kt, ds, preferred_element_type=WIDE)
+            qh[h, rows, :] = (dqt.T*HEAD**-0.5).astype(LOW)
+        kh[h] = (dk*HEAD**-0.5).astype(LOW)
+        vh[h] = dv.astype(LOW)
+        return carry
+    lax.fori_loop(0, HEADS, head, 0)
+    def drain(i, carry):
+        rows = pl.ds(pl.multiple_of(i*CHUNK, CHUNK), CHUNK)
+        out_ref[rows, :] = jnp.concatenate([g[h, rows, :][:, :HEAD] for g in (qh,kh,vh) for h in range(HEADS)], axis=1)
+        return carry
+    lax.fori_loop(0, T//CHUNK, drain, 0)
+
+
+def attend_back(qkv, segments, mixed, lse, upstream):
+    tokens = qkv.shape[0]
+    return pl.pallas_call(
+        attend_back_kernel,
+        out_shape=jax.ShapeDtypeStruct((tokens, 3 * HEADS * HEAD), LOW),
+        in_specs=[VMEM] * 5,
+        out_specs=VMEM,
+        scratch_shapes=[pltpu.VMEM((HEADS, tokens, LANES), LOW)] * 4,
+        compiler_params=pltpu.CompilerParams(vmem_limit_bytes=63 * 2**20),
+        name="attend_back",
+    )(qkv, segments.reshape(tokens, 1), mixed, lse, upstream)
 
 
 def swap(values, axis):
@@ -147,41 +415,6 @@
 
 def shifted(values, distance, count):
     return lax.ppermute(values, "far", [(i, (i + distance) % count) for i in range(count)])
-
-
-def collect_far(shard):
-    count = lax.axis_size("far")
-    if count > 4:
-        return lax.all_gather(shard, "far", axis=0)
-    here = lax.axis_index("far")
-    held = jnp.zeros((count,) + shard.shape, shard.dtype)
-    held = lax.dynamic_update_index_in_dim(held, shard, here, 0)
-    for distance in range(1, count):
-        came = shifted(shard, distance, count)
-        held = lax.dynamic_update_index_in_dim(held, came, (here - distance) % count, 0)
-    return held
-
-
-def gather_weight(shard, first):
-    near, core, half = lax.axis_index("near"), lax.axis_index("core"), lax.axis_index("mod")
-    own = collect_far(shard)
-    if first == "near":
-        by_near = swap(own, "near")
-        by_mod = swap(own, "mod")
-        by_both = swap(by_near, "mod")
-    else:
-        by_mod = swap(own, "mod")
-        by_near = swap(own, "near")
-        by_both = swap(by_mod, "near")
-    count, rows, columns = own.shape
-    whole = jnp.zeros((2, count, 2, 2, rows, columns), shard.dtype)
-    for piece, n, m in ((own, 0, 0), (by_near, 1, 0), (by_mod, 0, 1), (by_both, 1, 1)):
-        other = swap(piece, "core")
-        for part, k in ((piece, 0), (other, 1)):
-            whole = lax.dynamic_update_slice(
-                whole, part[None, :, None, None], (half ^ m, 0, near ^ n, core ^ k, 0, 0)
-            )
-    return whole.reshape(2, count * 4 * rows, columns)
 
 
 def scatter_gradient(left, right, first):
@@ -268,8 +501,6 @@
     devices = lax.axis_size(ALL)
     row_index = lax.axis_index(ROWS)
     images = cond.shape[0] // 2
-    head_width = width // HEADS
-    block_rows = min(512, tokens)
 
     cond_silu, silu_back = jax.vjp(jax.nn.silu, cond.astype(WIDE))
     silu_all = lax.all_gather(cond_silu.astype(LOW), ROWS, axis=0, tiled=True)
@@ -283,11 +514,14 @@
     ).reshape(images, -1)
 
     bias_full = lax.all_gather(bias_weight.astype(LOW), ALL, axis=0, tiled=True).astype(WIDE)
-    qkv_low = gather_weight(qkv_weight.astype(LOW), "near")
-    proj_low = gather_weight(proj_weight.astype(LOW), "mod")
-    fc1_low = gather_weight(fc1_weight.astype(LOW), "near")
-    fc2_low = gather_weight(fc2_weight.astype(LOW), "mod")
-    hidden_width = fc2_low.shape[1]
+    qkv_w, proj_w, fc1_w = first_gather(
+        qkv_weight.astype(LOW), proj_weight.astype(LOW), fc1_weight.astype(LOW)
+    )
+
+    def joined(whole):
+        return whole.reshape(2, -1, whole.shape[-1])
+
+    qkv_low = joined(qkv_w)
 
     chooser = segments[:, None] == jnp.arange(images, dtype=jnp.int32)[None, :]
     per_token = times(chooser.astype(LOW), modulation)
@@ -298,14 +532,15 @@
     first_norm, first_inverse = normalize(residual)
     attn_input = (first_norm * (1.0 + scale_attn) + shift_attn).astype(LOW)
     joint_proj = jnp.concatenate([times(attn_input, qkv_low[0]), times(attn_input, qkv_low[1])], 1)
-    query_rows = (joint_proj[:, 0:width] + bias_full[0:width]).astype(LOW)
-    key_rows = joint_proj[:, width : 2 * width].astype(LOW)
-    value_rows = (joint_proj[:, 2 * width :] + bias_full[width : 2 * width]).astype(LOW)
-    head_shape = (tokens, HEADS, head_width)
-    query_heads = query_rows.reshape(head_shape)
-    key_heads = key_rows.reshape(head_shape)
-    value_heads = value_rows.reshape(head_shape)
-    mixture, log_totals = attend_forward(query_heads, key_heads, value_heads, segments, block_rows)
+    joint_bias = jnp.concatenate(
+        [bias_full[0:width], jnp.zeros((width,), WIDE), bias_full[width : 2 * width]]
+    )
+    joint_rows = (joint_proj + joint_bias).astype(LOW)
+    mixture, log_totals, proj_w, fc1_w, fc2_w = attend(
+        joint_rows, segments, fc2_weight.astype(LOW), proj_w, fc1_w
+    )
+    proj_low, fc1_low, fc2_low = joined(proj_w), joined(fc1_w), joined(fc2_w)
+    hidden_width = fc2_low.shape[1]
     attn_out = (
         jnp.concatenate([times(mixture, proj_low[0]), times(mixture, proj_low[1])], 1)
         + bias_full[2 * width : 3 * width]
@@ -350,16 +585,9 @@
     mixture_grad = (
         times_back(attn_halves[0], proj_low[0]) + times_back(attn_halves[1], proj_low[1])
     ).astype(LOW)
-    query_grad, key_grad, value_grad = attend_backward(
-        query_heads,
-        key_heads,
-        value_heads,
-        segments,
-        log_totals,
-        mixture_grad.reshape(head_shape),
-        block_rows,
-    )
-    joint_grad = jnp.concatenate([query_grad, key_grad, value_grad], axis=1)
+    joint_grad = attend_back(joint_rows, segments, mixture, log_totals, mixture_grad)
+    query_grad = joint_grad[:, 0:width]
+    value_grad = joint_grad[:, 2 * width :]
     joint_halves = halves(joint_grad)
     qkv_shard = scatter_gradient(attn_input, joint_halves, "near")
     input_grad = times_back(joint_halves[0], qkv_low[0]) + times_back(joint_halves[1], qkv_low[1])

time: 1390 us -> 1080 us (0.78)
  Pallas kernels: 0 us -> 291 us
  matrix products: 479 us -> 250 us
  waiting for transfers between devices: 315 us -> 165 us
  local copies, waits for them, and re-layouts: 195 us -> 85.7 us
  other arithmetic: 203 us -> 125 us
  starting transfers between devices: 98.6 us -> 45.6 us
  blocking collectives: 88.5 us -> 105 us
    pallas_call x0 -> x3, Pallas kernels: none -> 291 us  [the longest x1 143 us: attend(): pl.pallas_call(attend_kernel, out_shape=(jax.ShapeDtypeStruct((tokens, HE...]
    dot_general x14 -> x0, matrix products: 223 us -> none  [the longest x4 67.4 us: masked_scores(): jnp.einsum('qhd,khd->hqk', query_part, key_rows, preferred_element_type=j...]
    ppermute x57 -> x29, waiting for transfers between devices: 225 us -> 107 us  [swap(): return lax.ppermute(values, axis, [(0, 1), (1, 0)])]
    dynamic_update_slice x44 -> x0, local copies, waits for them, and re-layouts: 56.5 us -> none  [the longest x32 47.6 us: gather_weight(): lax.dynamic_update_slice(whole, part[None, :, None, None], (half ^ m, 0,...]
    convert_element_type x4 -> x5, other arithmetic: 58.4 us -> 8.26 us  [the longest x1 4.77 us: body(): joint_rows = (joint_proj + joint_bias).astype(LOW)]
    reduce_sum x2 -> x0, other arithmetic: 30 us -> none  [one_block(): totals = jnp.sum(weights, axis=-1, keepdims=True)]
    ppermute x24 -> x12, starting transfers between devices: 36.4 us -> 11.1 us  [shifted(): lax.ppermute(values, 'far', [(i, (i + distance) % count) for i in range(c...]
    ppermute x24 -> x12, waiting for transfers between devices: 67.4 us -> 42.6 us  [shifted(): lax.ppermute(values, 'far', [(i, (i + distance) % count) for i in range(c...]
  transfers between devices with their start and end apart: 86 -> 46, of which waited for: 29 -> 19; matrix products, arithmetic and copies ran while one was open for 32% -> 5% of each run, Pallas kernels for 0% -> 7%
where the time goes in v2:
time: 1080 us; the launch traced here: 1070 us
  Pallas kernels  291 us (27%)
  matrix products  250 us (23%)
  waiting for transfers between devices  165 us (15%)
  other arithmetic  125 us (12%)
  blocking collectives  105 us (10%)
  local copies, waits for them, and re-layouts  85.7 us (8%)
  starting transfers between devices  45.6 us (4%)
    pallas_call x1, Pallas kernels, attend(): pl.pallas_call(attend_kernel, out_shape=(jax.ShapeDtypeStruct((tokens, HE...  143 us
    ppermute x29, waiting for transfers between devices, swap(): return lax.ppermute(values, axis, [(0, 1), (1, 0)])  107 us
    dot_general x9, matrix products, times_back(): lax.dot_general(left, right, (((1,), (1,)), ((), ())), preferred_element_...  92 us
    pallas_call x1, Pallas kernels, first_gather(): pl.pallas_call(first_kernel, out_shape=tuple((whole_shape(shard) for shar...  74.2 us
    pallas_call x1, Pallas kernels, attend_back(): pl.pallas_call(attend_back_kernel, out_shape=jax.ShapeDtypeStruct((tokens...  73.8 us
    dot_general x32, matrix products, piece(): jnp.dot(rows.reshape(tokens, -1).T, columns, preferred_element_type=WIDE)  73.5 us
    dot_general x10, matrix products, times(): return jnp.dot(left, right, preferred_element_type=WIDE)  65.9 us
    ppermute x12, waiting for transfers between devices, shifted(): lax.ppermute(values, 'far', [(i, (i + distance) % count) for i in range(c...  42.6 us
  transfers between devices with their start and end apart: 46, of which 19 were waited for; matrix products, arithmetic and copies ran while one was open for 5% of the time, Pallas kernels for 7%

profile of v2, /device:TPU:0, one launch (start us, length us, event | category | flops | bytes accessed | tf_op | source)
XLA Modules:
  0.0 1069.1 jit_solution(11776687105345448011)
XLA Ops:
  6.8 7.4 all-to-all-start
  16.3 41.2 %all-reduce = bf16[9216]{0:T(1024)(128)(2,1)S(1)} all-reduce(bf16[9216]{0:T(1024)(128)(2,1)} %dynamic-update-slice), channel_id=1, replica_groups=mesh['far'=4,'near'=2,'core'=2,'mod'=2] {'far','near','core','mod'}, use_global_device_ids=true, to_apply=%add | all-reduce | flops 9216 | bytes 36864
  67.0 74.2 %first_gather.1 = (bf16[2,4,2,2,72,1728]{5,4,3,2,1,0:T(8,128)(2,1)}, bf16[2,4,2,2,72,576]{5,4,3,2,1,0:T(8,128)(2,1)}, bf16[2,4,2,2,72,2304]{5,4,3,2,1,0:T(8,128)(2,1)}) custom-call(bf16[72,1728]{1,0:T(8,128)(2,1)} %convert_element_type.412.refs_0_, bf16[72,576]{1,0:T(8,128)(2,1)} %convert_element_type.413.refs_1_, bf16[72,2304]{1,0:T(8,128)(2,1)} %convert_element_type.414.refs_2_), custom_call_target="tpu_custom_call" | custom-call | tf_op jit(solution)/shard_map/first_gather/pallas_call | solution.py:225
  141.2 39.7 %all_gather.9 = bf16[128,1152]{1,0:T(8,128)(2,1)S(1)} all-gather(bf16[8,1152]{1,0:T(8,128)(2,1)} %fusion.198), channel_id=1, replica_groups=mesh['far'=4,'near'=2,'core'=2,'mod'=2] {'far','near','core'}, dimensions={0}, use_global_device_ids=true | all-gather | bytes 313344 | tf_op jit(solution)/shard_map/all_gather | solution.py:506
  180.8 5.7 fusion.242
  193.7 6.9 all-to-all-done.1
  200.8 11.5 %fusion.164 = f32[1024,6912]{1,0:T(8,128)} fusion(bf16[4,6912]{1,0:T(4,128)(2,1)S(1)} %reshape.348, s32[1024]{0:T(1024)S(1)} %copy-done.77), kind=kOutput, calls=%fused_computation.244 | convolution fusion | flops 56627200 | bytes 28370944 | tf_op jit(solution)/shard_map/dot_general | solution.py:465
  231.8 142.6 %attend.1 = (bf16[1024,1152]{1,0:T(8,128)(2,1)S(1)}, f32[1024,128]{1,0:T(8,128)S(1)}, bf16[2,4,2,2,72,576]{5,4,3,2,1,0:T(8,128)(2,1)}, bf16[2,4,2,2,72,2304]{5,4...) custom-call(bf16[1024,3456]{1,0:T(8,128)(2,1)} %fusion.15.refs_0_.qkv_ref, ...), custom_call_target="tpu_custom_call", output_to_operand_aliasing={{2}: (3, {}), {3}: (4, {})} | custom-call | tf_op jit(solution)/shard_map/attend/pallas_call | solution.py:322
  389.1 8.9 fusion.241
  398.0 9.5 convert_reduce_fusion.2
  407.5 9.0 fusion.249
  416.5 8.6 fusion.250
  425.1 9.6 copy.153
  434.7 14.3 %multiply_convert_fusion = bf16[1024,4608]{1,0:T(8,128)(2,1)} fusion(f32[1024,2304]{1,0:T(8,128)} %fusion.250, f32[1024,2304]{1,0:T(8,128)} %fusion.249, f32[4608]{0:T(1024)S(1)} %copy-done.74), kind=kLoop, calls=%fused_computation.21 | loop fusion | flops 51904512 | bytes 28329984 | tf_op jit(solution)/shard_map/convert_element_type | solution.py:556
  449.0 9.9 copy.154
  459.6 10.8 %fusion.14 = bf16[1024,4,2,2,288]{0,4,3,2,1:T(8,128)(2,1)S(1)} fusion(f32[1024,2,2,2,288]{0,4,3,2,1:T(8,128)} %bitcast.406, f32[1024,2,2,2,288]{0,4,3,2,1:T(8,128)} %bitcast.405, f32[4,2,2,288]{3,2,1,0:T(2,128)S(1)} %copy-done.83), kind=kLoop, calls=%fused_computation.17 | loop fusion | flops 51904512 | bytes 28329984 | tf_op jit(solution)/shard_map/convert_element_type | solution.py:556
  484.6 6.2 fusion.240
  490.8 13.8 %fusion.105 = f32[1024,4608]{1,0:T(8,128)} fusion(bf16[4608,576]{1,0:T(8,128)(2,1)} %bitcast.415, bf16[1024,1152]{1,0:T(8,128)(2,1)S(1)} %copy-done.17), kind=kOutput, calls=%fused_computation.180 | convolution fusion | flops 5435817984 | bytes 25493504 | tf_op jit(solution)/shard_map/dot_general | solution.py:469
  504.7 11.8 %fusion.251 = f32[1024,576]{1,0:T(8,128)} fusion(bf16[1024,4608]{1,0:T(8,128)(2,1)S(1)} %bitcast.412, bf16[4608,576]{1,0:T(8,128)(2,1)} %bitcast.416), kind=kOutput, calls=%fused_computation.379 | convolution fusion | flops 5435817984 | bytes 17104896 | tf_op jit(solution)/shard_map/dot_general | solution.py:465
  516.5 9.0 fusion.252
  525.5 25.6 %convert_reduce_fusion = (f32[4608]{0:T(1024)}, bf16[1024,4608]{1,0:T(8,128)(2,1)}) fusion(f32[4608]{0:T(1024)S(1)} %copy-done.74, f32[1024,2304]{1,0:T(8,128)} %fusion.250, f32[1024,2304]{1,0:T(8,128)} %fusion.249, f32[1024,4608]{1,0:T(8,128)} %fusion.105, bf16[4608,576]{1,0:T(8,128)(2,1)} %bitcast.413, bf16[1024,1152]{1,0:T(8,128)(2,1)S(1)} %copy-done.17), kind=kOutput, calls=%fused_computation.20 | convolution fusion | flops 5553778176 | bytes 53843968 | tf_op jit(solution)/shard_map/dot_general | solution.py:469
  551.0 11.3 %fusion.40 = f32[1024,1152]{1,0:T(8,128)} fusion(bf16[1152,2304]{1,0:T(8,128)(2,1)} %bitcast.429, bf16[1024,4608]{1,0:T(8,128)(2,1)} %get-tuple-element.122), kind=kOutput, calls=%fused_computation.84 | convolution fusion | flops 5435817984 | bytes 14745600 | tf_op jit(solution)/shard_map/dot_general | solution.py:469
  569.4 7.1 fusion.35
  593.9 12.4 %fusion.236 = (f32[1024]{0:T(1024)S(1)}, f32[1024]{0:T(1024)S(1)}, f32[1024,1152]{1,0:T(8,128)S(1)}) fusion(f32[1024,6912]{1,0:T(8,128)} %fusion.164, f32[1024]{0:T(1024)S(1)} %copy-done.91, f32[1024,1152]{1,0:T(8,128)S(1)} %bitcast.396, f32[1024]{0:T(1024)S(1)} %copy-done.82, f32[1024,1152]{1,0:T(8,128)} %fusion.40, bf16[1152,2304]{1,0:T(8,128)(2,1)} %bitcast.425, ...), kind=kOutput, calls=%fused_computation.365 | convolution fusion | flops 5445253120 | bytes 28917760 | tf_op jit(solution)/shard_map/dot_general | solution.py:469
  606.4 13.6 %convert_reduce_fusion.3 = (f32[1152]{0:T(1024)S(1)}, bf16[1024,1152]{1,0:T(8,128)(2,1)S(1)}, f32[1024,1152]{1,0:T(8,128)}, bf16[1024,1152]{1,0:T(8,128)(2,1)}) fusion(f32[1024,6912]{1,0:T(8,128)} %fusion.164, f32[1024]{0:T(1024)S(1)} %get-tuple-element.123, f32[1024,1152]{1,0:T(8,128)S(1)} %bitcast.396, f32[1024]{0:T(1024)S(1)} %copy-done.82, ...), kind=kLoop, calls=%fused_computation.66 | loop fusion | flops 22412160 | bytes 40133632 | tf_op jit(solution)/shard_map/reduce_sum | solution.py:622
  637.6 6.0 add_convert_fusion.up_ref
  643.6 73.8 %attend_back.1 = bf16[1024,3456]{1,0:T(8,128)(2,1)} custom-call(bf16[1024,3456]{1,0:T(8,128)(2,1)} %fusion.15.refs_0_.qkv_ref, s32[1024,1]{1,0:T(8,128)} %copy-done.2, bf16[1024,1152]{1,0:T(8,128)(2,1)} %copy-done, f32[1024,128]{1,0:T(8,128)} %copy-done.3, bf16[1024,1152]{1,0:T(8,128)(2,1)} %add_convert_fusion.up_ref), custom_call_target="tpu_custom_call" | custom-call | tf_op jit(solution)/shard_map/attend_back/pallas_call | solution.py:401
  720.5 8.0 slice_bitcast_fusion.2
  731.0 5.1 fusion.45
  751.0 6.7 fusion.47
  757.7 10.9 %constant_dynamic-update-slice_fusion.1 = (f32[1024,6912]{1,0:T(8,128)}, f32[1024,1152]{1,0:T(8,128)}) fusion(f32[1024,1152]{1,0:T(8,128)} %fusion.47, bf16[1152,1728]{1,0:T(8,128)(2,1)} %bitcast.435, bf16[1024,3456]{1,0:T(8,128)(2,1)S(1)} %bitcast.400), kind=kOutput, calls=%fused_computation.311 | convolution fusion | flops 4078043136 | bytes 21807104 | tf_op jit(solution)/shard_map/dot_general | solution.py:469
  773.6 7.4 fusion.28
  796.5 14.3 %convolution_convert_fusion = bf16[4,6912]{1,0:T(4,128)(2,1)} fusion(f32[1024,6912]{1,0:T(8,128)} %fusion.31, s32[1024]{0:T(1024)S(1)} %copy-done.78), kind=kOutput, calls=%fused_computation.32 | convolution fusion | flops 339770368 | bytes 28370944 | tf_op jit(solution)/shard_map/ts,tc->sc/dot_general | solution.py:603
  821.3 24.1 %all_gather.11 = bf16[128,3456]{1,0:T(8,128)(2,1)S(1)} all-gather(bf16[8,3456]{1,0:T(8,128)(2,1)S(1)} %all_to_all.70), channel_id=1, replica_groups=mesh['far'=4,'near'=2,'core'=2,'mod'=2] {'far','near','core'}, dimensions={0}, use_global_device_ids=true | all-gather | bytes 940032 | tf_op jit(solution)/shard_map/all_gather | solution.py:607
  855.5 6.2 all-to-all-done.3
  870.0 5.3 collective-permute-done.16
  879.4 5.7 collective-permute-done.13
  889.1 5.0 collective-permute-done.18
  908.8 16.9 %collective-permute-done.6 = bf16[4,72,1728]{2,1,0:T(8,128)(2,1)S(1)} collective-permute-done((bf16[4,72,1728]{2,1,0:T(8,128)(2,1)S(1)}, bf16[4,72,1728]{2,1,0:T(8,128)(2,1)S(1)}, u32[]{:S(2)}, u32[]{:S(2)}) %collective-permute-start.6) | collective-permute-done | bytes 995360 | tf_op jit(solution)/shard_map/ppermute | solution.py:413
  930.0 11.3 %collective-permute-done.36 = bf16[4,288,576]{2,1,0:T(8,128)(2,1)S(1)} collective-permute-done((bf16[4,288,576]{2,1,0:T(8,128)(2,1)S(1)}, bf16[4,288,576]{2,1,0:T(8,128)(2,1)S(1)}, u32[]{:S(2)}, u32[]{:S(2)}) %collective-permute-start.36) | collective-permute-done | bytes 1327136 | tf_op jit(solution)/shard_map/ppermute | solution.py:413
  945.5 6.0 collective-permute-done.3
  952.3 11.1 %collective-permute-done.7 = bf16[4,72,1728]{2,1,0:T(8,128)(2,1)S(1)} collective-permute-done((bf16[4,72,1728]{2,1,0:T(8,128)(2,1)S(1)}, bf16[4,72,1728]{2,1,0:T(8,128)(2,1)S(1)}, u32[]{:S(2)}, u32[]{:S(2)}) %collective-permute-start.7) | collective-permute-done | bytes 995360 | tf_op jit(solution)/shard_map/ppermute | solution.py:413
  968.1 11.8 %collective-permute-done.26 = bf16[4,72,2304]{2,1,0:T(8,128)(2,1)S(1)} collective-permute-done((bf16[4,72,2304]{2,1,0:T(8,128)(2,1)S(1)}, bf16[4,72,2304]{2,1,0:T(8,128)(2,1)S(1)}, u32[]{:S(2)}, u32[]{:S(2)}) %collective-permute-start.26) | collective-permute-done | bytes 1327136 | tf_op jit(solution)/shard_map/ppermute | solution.py:413
  980.8 11.1 %collective-permute-done.9 = bf16[72,1728]{1,0:T(8,128)(2,1)S(1)} collective-permute-done((bf16[72,1728]{1,0:T(8,128)(2,1)S(1)}, bf16[72,1728]{1,0:T(8,128)(2,1)S(1)}, u32[]{:S(2)}, u32[]{:S(2)}) %collective-permute-start.9) | collective-permute-done | bytes 248864 | tf_op jit(solution)/shard_map/ppermute | solution.py:417
  996.2 15.2 %collective-permute-done.37 = bf16[4,288,576]{2,1,0:T(8,128)(2,1)S(1)} collective-permute-done((bf16[4,288,576]{2,1,0:T(8,128)(2,1)S(1)}, bf16[4,288,576]{2,1,0:T(8,128)(2,1)S(1)}, u32[]{:S(2)}, u32[]{:S(2)}) %collective-permute-start.37) | collective-permute-done | bytes 1327136 | tf_op jit(solution)/shard_map/ppermute | solution.py:413
  1016.1 22.5 %collective-permute-done.23 = bf16[4,72,2304]{2,1,0:T(8,128)(2,1)S(1)} collective-permute-done((bf16[4,72,2304]{2,1,0:T(8,128)(2,1)S(1)}, bf16[4,72,2304]{2,1,0:T(8,128)(2,1)S(1)}, u32[]{:S(2)}, u32[]{:S(2)}) %collective-permute-start.23) | collective-permute-done | bytes 1327136 | tf_op jit(solution)/shard_map/ppermute | solution.py:413
  1044.9 7.1 collective-permute-done.28
  1052.0 15.3 %collective-permute-done.29 = bf16[72,2304]{1,0:T(8,128)(2,1)S(1)} collective-permute-done((bf16[72,2304]{1,0:T(8,128)(2,1)S(1)}, bf16[72,2304]{1,0:T(8,128)(2,1)S(1)}, u32[]{:S(2)}, u32[]{:S(2)}) %collective-permute-start.29) | collective-permute-done | bytes 331808 | tf_op jit(solution)/shard_map/ppermute | solution.py:417
  (484 shorter events, 239.3 us)
Async XLA Ops:
  6.8 179.8 %all-to-all-start = ((bf16[72,16,216]{2,0,1:T(8,128)(2,1)}), bf16[72,16,216]{2,0,1:T(8,128)(2,1)}, u32[]{:S(2)}, u32[]{:S(2)}) async-start(bf16[72,16,216]{2,0,1:T(8,128)(2,1)} %copy.132), calls=%async_computation | async-start | bytes 1179648 | tf_op jit(solution)/shard_map/all_to_all | solution.py:508
  61.1 151.1 %copy-start.79 = (f32[1024]{0:T(1024)}, f32[1024]{0:T(1024)S(1)}, u32[]{:S(2)}) copy-start(f32[1024]{0:T(1024)S(1)} %broadcast_multiply_fusion.5) | copy-start | bytes 12292
  64.9 166.9 %copy-start.2 = (s32[1024,1]{1,0:T(8,128)}, s32[1024,1]{1,0:T(8,128)S(1)}, u32[]{:S(2)}) copy-start(s32[1024,1]{1,0:T(8,128)S(1)} %copy.137.refs_1_.seg_ref) | copy-start | bytes 12292
  190.2 10.3 all-to-all-start.1
  810.8 7.5 all-to-all-start.2
  815.1 87.3 %collective-permute-start.35 = (bf16[4,288,576]{2,1,0:T(8,128)(2,1)}, bf16[4,288,576]{2,1,0:T(8,128)(2,1)}, u32[]{:S(2)}, u32[]{:S(2)}) collective-permute-start(bf16[4,288,576]{2,1,0:T(8,128)(2,1)} %fusion.82), channel_id=1, source_target_pairs={{0,2},{2,0},{1,3},{3,1},{4,6},{6,4},{5,7},{7,5},{8,10},{10,8},{9,1... | collective-permute-start | bytes 3981320 | tf_op jit(solution)/shard_map/ppermute | solution.py:413
  815.4 62.4 %collective-permute-start.11 = (bf16[4,72,576]{2,1,0:T(8,128)(2,1)}, bf16[4,72,576]{2,1,0:T(8,128)(2,1)}, u32[]{:S(2)}, u32[]{:S(2)}) collective-permute-start(bf16[4,72,576]{2,1,0:T(8,128)(2,1)} %convolution_convert_fusion.12), channel_id=1, source_target_pairs={{0,2},{2,0},{1,3},{3,1},{4,6},{6,4},{5,7},{7,5},{8,10},{10,8},{9,1... | collective-permute-start | bytes 995336 | tf_op jit(solution)/shard_map/ppermute | solution.py:413
  815.6 48.4 %collective-permute-start.12 = (bf16[4,72,576]{2,1,0:T(8,128)(2,1)}, bf16[4,72,576]{2,1,0:T(8,128)(2,1)}, u32[]{:S(2)}, u32[]{:S(2)}) collective-permute-start(bf16[4,72,576]{2,1,0:T(8,128)(2,1)} %convolution_convert_fusion.11), channel_id=1, source_target_pairs={{0,2},{2,0},{1,3},{3,1},{4,6},{6,4},{5,7},{7,5},{8,10},{10,8},{9,1... | collective-permute-start | bytes 995336 | tf_op jit(solution)/shard_map/ppermute | solution.py:413
  815.9 51.8 %collective-permute-start.14 = (bf16[4,72,576]{2,1,0:T(8,128)(2,1)}, bf16[4,72,576]{2,1,0:T(8,128)(2,1)}, u32[]{:S(2)}, u32[]{:S(2)}) collective-permute-start(bf16[4,72,576]{2,1,0:T(8,128)(2,1)} %convolution_convert_fusion.10), channel_id=1, source_target_pairs={{0,2},{2,0},{1,3},{3,1},{4,6},{6,4},{5,7},{7,5},{8,10},{10,8},{9,1... | collective-permute-start | bytes 995336 | tf_op jit(solution)/shard_map/ppermute | solution.py:413
  816.1 45.6 %collective-permute-start.15 = (bf16[4,72,576]{2,1,0:T(8,128)(2,1)}, bf16[4,72,576]{2,1,0:T(8,128)(2,1)}, u32[]{:S(2)}, u32[]{:S(2)}) collective-permute-start(bf16[4,72,576]{2,1,0:T(8,128)(2,1)} %convolution_convert_fusion.9), channel_id=1, source_target_pairs={{0,2},{2,0},{1,3},{3,1},{4,6},{6,4},{5,7},{7,5},{8,10},{10,8},{9,1... | collective-permute-start | bytes 995336 | tf_op jit(solution)/shard_map/ppermute | solution.py:413
  818.3 32.8 %all-to-all-start.4 = ((f32[32,1,288]{2,1,0:T(1,128)}), f32[32,1,288]{2,1,0:T(1,128)S(1)}, u32[]{:S(2)}, u32[]{:S(2)}) async-start(f32[32,1,288]{2,1,0:T(1,128)} %all_to_all.75), calls=%async_computation.4 | async-start | bytes 98304 | tf_op jit(solution)/shard_map/all_to_all | solution.py:627
  851.1 10.5 all-to-all-start.3
  861.8 25.0 %collective-permute-start.2 = (bf16[4,72,1728]{2,1,0:T(8,128)(2,1)}, bf16[4,72,1728]{2,1,0:T(8,128)(2,1)S(1)}, u32[]{:S(2)}, u32[]{:S(2)}) collective-permute-start(bf16[4,72,1728]{2,1,0:T(8,128)(2,1)} %convolution_convert_fusion.7), channel_id=1, source_target_pairs={{0,2},{2,0},{1,3},{3,1},{4,6},{6,4},{5,7},{7,5},{8,10},{10,8},{9,1... | collective-permute-start | bytes 2985992 | tf_op jit(solution)/shard_map/ppermute | solution.py:413
  864.0 11.4 %collective-permute-start.16 = (bf16[4,72,576]{2,1,0:T(8,128)(2,1)S(1)}, bf16[4,72,576]{2,1,0:T(8,128)(2,1)S(1)}, u32[]{:S(2)}, u32[]{:S(2)}) collective-permute-start(bf16[4,72,576]{2,1,0:T(8,128)(2,1)S(1)} %add_convert_fusion.25), channel_id=1, source_target_pairs={{0,1},{1,0},{2,3},{3,2},{4,5},{5,4},{6,7},{7,6},{8,9},{9,8},{10,11... | collective-permute-start | bytes 995336 | tf_op jit(solution)/shard_map/ppermute | solution.py:413
  867.6 9.4 collective-permute-start
  875.4 9.7 collective-permute-start.13
  877.0 9.5 collective-permute-start.17
  877.8 10.4 collective-permute-start.5
  885.1 15.4 %collective-permute-start.22 = (bf16[4,72,2304]{2,1,0:T(8,128)(2,1)S(1)}, bf16[4,72,2304]{2,1,0:T(8,128)(2,1)S(1)}, u32[]{:S(2)}, u32[]{:S(2)}) collective-permute-start(bf16[4,72,2304]{2,1,0:T(8,128)(2,1)S(1)} %copy-done.109), channel_id=1, source_target_pairs={{0,2},{2,0},{1,3},{3,1},{4,6},{6,4},{5,7},{7,5},{8,10},{10,8},{9,1... | collective-permute-start | bytes 3981320 | tf_op jit(solution)/shard_map/ppermute | solution.py:413
  886.5 19.7 %collective-permute-start.25 = (bf16[4,72,2304]{2,1,0:T(8,128)(2,1)S(1)}, bf16[4,72,2304]{2,1,0:T(8,128)(2,1)S(1)}, u32[]{:S(2)}, u32[]{:S(2)}) collective-permute-start(bf16[4,72,2304]{2,1,0:T(8,128)(2,1)S(1)} %copy-done.108), channel_id=1, source_target_pairs={{0,2},{2,0},{1,3},{3,1},{4,6},{6,4},{5,7},{7,5},{8,10},{10,8},{9,1... | collective-permute-start | bytes 3981320 | tf_op jit(solution)/shard_map/ppermute | solution.py:413
  886.7 7.4 collective-permute-start.18
  888.2 9.5 collective-permute-start.19
  894.1 5.4 collective-permute-start.20
  897.7 28.8 %collective-permute-start.32 = (bf16[4,288,576]{2,1,0:T(8,128)(2,1)S(1)}, bf16[4,288,576]{2,1,0:T(8,128)(2,1)S(1)}, u32[]{:S(2)}, u32[]{:S(2)}) collective-permute-start(bf16[4,288,576]{2,1,0:T(8,128)(2,1)S(1)} %copy-done.105), channel_id=1, source_target_pairs={{0,2},{2,0},{1,3},{3,1},{4,6},{6,4},{5,7},{7,5},{8,10},{10,8},{9,1... | collective-permute-start | bytes 3981320 | tf_op jit(solution)/shard_map/ppermute | solution.py:413
  899.5 9.2 collective-permute-start.4
  900.5 25.3 %collective-permute-start.6 = (bf16[4,72,1728]{2,1,0:T(8,128)(2,1)S(1)}, bf16[4,72,1728]{2,1,0:T(8,128)(2,1)S(1)}, u32[]{:S(2)}, u32[]{:S(2)}) collective-permute-start(bf16[4,72,1728]{2,1,0:T(8,128)(2,1)S(1)} %add_convert_fusion.18), channel_id=1, source_target_pairs={{0,4},{4,0},{1,5},{5,1},{2,6},{6,2},{3,7},{7,3},{8,12},{12,8},{9,1... | collective-permute-start | bytes 2985992 | tf_op jit(solution)/shard_map/ppermute | solution.py:413
  902.4 27.1 %collective-permute-start.34 = (bf16[4,288,576]{2,1,0:T(8,128)(2,1)S(1)}, bf16[4,288,576]{2,1,0:T(8,128)(2,1)S(1)}, u32[]{:S(2)}, u32[]{:S(2)}) collective-permute-start(bf16[4,288,576]{2,1,0:T(8,128)(2,1)S(1)} %copy-done.104), channel_id=1, source_target_pairs={{0,2},{2,0},{1,3},{3,1},{4,6},{6,4},{5,7},{7,5},{8,10},{10,8},{9,1... | collective-permute-start | bytes 3981320 | tf_op jit(solution)/shard_map/ppermute | solution.py:413
  906.2 35.2 %collective-permute-start.36 = (bf16[4,288,576]{2,1,0:T(8,128)(2,1)S(1)}, bf16[4,288,576]{2,1,0:T(8,128)(2,1)S(1)}, u32[]{:S(2)}, u32[]{:S(2)}) collective-permute-start(bf16[4,288,576]{2,1,0:T(8,128)(2,1)S(1)} %add_convert_fusion.4), channel_id=1, source_target_pairs={{0,1},{1,0},{2,3},{3,2},{4,5},{5,4},{6,7},{7,6},{8,9},{9,8},{10,11... | collective-permute-start | bytes 3981320 | tf_op jit(solution)/shard_map/ppermute | solution.py:413
  908.7 20.7 %collective-permute-start.1 = (bf16[4,72,1728]{2,1,0:T(8,128)(2,1)S(1)}, bf16[4,72,1728]{2,1,0:T(8,128)(2,1)S(1)}, u32[]{:S(2)}, u32[]{:S(2)}) collective-permute-start(bf16[4,72,1728]{2,1,0:T(8,128)(2,1)S(1)} %copy-done.110), channel_id=1, source_target_pairs={{0,2},{2,0},{1,3},{3,1},{4,6},{6,4},{5,7},{7,5},{8,10},{10,8},{9,1... | collective-permute-start | bytes 2985992 | tf_op jit(solution)/shard_map/ppermute | solution.py:413
  925.7 25.7 %collective-permute-start.3 = (bf16[4,72,1728]{2,1,0:T(8,128)(2,1)S(1)}, bf16[4,72,1728]{2,1,0:T(8,128)(2,1)S(1)}, u32[]{:S(2)}, u32[]{:S(2)}) collective-permute-start(bf16[4,72,1728]{2,1,0:T(8,128)(2,1)S(1)} %add_convert_fusion.21), channel_id=1, source_target_pairs={{0,4},{4,0},{1,5},{5,1},{2,6},{6,2},{3,7},{7,3},{8,12},{12,8},{9,1... | collective-permute-start | bytes 2985992 | tf_op jit(solution)/shard_map/ppermute | solution.py:413
  926.5 37.0 %collective-permute-start.7 = (bf16[4,72,1728]{2,1,0:T(8,128)(2,1)S(1)}, bf16[4,72,1728]{2,1,0:T(8,128)(2,1)S(1)}, u32[]{:S(2)}, u32[]{:S(2)}) collective-permute-start(bf16[4,72,1728]{2,1,0:T(8,128)(2,1)S(1)} %add_convert_fusion.17), channel_id=1, source_target_pairs={{0,1},{1,0},{2,3},{3,2},{4,5},{5,4},{6,7},{7,6},{8,9},{9,8},{10,11... | collective-permute-start | bytes 2985992 | tf_op jit(solution)/shard_map/ppermute | solution.py:413
  929.5 36.3 %collective-permute-start.31 = (bf16[4,288,576]{2,1,0:T(8,128)(2,1)S(1)}, bf16[4,288,576]{2,1,0:T(8,128)(2,1)S(1)}, u32[]{:S(2)}, u32[]{:S(2)}) collective-permute-start(bf16[4,288,576]{2,1,0:T(8,128)(2,1)S(1)} %copy-done.103), channel_id=1, source_target_pairs={{0,2},{2,0},{1,3},{3,1},{4,6},{6,4},{5,7},{7,5},{8,10},{10,8},{9,1... | collective-permute-start | bytes 3981320 | tf_op jit(solution)/shard_map/ppermute | solution.py:413
  929.6 37.2 %collective-permute-start.24 = (bf16[4,72,2304]{2,1,0:T(8,128)(2,1)S(1)}, bf16[4,72,2304]{2,1,0:T(8,128)(2,1)S(1)}, u32[]{:S(2)}, u32[]{:S(2)}) collective-permute-start(bf16[4,72,2304]{2,1,0:T(8,128)(2,1)S(1)} %copy-done.107), channel_id=1, source_target_pairs={{0,2},{2,0},{1,3},{3,1},{4,6},{6,4},{5,7},{7,5},{8,10},{10,8},{9,1... | collective-permute-start | bytes 3981320 | tf_op jit(solution)/shard_map/ppermute | solution.py:413
  941.4 38.5 %collective-permute-start.26 = (bf16[4,72,2304]{2,1,0:T(8,128)(2,1)S(1)}, bf16[4,72,2304]{2,1,0:T(8,128)(2,1)S(1)}, u32[]{:S(2)}, u32[]{:S(2)}) collective-permute-start(bf16[4,72,2304]{2,1,0:T(8,128)(2,1)S(1)} %add_convert_fusion.11), channel_id=1, source_target_pairs={{0,4},{4,0},{1,5},{5,1},{2,6},{6,2},{3,7},{7,3},{8,12},{12,8},{9,1... | collective-permute-start | bytes 3981320 | tf_op jit(solution)/shard_map/ppermute | solution.py:413
  951.4 44.8 %collective-permute-start.33 = (bf16[4,288,576]{2,1,0:T(8,128)(2,1)S(1)}, bf16[4,288,576]{2,1,0:T(8,128)(2,1)S(1)}, u32[]{:S(2)}, u32[]{:S(2)}) collective-permute-start(bf16[4,288,576]{2,1,0:T(8,128)(2,1)S(1)} %add_convert_fusion.7), channel_id=1, source_target_pairs={{0,1},{1,0},{2,3},{3,2},{4,5},{5,4},{6,7},{7,6},{8,9},{9,8},{10,11... | collective-permute-start | bytes 3981320 | tf_op jit(solution)/shard_map/ppermute | solution.py:413
  963.5 48.0 %collective-permute-start.37 = (bf16[4,288,576]{2,1,0:T(8,128)(2,1)S(1)}, bf16[4,288,576]{2,1,0:T(8,128)(2,1)S(1)}, u32[]{:S(2)}, u32[]{:S(2)}) collective-permute-start(bf16[4,288,576]{2,1,0:T(8,128)(2,1)S(1)} %add_convert_fusion.3), channel_id=1, source_target_pairs={{0,4},{4,0},{1,5},{5,1},{2,6},{6,2},{3,7},{7,3},{8,12},{12,8},{9,1... | collective-permute-start | bytes 3981320 | tf_op jit(solution)/shard_map/ppermute | solution.py:413
  965.8 14.5 %collective-permute-start.10 = (bf16[72,1728]{1,0:T(8,128)(2,1)S(1)}, bf16[72,1728]{1,0:T(8,128)(2,1)S(1)}, u32[]{:S(2)}, u32[]{:S(2)}) collective-permute-start(bf16[72,1728]{1,0:T(8,128)(2,1)S(1)} %get-tuple-element.109), channel_id=1, source_target_pairs={{0,24},{8,0},{16,8},{24,16},{1,25},{9,1},{17,9},{25,17},{2,26},{10... | collective-permute-start | bytes 746504 | tf_op jit(solution)/shard_map/ppermute | solution.py:417
  966.8 13.6 %collective-permute-start.8 = (bf16[72,1728]{1,0:T(8,128)(2,1)S(1)}, bf16[72,1728]{1,0:T(8,128)(2,1)S(1)}, u32[]{:S(2)}, u32[]{:S(2)}) collective-permute-start(bf16[72,1728]{1,0:T(8,128)(2,1)S(1)} %get-tuple-element.108), channel_id=1, source_target_pairs={{0,8},{8,16},{16,24},{24,0},{1,9},{9,17},{17,25},{25,1},{2,10},{10... | collective-permute-start | bytes 746504 | tf_op jit(solution)/shard_map/ppermute | solution.py:417
  979.9 12.0 %collective-permute-start.9 = (bf16[72,1728]{1,0:T(8,128)(2,1)S(1)}, bf16[72,1728]{1,0:T(8,128)(2,1)S(1)}, u32[]{:S(2)}, u32[]{:S(2)}) collective-permute-start(bf16[72,1728]{1,0:T(8,128)(2,1)S(1)} %get-tuple-element.110), channel_id=1, source_target_pairs={{0,16},{8,24},{16,0},{24,8},{1,17},{9,25},{17,1},{25,9},{2,18},{10... | collective-permute-start | bytes 746504 | tf_op jit(solution)/shard_map/ppermute | solution.py:417
  980.3 33.4 %collective-permute-start.21 = (bf16[4,72,2304]{2,1,0:T(8,128)(2,1)S(1)}, bf16[4,72,2304]{2,1,0:T(8,128)(2,1)S(1)}, u32[]{:S(2)}, u32[]{:S(2)}) collective-permute-start(bf16[4,72,2304]{2,1,0:T(8,128)(2,1)S(1)} %copy-done.106), channel_id=1, source_target_pairs={{0,2},{2,0},{1,3},{3,1},{4,6},{6,4},{5,7},{7,5},{8,10},{10,8},{9,1... | collective-permute-start | bytes 3981320 | tf_op jit(solution)/shard_map/ppermute | solution.py:413
  980.4 58.2 %collective-permute-start.23 = (bf16[4,72,2304]{2,1,0:T(8,128)(2,1)S(1)}, bf16[4,72,2304]{2,1,0:T(8,128)(2,1)S(1)}, u32[]{:S(2)}, u32[]{:S(2)}) collective-permute-start(bf16[4,72,2304]{2,1,0:T(8,128)(2,1)S(1)} %add_convert_fusion.14), channel_id=1, source_target_pairs={{0,4},{4,0},{1,5},{5,1},{2,6},{6,2},{3,7},{7,3},{8,12},{12,8},{9,1... | collective-permute-start | bytes 3981320 | tf_op jit(solution)/shard_map/ppermute | solution.py:413
  991.9 46.7 %collective-permute-start.27 = (bf16[4,72,2304]{2,1,0:T(8,128)(2,1)S(1)}, bf16[4,72,2304]{2,1,0:T(8,128)(2,1)S(1)}, u32[]{:S(2)}, u32[]{:S(2)}) collective-permute-start(bf16[4,72,2304]{2,1,0:T(8,128)(2,1)S(1)} %add_convert_fusion.10), channel_id=1, source_target_pairs={{0,1},{1,0},{2,3},{3,2},{4,5},{5,4},{6,7},{7,6},{8,9},{9,8},{10,11... | collective-permute-start | bytes 3981320 | tf_op jit(solution)/shard_map/ppermute | solution.py:413
  1012.2 28.7 %collective-permute-start.38 = (bf16[288,576]{1,0:T(8,128)(2,1)S(1)}, bf16[288,576]{1,0:T(8,128)(2,1)S(1)}, u32[]{:S(2)}, u32[]{:S(2)}) collective-permute-start(bf16[288,576]{1,0:T(8,128)(2,1)S(1)} %get-tuple-element.102), channel_id=1, source_target_pairs={{0,8},{8,16},{16,24},{24,0},{1,9},{9,17},{17,25},{25,1},{2,10},{10... | collective-permute-start | bytes 995336 | tf_op jit(solution)/shard_map/ppermute | solution.py:417
  1012.9 30.3 %collective-permute-start.39 = (bf16[288,576]{1,0:T(8,128)(2,1)S(1)}, bf16[288,576]{1,0:T(8,128)(2,1)S(1)}, u32[]{:S(2)}, u32[]{:S(2)}) collective-permute-start(bf16[288,576]{1,0:T(8,128)(2,1)S(1)} %get-tuple-element.104), channel_id=1, source_target_pairs={{0,16},{8,24},{16,0},{24,8},{1,17},{9,25},{17,1},{25,9},{2,18},{10... | collective-permute-start | bytes 995336 | tf_op jit(solution)/shard_map/ppermute | solution.py:417
  1013.8 29.5 %collective-permute-start.40 = (bf16[288,576]{1,0:T(8,128)(2,1)S(1)}, bf16[288,576]{1,0:T(8,128)(2,1)S(1)}, u32[]{:S(2)}, u32[]{:S(2)}) collective-permute-start(bf16[288,576]{1,0:T(8,128)(2,1)S(1)} %get-tuple-element.103), channel_id=1, source_target_pairs={{0,24},{8,0},{16,8},{24,16},{1,25},{9,1},{17,9},{25,17},{2,26},{10... | collective-permute-start | bytes 995336 | tf_op jit(solution)/shard_map/ppermute | solution.py:417
  1039.3 12.7 %collective-permute-start.28 = (bf16[72,2304]{1,0:T(8,128)(2,1)S(1)}, bf16[72,2304]{1,0:T(8,128)(2,1)S(1)}, u32[]{:S(2)}, u32[]{:S(2)}) collective-permute-start(bf16[72,2304]{1,0:T(8,128)(2,1)S(1)} %get-tuple-element.105), channel_id=1, source_target_pairs={{0,8},{8,16},{16,24},{24,0},{1,9},{9,17},{17,25},{25,1},{2,10},{10... | collective-permute-start | bytes 995336 | tf_op jit(solution)/shard_map/ppermute | solution.py:417
  1040.0 27.3 %collective-permute-start.29 = (bf16[72,2304]{1,0:T(8,128)(2,1)S(1)}, bf16[72,2304]{1,0:T(8,128)(2,1)S(1)}, u32[]{:S(2)}, u32[]{:S(2)}) collective-permute-start(bf16[72,2304]{1,0:T(8,128)(2,1)S(1)} %get-tuple-element.107), channel_id=1, source_target_pairs={{0,16},{8,24},{16,0},{24,8},{1,17},{9,25},{17,1},{25,9},{2,18},{10... | collective-permute-start | bytes 995336 | tf_op jit(solution)/shard_map/ppermute | solution.py:417
  1040.9 26.4 %collective-permute-start.30 = (bf16[72,2304]{1,0:T(8,128)(2,1)S(1)}, bf16[72,2304]{1,0:T(8,128)(2,1)S(1)}, u32[]{:S(2)}, u32[]{:S(2)}) collective-permute-start(bf16[72,2304]{1,0:T(8,128)(2,1)S(1)} %get-tuple-element.106), channel_id=1, source_target_pairs={{0,24},{8,0},{16,8},{24,16},{1,25},{9,1},{17,9},{25,17},{2,26},{10... | collective-permute-start | bytes 995336 | tf_op jit(solution)/shard_map/ppermute | solution.py:417
  (136 other events, 1717.7 us)

commit v3 on v2

--- a/solution.py
+++ b/solution.py
@@ -339,87 +339,358 @@
     )(qkv, segments.reshape(tokens, 1), fc2_s, proj_w, fc1_w)
 
 
+def row_spans(rows):
+    first = rows if rows % 16 else 8 * ((rows // 8 + 1) // 2)
+    return [(0, first)] + ([(first, rows - first)] if first < rows else [])
+
+
+class Reduce:
+    def __init__(self, quads, span, first, buffers, sems):
+        self.quads, self.span, self.first = quads, span, first
+        self.second = "near" if first == "mod" else "mod"
+        self.came_both, self.came_first, self.came_second, self.joint, self.total_, self.came_far = buffers
+        self.sends, self.receives, self.locals_ = sems
+        self.here = places()
+        self.count = lax.axis_size("far")
+
+    @staticmethod
+    def scratch(count, span, columns, own_total=True):
+        block = (count, span[1], columns)
+        buffers = [pltpu.VMEM(block, LOW)] * (5 if own_total else 4)
+        buffers += [pltpu.VMEM((count - 1,) + block[1:], LOW)]
+        return buffers + [pltpu.SemaphoreType.DMA((count + 2,))] * 2 + [pltpu.SemaphoreType.DMA((2,))]
+
+    def _part(self, *flips):
+        quad = self.quads["near" in flips, "mod" in flips]
+        return quad.at[:, pl.ds(*self.span)]
+
+    def _swap(self, source, target, slot, axis):
+        return remote(source, target, self.sends, self.receives, slot, {axis: 1 - self.here[axis]})
+
+    def _both(self):
+        return self._swap(self._part("near", "mod"), self.came_both, 0, self.first)
+
+    def _first(self):
+        return self._swap(self._part(self.first), self.came_first, 1, self.first)
+
+    def _second(self):
+        return self._swap(self.joint, self.came_second, 2, self.second)
+
+    def _local(self, source, target, slot):
+        return pltpu.make_async_copy(source, target, self.locals_.at[slot])
+
+    def _load(self, number):
+        if number == 0:
+            return self._local(self._part(self.second), self.joint, 0)
+        return self._local(self._part(), self.total_, 1)
+
+    def _far(self, distance):
+        target = lax.rem(self.here["far"] + distance, self.count)
+        return remote(
+            self.total_.at[target],
+            self.came_far.at[distance - 1],
+            self.sends,
+            self.receives,
+            2 + distance,
+            dict(far=target),
+        )
+
+    def start(self):
+        self._both().start()
+        self._first().start()
+        self._load(0).start()
+        self._load(1).start()
+
+    def merge(self):
+        self._load(0).wait()
+        self._both().wait_recv()
+
+        def add(at, carry):
+            self.joint[at] = (self.joint[at].astype(WIDE) + self.came_both[at].astype(WIDE)).astype(LOW)
+            return carry
+
+        lax.fori_loop(0, self.count, add, 0)
+        self._second().start()
+
+    def total(self):
+        self._load(1).wait()
+        self._first().wait_recv()
+        self._second().wait_recv()
+
+        def add(at, carry):
+            self.total_[at] = (
+                self.total_[at].astype(WIDE)
+                + self.came_first[at].astype(WIDE)
+                + self.came_second[at].astype(WIDE)
+            ).astype(LOW)
+            return carry
+
+        lax.fori_loop(0, self.count, add, 0)
+        self._both().wait_send()
+        self._first().wait_send()
+        self._second().wait_send()
+
+    def start_far(self):
+        for distance in range(1, self.count):
+            self._far(distance).start()
+
+    def final(self, out):
+        value = self.total_[self.here["far"]].astype(WIDE)
+        for distance in range(1, self.count):
+            self._far(distance).wait_recv()
+            value = value + self.came_far[distance - 1].astype(WIDE)
+        out[pl.ds(*self.span), :] = value
+        for distance in range(1, self.count):
+            self._far(distance).wait_send()
+
+
+ORDERS = ("mod", "near")
+
+
+def run(parts, *names):
+    for part in parts:
+        for name in names:
+            getattr(part, name)()
+
+
+def reduce_kernel_parts(quads, scratch, totals=None):
+    by_flips = dict(zip(((False, False), (True, False), (False, True), (True, True)), quads))
+    parts = []
+    for number, span in enumerate(row_spans(quads[0].shape[1])):
+        used = 6 if totals is None else 5
+        buffers, scratch = list(scratch[:used]), scratch[used:]
+        if totals is not None:
+            buffers.insert(4, totals[number])
+        sems, scratch = scratch[:3], scratch[3:]
+        parts.append(Reduce(by_flips, span, ORDERS[number], buffers, sems))
+    return parts, scratch
+
+
+def reduce_scratch(shape, own_total=True):
+    count, rows, columns = shape
+    shapes = []
+    for span in row_spans(rows):
+        shapes += Reduce.scratch(count, span, columns, own_total)
+    return shapes
+
+
+def last_kernel(*refs, spans):
+    quads, totals, refs = refs[:4], refs[4 : 4 + spans], refs[4 + spans :]
+    qkv_out, fc1_out, *scratch = refs
+    qkv, scratch = reduce_kernel_parts(quads, scratch)
+    fc1 = []
+    for total, span in zip(totals, row_spans(fc1_out.shape[0])):
+        buffers = (None, None, None, None, total, scratch[0])
+        fc1.append(Reduce(None, span, "mod", buffers, (scratch[1], scratch[2], None)))
+        scratch = scratch[3:]
+    greet()
+    run(qkv, "start")
+    run(fc1, "start_far")
+    run(qkv, "merge")
+    run(qkv, "total", "start_far")
+    for part in fc1:
+        part.final(fc1_out)
+    for part in qkv:
+        part.final(qkv_out)
+
+
+def last_scatter(quads, totals):
+    count, rows, columns = quads[0].shape
+    fc1_columns = totals[0].shape[2]
+    fc1_scratch = []
+    for total in totals:
+        fc1_scratch += [
+            pltpu.VMEM((count - 1,) + total.shape[1:], LOW),
+            pltpu.SemaphoreType.DMA((count + 2,)),
+            pltpu.SemaphoreType.DMA((count + 2,)),
+        ]
+    return pl.pallas_call(
+        partial(last_kernel, spans=len(totals)),
+        out_shape=(
+            jax.ShapeDtypeStruct((rows, columns), WIDE),
+            jax.ShapeDtypeStruct((sum(total.shape[1] for total in totals), fc1_columns), WIDE),
+        ),
+        in_specs=[ANY] * 4 + [VMEM] * len(totals),
+        out_specs=(VMEM,) * 2,
+        scratch_shapes=reduce_scratch(quads[0].shape) + fc1_scratch,
+        compiler_params=pltpu.CompilerParams(
+            collective_id=3, has_side_effects=True, vmem_limit_bytes=50 * 2**20
+        ),
+        name="last_scatter",
+    )(*quads, *totals)
+
+
 def split3(v):
     hi = v.astype(LOW).astype(WIDE)
-    mid = (v-hi).astype(LOW).astype(WIDE)
-    lo = (v-hi-mid)
+    mid = (v - hi).astype(LOW).astype(WIDE)
+    lo = v - hi - mid
     return hi, mid, lo
 
-def attend_back_kernel(qkv_ref, seg_ref, mixed_ref, lse_ref, up_ref, out_ref, qh, kh, vh, uh):
-    T = qkv_ref.shape[0]
-    D = HEADS*HEAD
+
+def attend_back_kernel(*refs, spans):
+    qkv_ref, seg_ref, mixed_ref, lse_ref, up_ref = refs[:5]
+    fc2_q, fc1_q, proj_q = refs[5:9], refs[9:13], refs[13:17]
+    out_ref, fc2_out, proj_out = refs[17:20]
+    fc1_totals = refs[20 : 20 + spans]
+    qh, kh, vh, uh, stage, stage_sems, leave, leave_sems, *scratch = refs[20 + spans :]
+    fc2, scratch = reduce_kernel_parts(fc2_q, scratch)
+    proj, scratch = reduce_kernel_parts(proj_q, scratch)
+    fc1, scratch = reduce_kernel_parts(fc1_q, scratch, fc1_totals)
+    T = mixed_ref.shape[0]
+    chunks = T // CHUNK
+    greet()
+    run(fc2, "start")
+    run(proj, "start")
+
+    def load(i):
+        rows = pl.ds(pl.multiple_of(i * CHUNK, CHUNK), CHUNK)
+        slot = lax.rem(i, 2)
+        return pltpu.make_async_copy(qkv_ref.at[rows], stage.at[slot], stage_sems.at[slot])
+
+    load(0).start()
+
     def fill(i, carry):
-        rows = pl.ds(pl.multiple_of(i*CHUNK, CHUNK), CHUNK)
+        rows = pl.ds(pl.multiple_of(i * CHUNK, CHUNK), CHUNK)
+
+        @pl.when(i + 1 < chunks)
+        def _():
+            load(i + 1).start()
+
+        load(i).wait()
+        qkv = stage.at[lax.rem(i, 2)]
         lane = lanes((CHUNK, LANES))
         qc, kc = seg_codes(seg_ref[rows, :], CHUNK)
-        kc = jnp.where(jnp.logical_and(lane >= HEAD+4, lane < HEAD+7), 1.0, kc).astype(LOW)
-        ones = jnp.where(jnp.logical_and(lane >= HEAD, lane < HEAD+3), 1.0, 0.0).astype(LOW)
+        kc = jnp.where(jnp.logical_and(lane >= HEAD + 4, lane < HEAD + 7), 1.0, kc).astype(LOW)
+        ones = jnp.where(jnp.logical_and(lane >= HEAD, lane < HEAD + 3), 1.0, 0.0).astype(LOW)
+
         def spread(v, at, base):
             hi, mid, lo = split3(v)
-            return jnp.where(lane == at, hi, jnp.where(lane == at+1, mid, jnp.where(lane == at+2, lo, base)))
+            return jnp.where(
+                lane == at, hi, jnp.where(lane == at + 1, mid, jnp.where(lane == at + 2, lo, base))
+            )
+
         for h in range(HEADS):
-            a, b = h*HEAD, (h+1)*HEAD
-            qa = spread(-lse_ref[rows, h:h+1]*(1.0/HEAD**-0.5), HEAD+4, qc).astype(LOW)
-            qh[h, rows, :] = pad_head(qkv_ref[rows, a:b], qa)
-            kh[h, rows, :] = pad_head(qkv_ref[rows, D+a:D+b], kc)
-            vh[h, rows, :] = pad_head(qkv_ref[rows, 2*D+a:2*D+b], ones)
+            a, b = h * HEAD, (h + 1) * HEAD
+            qa = spread(-lse_ref[rows, h : h + 1] * HEAD**0.5, HEAD + 4, qc).astype(LOW)
+            qh[h, rows, :] = pad_head(qkv[:, a:b], qa)
+            kh[h, rows, :] = pad_head(qkv[:, D + a : D + b], kc)
+            vh[h, rows, :] = pad_head(qkv[:, 2 * D + a : 2 * D + b], ones)
             u = up_ref[rows, a:b]
-            delta = jnp.sum(u.astype(WIDE)*mixed_ref[rows, a:b].astype(WIDE), axis=1, keepdims=True)
-            ua = spread(-delta, HEAD, jnp.zeros((CHUNK,LANES),WIDE)).astype(LOW)
+            delta = jnp.sum(u.astype(WIDE) * mixed_ref[rows, a:b].astype(WIDE), axis=1, keepdims=True)
+            ua = spread(-delta, HEAD, jnp.zeros((CHUNK, LANES), WIDE)).astype(LOW)
             uh[h, rows, :] = pad_head(u, ua)
         return carry
-    lax.fori_loop(0, T//CHUNK, fill, 0)
-    NT = (((1,),(1,)),((),()))
+
+    lax.fori_loop(0, chunks, fill, 0)
+    across = (((1,), (1,)), ((), ()))
+    tasks = {
+        2: lambda: (run(fc2, "merge"), run(fc1, "start")),
+        7: lambda: run(proj, "merge"),
+        10: lambda: run(fc2, "total", "start_far"),
+        12: lambda: run(proj, "total", "start_far"),
+        13: lambda: run(fc1, "merge"),
+    }
+
     def head(h, carry):
-        k = kh[h]; v = vh[h]
+        k = kh[h]
+        v = vh[h]
         kt = k.T
-        dk = jnp.zeros((T, LANES), WIDE); dv = jnp.zeros((T, LANES), WIDE)
-        for i in range(T//CHUNK):
-            rows = pl.ds(i*CHUNK, CHUNK)
-            q = qh[h, rows, :]; u = uh[h, rows, :]
-            s = lax.dot_general(k, q, NT, preferred_element_type=WIDE)
-            p = jnp.exp2(s*(HEAD**-0.5*LOG2E))
-            dp = lax.dot_general(v, u, NT, preferred_element_type=WIDE)
-            ds = (p*dp).astype(LOW)
+        dk = jnp.zeros((T, LANES), WIDE)
+        dv = jnp.zeros((T, LANES), WIDE)
+        for i in range(chunks):
+            rows = pl.ds(i * CHUNK, CHUNK)
+            q = qh[h, rows, :]
+            u = uh[h, rows, :]
+            s = lax.dot_general(k, q, across, preferred_element_type=WIDE)
+            p = jnp.exp2(s * (HEAD**-0.5 * LOG2E))
+            dp = lax.dot_general(v, u, across, preferred_element_type=WIDE)
+            ds = (p * dp).astype(LOW)
             dv = dv + jnp.dot(p.astype(LOW), u, preferred_element_type=WIDE)
             dk = dk + jnp.dot(ds, q, preferred_element_type=WIDE)
             dqt = jnp.dot(kt, ds, preferred_element_type=WIDE)
-            qh[h, rows, :] = (dqt.T*HEAD**-0.5).astype(LOW)
-        kh[h] = (dk*HEAD**-0.5).astype(LOW)
+            qh[h, rows, :] = (dqt.T * HEAD**-0.5).astype(LOW)
+        kh[h] = (dk * HEAD**-0.5).astype(LOW)
         vh[h] = dv.astype(LOW)
+        for at, task in tasks.items():
+
+            @pl.when(h == at)
+            def _(task=task):
+                task()
+
         return carry
+
     lax.fori_loop(0, HEADS, head, 0)
+
+    def store(i, side):
+        rows = pl.ds(pl.multiple_of(i * CHUNK, CHUNK), CHUNK)
+        return pltpu.make_async_copy(
+            leave.at[side], out_ref.at[side, rows], leave_sems.at[side]
+        )
+
     def drain(i, carry):
-        rows = pl.ds(pl.multiple_of(i*CHUNK, CHUNK), CHUNK)
-        out_ref[rows, :] = jnp.concatenate([g[h, rows, :][:, :HEAD] for g in (qh,kh,vh) for h in range(HEADS)], axis=1)
+        rows = pl.ds(pl.multiple_of(i * CHUNK, CHUNK), CHUNK)
+        parts = [g[h, rows, :][:, :HEAD] for g in (qh, kh, vh) for h in range(HEADS)]
+        for side in range(2):
+
+            @pl.when(i > 0)
+            def _(side=side):
+                store(i - 1, side).wait()
+
+            own = parts[side * len(parts) // 2 : (side + 1) * len(parts) // 2]
+            leave[side] = jnp.concatenate(own, axis=1)
+            store(i, side).start()
         return carry
-    lax.fori_loop(0, T//CHUNK, drain, 0)
-
-
-def attend_back(qkv, segments, mixed, lse, upstream):
+
+    lax.fori_loop(0, chunks, drain, 0)
+    run(fc1, "total")
+    for side in range(2):
+        store(chunks - 1, side).wait()
+    for part in fc2:
+        part.final(fc2_out)
+    for part in proj:
+        part.final(proj_out)
+
+
+def attend_back(qkv, segments, mixed, lse, upstream, fc2_q, fc1_q, proj_q):
     tokens = qkv.shape[0]
-    return pl.pallas_call(
-        attend_back_kernel,
-        out_shape=jax.ShapeDtypeStruct((tokens, 3 * HEADS * HEAD), LOW),
-        in_specs=[VMEM] * 5,
-        out_specs=VMEM,
-        scratch_shapes=[pltpu.VMEM((HEADS, tokens, LANES), LOW)] * 4,
-        compiler_params=pltpu.CompilerParams(vmem_limit_bytes=63 * 2**20),
+    spans = row_spans(fc1_q[0].shape[1])
+
+    def shard(quads):
+        return jax.ShapeDtypeStruct(quads[0].shape[1:], WIDE)
+
+    out = pl.pallas_call(
+        partial(attend_back_kernel, spans=len(spans)),
+        out_shape=(
+            jax.ShapeDtypeStruct((2, tokens, 3 * HEADS * HEAD // 2), LOW),
+            shard(fc2_q),
+            shard(proj_q),
+        )
+        + tuple(
+            jax.ShapeDtypeStruct((fc1_q[0].shape[0], span[1], fc1_q[0].shape[2]), LOW)
+            for span in spans
+        ),
+        in_specs=[ANY] + [VMEM] * 4 + [ANY] * 12,
+        out_specs=(ANY, VMEM, VMEM) + (VMEM,) * len(spans),
+        scratch_shapes=[pltpu.VMEM((HEADS, tokens, LANES), LOW)] * 4
+        + [pltpu.VMEM((2, CHUNK, 3 * HEADS * HEAD), LOW), pltpu.SemaphoreType.DMA((2,))]
+        + [pltpu.VMEM((2, CHUNK, 3 * HEADS * HEAD // 2), LOW), pltpu.SemaphoreType.DMA((2,))]
+        + reduce_scratch(fc2_q[0].shape)
+        + reduce_scratch(proj_q[0].shape)
+        + reduce_scratch(fc1_q[0].shape, False),
+        compiler_params=pltpu.CompilerParams(
+            collective_id=2, has_side_effects=True, vmem_limit_bytes=63 * 2**20
+        ),
         name="attend_back",
-    )(qkv, segments.reshape(tokens, 1), mixed, lse, upstream)
+    )(qkv, segments.reshape(tokens, 1), mixed, lse, upstream, *fc2_q, *fc1_q, *proj_q)
+    return out[0], out[1], out[2], out[3:]
 
 
 def swap(values, axis):
     return lax.ppermute(values, axis, [(0, 1), (1, 0)])
 
 
-def shifted(values, distance, count):
-    return lax.ppermute(values, "far", [(i, (i + distance) % count) for i in range(count)])
-
-
-def scatter_gradient(left, right, first):
+def chip_quads(left, right):
     count = lax.axis_size("far")
-    here = lax.axis_index("far")
     near, core, half = lax.axis_index("near"), lax.axis_index("core"), lax.axis_index("mod")
     tokens = left.shape[0]
     blocks = left.reshape(tokens, count, 2, 2, -1)
@@ -428,37 +699,14 @@
         rows = lax.dynamic_index_in_dim(blocks, near ^ n, 2, False)
         rows = lax.dynamic_index_in_dim(rows, core ^ k, 2, False)
         columns = lax.dynamic_index_in_dim(right, half ^ m, 0, False)
-        product = jnp.dot(
-            rows.reshape(tokens, -1).T, columns, preferred_element_type=WIDE
-        )
+        product = times(rows.reshape(tokens, -1).T, columns)
         return product.reshape(count, -1, columns.shape[1])
 
     def chip_sum(n, m):
         came = swap(piece(n, 1, m).astype(LOW), "core")
         return (piece(n, 0, m) + came.astype(WIDE)).astype(LOW)
 
-    def joined(kept, sent, axis):
-        return (kept.astype(WIDE) + swap(sent, axis).astype(WIDE)).astype(LOW)
-
-    if first == "mod":
-        far_side = chip_sum(1, 1)
-        near_side = chip_sum(0, 1)
-        sent = joined(chip_sum(1, 0), far_side, "mod")
-        kept = joined(chip_sum(0, 0), near_side, "mod")
-        total = joined(kept, sent, "near")
-    else:
-        far_side = chip_sum(1, 1)
-        near_side = chip_sum(1, 0)
-        sent = joined(chip_sum(0, 1), far_side, "near")
-        kept = joined(chip_sum(0, 0), near_side, "near")
-        total = joined(kept, sent, "mod")
-    if count > 4:
-        return lax.psum_scatter(total.astype(WIDE), "far", scatter_dimension=0, tiled=False)
-    result = lax.dynamic_index_in_dim(total, here, 0, False).astype(WIDE)
-    for distance in range(1, count):
-        block = lax.dynamic_index_in_dim(total, (here + distance) % count, 0, False)
-        result = result + shifted(block, distance, count).astype(WIDE)
-    return result
+    return [chip_sum(n, m) for n, m in ((0, 0), (1, 0), (0, 1), (1, 1))]
 
 
 def times(left, right):
@@ -568,11 +816,11 @@
     branch_grad = (gate_mlp * upstream).astype(LOW)
     gate_mlp_grad = upstream * branch
     branch_halves = halves(branch_grad)
-    fc2_shard = scatter_gradient(hidden, branch_halves, "mod")
+    fc2_quads = chip_quads(hidden, branch_halves)
     hidden_grad = times_back(branch_halves[0], fc2_low[0]) + times_back(branch_halves[1], fc2_low[1])
     pre_grad = gelu_back(hidden_grad)[0].astype(LOW)
     pre_halves = halves(pre_grad)
-    fc1_shard = scatter_gradient(mlp_input, pre_halves, "near")
+    fc1_quads = chip_quads(mlp_input, pre_halves)
     mlp_grad = times_back(pre_halves[0], fc1_low[0]) + times_back(pre_halves[1], fc1_low[1])
     scale_mlp_grad = mlp_grad * second_norm
     middle_grad = upstream + normalize_back(
@@ -581,15 +829,24 @@
     attn_grad = (gate_attn * middle_grad).astype(LOW)
     gate_attn_grad = middle_grad * attn_out
     attn_halves = halves(attn_grad)
-    proj_shard = scatter_gradient(mixture, attn_halves, "mod")
+    proj_quads = chip_quads(mixture, attn_halves)
     mixture_grad = (
         times_back(attn_halves[0], proj_low[0]) + times_back(attn_halves[1], proj_low[1])
     ).astype(LOW)
-    joint_grad = attend_back(joint_rows, segments, mixture, log_totals, mixture_grad)
-    query_grad = joint_grad[:, 0:width]
-    value_grad = joint_grad[:, 2 * width :]
-    joint_halves = halves(joint_grad)
-    qkv_shard = scatter_gradient(attn_input, joint_halves, "near")
+    joint_halves, fc2_shard, proj_shard, fc1_totals = attend_back(
+        joint_rows,
+        segments,
+        mixture,
+        log_totals,
+        mixture_grad,
+        fc2_quads,
+        fc1_quads,
+        proj_quads,
+    )
+    query_grad = joint_halves[0, :, 0:width]
+    value_grad = joint_halves[1, :, width // 2 :]
+    qkv_quads = chip_quads(attn_input, joint_halves)
+    qkv_shard, fc1_shard = last_scatter(qkv_quads, fc1_totals)
     input_grad = times_back(joint_halves[0], qkv_low[0]) + times_back(joint_halves[1], qkv_low[1])
     scale_attn_grad = input_grad * first_norm
     x_grad = middle_grad + normalize_back(

time: 1080 us -> 1030 us (0.954)
  waiting for transfers between devices: 165 us -> 14.9 us
  Pallas kernels: 291 us -> 415 us
  starting transfers between devices: 45.6 us -> 28.3 us
  other arithmetic: 125 us -> 109 us
    pallas_call x1 -> x2, Pallas kernels: 73.8 us -> 198 us  [the longest x1 132 us: attend_back(): pl.pallas_call(partial(attend_back_kernel, spans=len(spans)), out_shape=(...]
    ppermute x29 -> x17, waiting for transfers between devices: 107 us -> 1.9 us  [swap(): return lax.ppermute(values, axis, [(0, 1), (1, 0)])]
    dot_general x10 -> x42, matrix products: 65.9 us -> 152 us  [times(): return jnp.dot(left, right, preferred_element_type=WIDE)]
    dot_general x32 -> x0, matrix products: 73.5 us -> none  [piece(): jnp.dot(rows.reshape(tokens, -1).T, columns, preferred_element_type=WIDE)]
    ppermute x12 -> x0, waiting for transfers between devices: 42.6 us -> none  [shifted(): lax.ppermute(values, 'far', [(i, (i + distance) % count) for i in range(c...]
    ppermute x12 -> x0, starting transfers between devices: 11.1 us -> none  [shifted(): lax.ppermute(values, 'far', [(i, (i + distance) % count) for i in range(c...]
  transfers between devices with their start and end apart: 46 -> 22, of which waited for: 19 -> 3; matrix products, arithmetic and copies ran while one was open for 5% -> 12% of each run, Pallas kernels for 7% -> 7%
where the time goes in v3:
time: 1030 us; the launch traced here: 1020 us
  Pallas kernels  415 us (40%)
  matrix products  260 us (25%)
  other arithmetic  109 us (11%)
  blocking collectives  105 us (10%)
  local copies, waits for them, and re-layouts  88.1 us (9%)
  starting transfers between devices  28.3 us (3%)
  waiting for transfers between devices  14.9 us (1%)
    dot_general x42, matrix products, times(): return jnp.dot(left, right, preferred_element_type=WIDE)  152 us
    pallas_call x1, Pallas kernels, attend(): pl.pallas_call(attend_kernel, out_shape=(jax.ShapeDtypeStruct((tokens, HE...  143 us
    pallas_call x1, Pallas kernels, attend_back(): pl.pallas_call(partial(attend_back_kernel, spans=len(spans)), out_shape=(...  132 us
    dot_general x9, matrix products, times_back(): lax.dot_general(left, right, (((1,), (1,)), ((), ())), preferred_element_...  90.1 us
    pallas_call x1, Pallas kernels, first_gather(): pl.pallas_call(first_kernel, out_shape=tuple((whole_shape(shard) for shar...  74.2 us
    pallas_call x1, Pallas kernels, last_scatter(): pl.pallas_call(partial(last_kernel, spans=len(totals)), out_shape=(jax.Sh...  66.1 us
    unnamed x1, blocking collectives  41.2 us
    all_gather x1, blocking collectives, body(): silu_all = lax.all_gather(cond_silu.astype(LOW), ROWS, axis=0, tiled=True)  39.6 us
  transfers between devices with their start and end apart: 22, of which 3 were waited for; matrix products, arithmetic and copies ran while one was open for 12% of the time, Pallas kernels for 7%

profile of v3, /device:TPU:0, one launch (start us, length us, event | category | flops | bytes accessed | tf_op | source)
XLA Modules:
  0.0 1022.4 jit_solution(9846299918465615247)
XLA Ops:
  6.8 7.4 all-to-all-start
  16.3 41.2 %all-reduce = bf16[9216]{0:T(1024)(128)(2,1)S(1)} all-reduce(bf16[9216]{0:T(1024)(128)(2,1)} %dynamic-update-slice), channel_id=1, replica_groups=mesh['far'=4,'near'=2,'core'=2,'mod'=2] {'far','near','core','mod'}, use_global_device_ids=true, to_apply=%add | all-reduce | flops 9216 | bytes 36864
  66.9 74.2 %first_gather.1 = (bf16[2,4,2,2,72,1728]{5,4,3,2,1,0:T(8,128)(2,1)}, bf16[2,4,2,2,72,576]{5,4,3,2,1,0:T(8,128)(2,1)}, bf16[2,4,2,2,72,2304]{5,4,3,2,1,0:T(8,128)(2,1)}) custom-call(bf16[72,1728]{1,0:T(8,128)(2,1)} %convert_element_type.246.refs_0_, bf16[72,576]{1,0:T(8,128)(2,1)} %convert_element_type.247.refs_1_, bf16[72,2304]{1,0:T(8,128)(2,1)} %convert_element_type.248.refs_2_), custom_call_target="tpu_custom_call" | custom-call | tf_op jit(solution)/shard_map/first_gather/pallas_call | solution.py:225
  141.1 39.6 %all_gather.9 = bf16[128,1152]{1,0:T(8,128)(2,1)S(1)} all-gather(bf16[8,1152]{1,0:T(8,128)(2,1)} %fusion.244), channel_id=1, replica_groups=mesh['far'=4,'near'=2,'core'=2,'mod'=2] {'far','near','core'}, dimensions={0}, use_global_device_ids=true | all-gather | bytes 313344 | tf_op jit(solution)/shard_map/all_gather | solution.py:754
  180.8 5.8 fusion.288
  193.7 6.9 all-to-all-done.1
  200.8 11.5 %fusion.214 = f32[1024,6912]{1,0:T(8,128)} fusion(bf16[4,6912]{1,0:T(4,128)(2,1)S(1)} %reshape.342, s32[1024]{0:T(1024)S(1)} %copy-done.71), kind=kOutput, calls=%fused_computation.242 | convolution fusion | flops 56627200 | bytes 28370944 | tf_op jit(solution)/shard_map/dot_general | solution.py:713
  212.2 4.6 fusion.23
  217.2 4.9 fusion.291
  222.1 4.9 fusion.292
  227.0 4.9 fusion.15.refs_0_
  231.9 142.6 %attend.1 = (bf16[1024,1152]{1,0:T(8,128)(2,1)S(1)}, f32[1024,128]{1,0:T(8,128)S(1)}, bf16[2,4,2,2,72,576]{5,4,3,2,1,0:T(8,128)(2,1)}, bf16[2,4,2,2,72,2304]{5,4...) custom-call(bf16[1024,3456]{1,0:T(8,128)(2,1)} %fusion.15.refs_0_, ...), custom_call_target="tpu_custom_call", output_to_operand_aliasing={{2}: (3, {}), {3}: (4, {})} | custom-call | tf_op jit(solution)/shard_map/attend/pallas_call | solution.py:322
  375.2 4.5 fusion.289
  395.3 8.9 fusion.287
  404.2 8.5 convert_reduce_fusion.2
  412.8 6.3 fusion.295
  419.1 12.9 %fusion.296 = f32[1024,2304]{1,0:T(8,128)S(1)} fusion(bf16[1024,1152]{1,0:T(8,128)(2,1)} %copy-done.26, bf16[1152,2304]{1,0:T(8,128)(2,1)} %bitcast.387), kind=kOutput, calls=%fused_computation.358 | convolution fusion | flops 5435817984 | bytes 17104896 | tf_op jit(solution)/shard_map/dot_general | solution.py:713
  432.1 5.4 fusion.286
  439.2 6.9 multiply_convert_fusion
  446.1 11.8 %fusion.297 = f32[1024,576]{1,0:T(8,128)} fusion(bf16[1024,4608]{1,0:T(8,128)(2,1)S(1)} %multiply_convert_fusion, bf16[4608,576]{1,0:T(8,128)(2,1)} %bitcast.385), kind=kOutput, calls=%fused_computation.359 | convolution fusion | flops 5435817984 | bytes 17104896 | tf_op jit(solution)/shard_map/dot_general | solution.py:713
  457.9 9.0 fusion.298
  466.9 13.3 %fusion.163 = f32[1024,4608]{1,0:T(8,128)} fusion(bf16[4608,576]{1,0:T(8,128)(2,1)} %bitcast.386, bf16[1024,1152]{1,0:T(8,128)(2,1)S(1)} %get-tuple-element.68), kind=kOutput, calls=%fused_computation.191 | convolution fusion | flops 5435817984 | bytes 25493504 | tf_op jit(solution)/shard_map/dot_general | solution.py:717
  480.1 25.6 %convert_reduce_fusion = (f32[4608]{0:T(1024)}, bf16[1024,4608]{1,0:T(8,128)(2,1)}) fusion(f32[4608]{0:T(1024)S(1)} %copy-done.70, f32[1024,2304]{1,0:T(8,128)} %copy-done.9, f32[1024,2304]{1,0:T(8,128)} %copy-done.8, f32[1024,4608]{1,0:T(8,128)} %fusion.163, bf16[4608,576]{1,0:T(8,128)(2,1)} %bitcast.383, bf16[1024,1152]{1,0:T(8,128)(2,1)} %copy-done.16), kind=kOutput, calls=%fused_computation.20 | convolution fusion | flops 5553778176 | bytes 54431744 | tf_op jit(solution)/shard_map/dot_general | solution.py:717
  505.7 11.3 %fusion.40 = f32[1024,1152]{1,0:T(8,128)} fusion(bf16[1152,2304]{1,0:T(8,128)(2,1)} %bitcast.389, bf16[1024,4608]{1,0:T(8,128)(2,1)} %get-tuple-element.118), kind=kOutput, calls=%fused_computation.80 | convolution fusion | flops 5435817984 | bytes 14745600 | tf_op jit(solution)/shard_map/dot_general | solution.py:717
  517.0 13.1 %fusion.282 = (f32[1024]{0:T(1024)S(1)}, f32[1024]{0:T(1024)S(1)}, f32[1024,1152]{1,0:T(8,128)S(1)}) fusion(f32[1024,6912]{1,0:T(8,128)} %fusion.214, f32[1024]{0:T(1024)S(1)} %add_rsqrt_fusion, f32[1024,1152]{1,0:T(8,128)} %copy-done.3, f32[1024]{0:T(1024)S(1)} %broadcast_multiply_fusion.4, f32[1024,1152]{1,0:T(8,128)} %fusion.40, ...), kind=kOutput, calls=%fused_computation.345 | convolution fusion | flops 5445253120 | bytes 28917760 | tf_op jit(solution)/shard_map/dot_general | solution.py:717
  530.1 14.2 %convert_reduce_fusion.3 = (f32[1152]{0:T(1024)}, bf16[1024,1152]{1,0:T(8,128)(2,1)S(1)}, f32[1024,1152]{1,0:T(8,128)}, bf16[1024,1152]{1,0:T(8,128)(2,1)}) fusion(f32[1024,6912]{1,0:T(8,128)} %fusion.214, f32[1024]{0:T(1024)S(1)} %get-tuple-element.119, f32[1024,1152]{1,0:T(8,128)S(1)} %bitcast.370, f32[1024]{0:T(1024)S(1)} %broadcast_multiply_fusion.4, ...), kind=kLoop, calls=%fused_computation.62 | loop fusion | flops 22412160 | bytes 40133632 | tf_op jit(solution)/shard_map/reduce_sum | solution.py:879
  550.1 8.2 slice_bitcast_fusion
  560.8 8.5 fusion.33
  574.7 9.6 copy.142
  584.3 9.7 copy.143
  598.6 9.1 fusion.14
  620.7 4.3 fusion.160
  625.1 4.5 copy.154
  630.7 4.5 convolution_convert_fusion.1
  672.6 131.9 %attend_back.1 = (bf16[2,1024,1728]{2,1,0:T(8,128)(2,1)}, f32[288,576]{1,0:T(8,128)}, f32[72,576]{1,0:T(8,128)}, bf16[4,72,2304]{2,1,0:T(8,128)(2,1)}) custom-call(bf16[1024,3456]{1,0:T(8,128)(2,1)} %fusion.15.refs_0_, s32[1024,1]{1,0:T(8,128)} %copy-done.1, bf16[1024,1152]{1,0:T(8,128)(2,1)} %copy-done, f32[1024,128]{1,0:T(8,128)} %copy-done.2, ...), custom_call_target="tpu_custom_call" | custom-call | tf_op jit(solution)/shard_map/attend_back/pallas_call | solution.py:661
  804.5 4.1 convert_reduce_fusion.4
  808.6 4.4 fusion.72
  819.8 6.7 fusion.59
  827.0 11.1 %constant_dynamic-update-slice_fusion.1 = (f32[1024,6912]{1,0:T(8,128)}, f32[1024,1152]{1,0:T(8,128)}) fusion(f32[1024,1152]{1,0:T(8,128)} %fusion.59, bf16[1152,1728]{1,0:T(8,128)(2,1)S(1)} %bitcast.396, bf16[2,1024,1728]{2,1,0:T(8,128)(2,1)} %get-tuple-element.46), kind=kOutput, calls=%fused_computation.291 | convolution fusion | flops 4078043136 | bytes 21807104 | tf_op jit(solution)/shard_map/dot_general | solution.py:717
  838.2 4.9 fusion.283
  843.2 8.0 fusion.28
  864.8 14.3 %convolution_convert_fusion = bf16[4,6912]{1,0:T(4,128)(2,1)} fusion(f32[1024,6912]{1,0:T(8,128)} %fusion.31, s32[1024]{0:T(1024)S(1)} %copy-done.72), kind=kOutput, calls=%fused_computation.28 | convolution fusion | flops 339770368 | bytes 28370944 | tf_op jit(solution)/shard_map/ts,tc->sc/dot_general | solution.py:860
  889.1 4.7 all-to-all-start.4
  893.9 24.3 %all_gather.11 = bf16[128,3456]{1,0:T(8,128)(2,1)S(1)} all-gather(bf16[8,3456]{1,0:T(8,128)(2,1)S(1)} %all_to_all.70), channel_id=1, replica_groups=mesh['far'=4,'near'=2,'core'=2,'mod'=2] {'far','near','core'}, dimensions={0}, use_global_device_ids=true | all-gather | bytes 940032 | tf_op jit(solution)/shard_map/all_gather | solution.py:864
  927.4 6.2 all-to-all-done.3
  938.3 4.9 fusion.85.refs_3_
  943.2 4.7 fusion.88.refs_2_
  953.0 66.1 %last_scatter.1 = (f32[72,1728]{1,0:T(8,128)S(1)}, f32[72,2304]{1,0:T(8,128)S(1)}) custom-call(bf16[4,72,1728]{2,1,0:T(8,128)(2,1)S(1)} %fusion.104.refs_0_, bf16[4,72,1728]{2,1,0:T(8,128)(2,1)S(1)} %fusion.101.refs_1_, bf16[4,72,1728]{2,1,0:T(8,128)(2,1)} %fusion.88.refs_2_, bf16[4,72,1728]{2,1,0:T(8,128)(2,1)} %fusion.85.refs_3_, ...), custom_call_target="tpu_custom_call" | custom-call | tf_op jit(solution)/shard_map/last_scatter/pallas_call | solution.py:507
  (397 shorter events, 165.0 us)
Async XLA Ops:
  0.7 59.4 %copy-start.93 = (f32[1,216]{1,0:T(1,128)S(1)}, f32[1,216]{1,0:T(1,128)}, u32[]{:S(2)}) copy-start(f32[1,216]{1,0:T(1,128)} %param.47) | copy-start | bytes 2596
  0.7 60.0 %copy-start.4 = (bf16[1024,1152]{1,0:T(8,128)(2,1)S(1)}, bf16[1024,1152]{1,0:T(8,128)(2,1)}, u32[]{:S(2)}) copy-start(bf16[1024,1152]{1,0:T(8,128)(2,1)} %param.25) | copy-start | bytes 7077892
  0.7 61.8 %copy-start.40 = (f32[72,2304]{1,0:T(8,128)S(1)}, f32[72,2304]{1,0:T(8,128)}, u32[]{:S(2)}) copy-start(f32[72,2304]{1,0:T(8,128)} %param.35) | copy-start | bytes 1990660
  2.1 61.1 %copy-start.31 = (bf16[72,3456]{1,0:T(8,128)(2,1)}, bf16[72,3456]{1,0:T(8,128)(2,1)S(1)}, u32[]{:S(2)}) copy-start(bf16[72,3456]{1,0:T(8,128)(2,1)S(1)} %convert_element_type.242) | copy-start | bytes 1492996
  4.7 59.9 %copy-start.71 = (s32[1024]{0:T(1024)S(1)}, s32[1024]{0:T(1024)}, u32[]{:S(2)}) copy-start(s32[1024]{0:T(1024)} %param.27) | copy-start | bytes 12292
  6.8 179.8 %all-to-all-start = ((bf16[72,16,216]{2,0,1:T(8,128)(2,1)}), bf16[72,16,216]{2,0,1:T(8,128)(2,1)}, u32[]{:S(2)}, u32[]{:S(2)}) async-start(bf16[72,16,216]{2,0,1:T(8,128)(2,1)} %copy.132), calls=%async_computation | async-start | bytes 1179648 | tf_op jit(solution)/shard_map/all_to_all | solution.py:756
  61.1 151.2 %copy-start.73 = (f32[1024]{0:T(1024)}, f32[1024]{0:T(1024)S(1)}, u32[]{:S(2)}) copy-start(f32[1024]{0:T(1024)S(1)} %broadcast_multiply_fusion.5) | copy-start | bytes 12292
  64.8 167.0 %copy-start.1 = (s32[1024,1]{1,0:T(8,128)}, s32[1024,1]{1,0:T(8,128)S(1)}, u32[]{:S(2)}) copy-start(s32[1024,1]{1,0:T(8,128)S(1)} %copy.137.refs_1_) | copy-start | bytes 12292
  190.2 10.3 %all-to-all-start.1 = ((bf16[32,4,216]{2,1,0:T(4,128)(2,1)}), bf16[32,4,216]{2,1,0:T(4,128)(2,1)S(1)}, u32[]{:S(2)}, u32[]{:S(2)}) async-start(bf16[32,4,216]{2,1,0:T(4,128)(2,1)} %all_to_all.64), calls=%async_computation.1 | async-start | bytes 131072 | tf_op jit(solution)/shard_map/all_to_all | solution.py:759
  392.6 137.5 %copy-start.75 = (f32[1024]{0:T(1024)}, f32[1024]{0:T(1024)S(1)}, u32[]{:S(2)}) copy-start(f32[1024]{0:T(1024)S(1)} %broadcast_multiply_fusion.4) | copy-start | bytes 12292
  395.3 134.8 %copy-start.85 = (f32[1024]{0:T(1024)}, f32[1024]{0:T(1024)S(1)}, u32[]{:S(2)}) copy-start(f32[1024]{0:T(1024)S(1)} %add_rsqrt_fusion) | copy-start | bytes 12292
  412.8 54.1 %copy-start.16 = (bf16[1024,1152]{1,0:T(8,128)(2,1)}, bf16[1024,1152]{1,0:T(8,128)(2,1)S(1)}, u32[]{:S(2)}) copy-start(bf16[1024,1152]{1,0:T(8,128)(2,1)S(1)} %get-tuple-element.68) | copy-start | bytes 7077892
  629.6 11.5 %collective-permute-start.11 = (bf16[4,72,576]{2,1,0:T(8,128)(2,1)}, bf16[4,72,576]{2,1,0:T(8,128)(2,1)S(1)}, u32[]{:S(2)}, u32[]{:S(2)}) collective-permute-start(bf16[4,72,576]{2,1,0:T(8,128)(2,1)} %convolution_convert_fusion.5), channel_id=1, source_target_pairs={{0,2},{2,0},{1,3},{3,1},{4,6},{6,4},{5,7},{7,5},{8,10},{10,8},{9,1... | collective-permute-start | bytes 995336 | tf_op jit(solution)/shard_map/ppermute | solution.py:689
  630.0 12.8 %collective-permute-start.10 = (bf16[4,72,576]{2,1,0:T(8,128)(2,1)S(1)}, bf16[4,72,576]{2,1,0:T(8,128)(2,1)S(1)}, u32[]{:S(2)}, u32[]{:S(2)}) collective-permute-start(bf16[4,72,576]{2,1,0:T(8,128)(2,1)S(1)} %convolution_convert_fusion.6), channel_id=1, source_target_pairs={{0,2},{2,0},{1,3},{3,1},{4,6},{6,4},{5,7},{7,5},{8,10},{10,8},{9,1... | collective-permute-start | bytes 995336 | tf_op jit(solution)/shard_map/ppermute | solution.py:689
  630.2 14.4 %collective-permute-start.9 = (bf16[4,72,576]{2,1,0:T(8,128)(2,1)S(1)}, bf16[4,72,576]{2,1,0:T(8,128)(2,1)S(1)}, u32[]{:S(2)}, u32[]{:S(2)}) collective-permute-start(bf16[4,72,576]{2,1,0:T(8,128)(2,1)S(1)} %convolution_convert_fusion.7), channel_id=1, source_target_pairs={{0,2},{2,0},{1,3},{3,1},{4,6},{6,4},{5,7},{7,5},{8,10},{10,8},{9,1... | collective-permute-start | bytes 995336 | tf_op jit(solution)/shard_map/ppermute | solution.py:689
  630.6 15.7 %collective-permute-start.8 = (bf16[4,72,576]{2,1,0:T(8,128)(2,1)S(1)}, bf16[4,72,576]{2,1,0:T(8,128)(2,1)S(1)}, u32[]{:S(2)}, u32[]{:S(2)}) collective-permute-start(bf16[4,72,576]{2,1,0:T(8,128)(2,1)S(1)} %convolution_convert_fusion.8), channel_id=1, source_target_pairs={{0,2},{2,0},{1,3},{3,1},{4,6},{6,4},{5,7},{7,5},{8,10},{10,8},{9,1... | collective-permute-start | bytes 995336 | tf_op jit(solution)/shard_map/ppermute | solution.py:689
  635.3 12.6 %collective-permute-start.7 = (bf16[4,72,2304]{2,1,0:T(8,128)(2,1)S(1)}, bf16[4,72,2304]{2,1,0:T(8,128)(2,1)S(1)}, u32[]{:S(2)}, u32[]{:S(2)}) collective-permute-start(bf16[4,72,2304]{2,1,0:T(8,128)(2,1)S(1)} %convolution_convert_fusion.1), channel_id=1, source_target_pairs={{0,2},{2,0},{1,3},{3,1},{4,6},{6,4},{5,7},{7,5},{8,10},{10,8},{9,1... | collective-permute-start | bytes 3981320 | tf_op jit(solution)/shard_map/ppermute | solution.py:689
  641.1 9.7 collective-permute-start.6
  642.9 21.2 %collective-permute-start.5 = (bf16[4,72,2304]{2,1,0:T(8,128)(2,1)S(1)}, bf16[4,72,2304]{2,1,0:T(8,128)(2,1)S(1)}, u32[]{:S(2)}, u32[]{:S(2)}) collective-permute-start(bf16[4,72,2304]{2,1,0:T(8,128)(2,1)S(1)} %copy-done.104), channel_id=1, source_target_pairs={{0,2},{2,0},{1,3},{3,1},{4,6},{6,4},{5,7},{7,5},{8,10},{10,8},{9,1... | collective-permute-start | bytes 3981320 | tf_op jit(solution)/shard_map/ppermute | solution.py:689
  644.6 9.3 collective-permute-start.3
  646.2 20.5 %collective-permute-start.4 = (bf16[4,72,2304]{2,1,0:T(8,128)(2,1)S(1)}, bf16[4,72,2304]{2,1,0:T(8,128)(2,1)S(1)}, u32[]{:S(2)}, u32[]{:S(2)}) collective-permute-start(bf16[4,72,2304]{2,1,0:T(8,128)(2,1)S(1)} %copy-done.103), channel_id=1, source_target_pairs={{0,2},{2,0},{1,3},{3,1},{4,6},{6,4},{5,7},{7,5},{8,10},{10,8},{9,1... | collective-permute-start | bytes 3981320 | tf_op jit(solution)/shard_map/ppermute | solution.py:689
  647.9 9.4 collective-permute-start.2
  650.9 10.0 collective-permute-start.1
  653.8 15.6 %collective-permute-start = (bf16[4,288,576]{2,1,0:T(8,128)(2,1)S(1)}, bf16[4,288,576]{2,1,0:T(8,128)(2,1)S(1)}, u32[]{:S(2)}, u32[]{:S(2)}) collective-permute-start(bf16[4,288,576]{2,1,0:T(8,128)(2,1)S(1)} %copy-done.99), channel_id=1, source_target_pairs={{0,2},{2,0},{1,3},{3,1},{4,6},{6,4},{5,7},{7,5},{8,10},{10,8},{9,1... | collective-permute-start | bytes 3981320 | tf_op jit(solution)/shard_map/ppermute | solution.py:689
  826.5 111.9 %collective-permute-start.16 = (bf16[4,72,1728]{2,1,0:T(8,128)(2,1)}, bf16[4,72,1728]{2,1,0:T(8,128)(2,1)}, u32[]{:S(2)}, u32[]{:S(2)}) collective-permute-start(bf16[4,72,1728]{2,1,0:T(8,128)(2,1)} %fusion.72), channel_id=1, source_target_pairs={{0,2},{2,0},{1,3},{3,1},{4,6},{6,4},{5,7},{7,5},{8,10},{10,8},{9,1... | collective-permute-start | bytes 2985992 | tf_op jit(solution)/shard_map/ppermute | solution.py:689
  826.5 123.8 %collective-permute-start.13 = (bf16[4,72,1728]{2,1,0:T(8,128)(2,1)}, bf16[4,72,1728]{2,1,0:T(8,128)(2,1)}, u32[]{:S(2)}, u32[]{:S(2)}) collective-permute-start(bf16[4,72,1728]{2,1,0:T(8,128)(2,1)} %fusion.63), channel_id=1, source_target_pairs={{0,2},{2,0},{1,3},{3,1},{4,6},{6,4},{5,7},{7,5},{8,10},{10,8},{9,1... | collective-permute-start | bytes 2985992 | tf_op jit(solution)/shard_map/ppermute | solution.py:689
  879.1 39.0 %copy-start.37 = (f32[72,3456]{1,0:T(8,128)S(1)}, f32[72,3456]{1,0:T(8,128)}, u32[]{:S(2)}) copy-start(f32[72,3456]{1,0:T(8,128)} %param.44) | copy-start | bytes 2985988
  879.1 39.0 %copy-start.62 = (f32[72,3456]{1,0:T(8,128)S(1)}, f32[72,3456]{1,0:T(8,128)}, u32[]{:S(2)}) copy-start(f32[72,3456]{1,0:T(8,128)} %param.46) | copy-start | bytes 2985988
  879.1 9.9 all-to-all-start.2
  885.8 35.8 %copy-start.32 = (bf16[72,3456]{1,0:T(8,128)(2,1)S(1)}, bf16[72,3456]{1,0:T(8,128)(2,1)}, u32[]{:S(2)}) copy-start(bf16[72,3456]{1,0:T(8,128)(2,1)} %copy-done.31) | copy-start | bytes 1492996
  888.5 54.6 %collective-permute-start.15 = (bf16[4,72,1728]{2,1,0:T(8,128)(2,1)}, bf16[4,72,1728]{2,1,0:T(8,128)(2,1)}, u32[]{:S(2)}, u32[]{:S(2)}) collective-permute-start(bf16[4,72,1728]{2,1,0:T(8,128)(2,1)} %fusion.69), channel_id=1, source_target_pairs={{0,2},{2,0},{1,3},{3,1},{4,6},{6,4},{5,7},{7,5},{8,10},{10,8},{9,1... | collective-permute-start | bytes 2985992 | tf_op jit(solution)/shard_map/ppermute | solution.py:689
  888.6 59.3 %collective-permute-start.14 = (bf16[4,72,1728]{2,1,0:T(8,128)(2,1)}, bf16[4,72,1728]{2,1,0:T(8,128)(2,1)}, u32[]{:S(2)}, u32[]{:S(2)}) collective-permute-start(bf16[4,72,1728]{2,1,0:T(8,128)(2,1)} %fusion.66), channel_id=1, source_target_pairs={{0,2},{2,0},{1,3},{3,1},{4,6},{6,4},{5,7},{7,5},{8,10},{10,8},{9,1... | collective-permute-start | bytes 2985992 | tf_op jit(solution)/shard_map/ppermute | solution.py:689
  889.1 33.7 %all-to-all-start.4 = ((f32[32,1,288]{2,1,0:T(1,128)}), f32[32,1,288]{2,1,0:T(1,128)S(1)}, u32[]{:S(2)}, u32[]{:S(2)}) async-start(f32[32,1,288]{2,1,0:T(1,128)} %all_to_all.75), calls=%async_computation.4 | async-start | bytes 98304 | tf_op jit(solution)/shard_map/all_to_all | solution.py:884
  893.8 32.9 %copy-start.94 = (f32[1,216]{1,0:T(1,128)S(1)}, f32[1,216]{1,0:T(1,128)}, u32[]{:S(2)}) copy-start(f32[1,216]{1,0:T(1,128)} %param.47) | copy-start | bytes 2596
  893.8 32.9 %copy-start.97 = (f32[1,216]{1,0:T(1,128)S(1)}, f32[1,216]{1,0:T(1,128)}, u32[]{:S(2)}) copy-start(f32[1,216]{1,0:T(1,128)} %param.49) | copy-start | bytes 2596
  893.8 32.9 %copy-start.98 = (f32[1,216]{1,0:T(1,128)S(1)}, f32[1,216]{1,0:T(1,128)}, u32[]{:S(2)}) copy-start(f32[1,216]{1,0:T(1,128)} %param.48) | copy-start | bytes 2596
  893.8 41.4 %copy-start.92 = (f32[288]{0:T(512)S(1)}, f32[288]{0:T(512)}, u32[]{:S(2)}) copy-start(f32[288]{0:T(512)} %param.41) | copy-start | bytes 3460
  893.8 41.4 %copy-start.95 = (f32[288]{0:T(512)S(1)}, f32[288]{0:T(512)}, u32[]{:S(2)}) copy-start(f32[288]{0:T(512)} %param.43) | copy-start | bytes 3460
  893.9 41.4 %copy-start.96 = (f32[288]{0:T(512)S(1)}, f32[288]{0:T(512)}, u32[]{:S(2)}) copy-start(f32[288]{0:T(512)} %param.42) | copy-start | bytes 3460
  893.9 43.8 %copy-start.80 = (bf16[8,1152]{1,0:T(8,128)(2,1)S(1)}, bf16[8,1152]{1,0:T(8,128)(2,1)}, u32[]{:S(2)}) copy-start(bf16[8,1152]{1,0:T(8,128)(2,1)} %param.26) | copy-start | bytes 55300
  922.7 10.8 %all-to-all-start.3 = ((f32[16,8,72]{2,1,0:T(8,128)}), f32[16,8,72]{2,1,0:T(8,128)S(1)}, u32[]{:S(2)}, u32[]{:S(2)}) async-start(f32[16,8,72]{2,1,0:T(8,128)} %convolution_bitcast_fusion), calls=%async_computation.3 | async-start | bytes 131072 | tf_op jit(solution)/shard_map/all_to_all | solution.py:874
  933.6 4.0 collective-permute-start.12
  952.9 66.2 %copy-start.41 = (f32[72,2304]{1,0:T(8,128)S(1)}, f32[72,2304]{1,0:T(8,128)}, u32[]{:S(2)}) copy-start(f32[72,2304]{1,0:T(8,128)} %param.35) | copy-start | bytes 1990660
  952.9 66.2 %copy-start.65 = (f32[72,2304]{1,0:T(8,128)S(1)}, f32[72,2304]{1,0:T(8,128)}, u32[]{:S(2)}) copy-start(f32[72,2304]{1,0:T(8,128)} %param.37) | copy-start | bytes 1990660
  952.9 66.2 %copy-start.66 = (f32[72,2304]{1,0:T(8,128)S(1)}, f32[72,2304]{1,0:T(8,128)}, u32[]{:S(2)}) copy-start(f32[72,2304]{1,0:T(8,128)} %param.36) | copy-start | bytes 1990660
  952.9 67.7 %copy-start.49 = (f32[72,1728]{1,0:T(8,128)S(1)}, f32[72,1728]{1,0:T(8,128)}, u32[]{:S(2)}) copy-start(f32[72,1728]{1,0:T(8,128)} %param.29) | copy-start | bytes 1492996
  952.9 67.6 %copy-start.67 = (f32[72,1728]{1,0:T(8,128)S(1)}, f32[72,1728]{1,0:T(8,128)}, u32[]{:S(2)}) copy-start(f32[72,1728]{1,0:T(8,128)} %param.31) | copy-start | bytes 1492996
  952.9 67.6 %copy-start.68 = (f32[72,1728]{1,0:T(8,128)S(1)}, f32[72,1728]{1,0:T(8,128)}, u32[]{:S(2)}) copy-start(f32[72,1728]{1,0:T(8,128)} %param.30) | copy-start | bytes 1492996
  (100 other events, 808.3 us)

commit v4 on v3

--- a/solution.py
+++ b/solution.py
@@ -28,20 +28,6 @@
 EPS = 1e-06
 MOMENTUM = 0.9
 DECAY = 0.5
-
-
-def normalize(values):
-    centre = values - jnp.mean(values, axis=-1, keepdims=True)
-    inverse = lax.rsqrt(jnp.mean(centre * centre, axis=-1, keepdims=True) + EPS)
-    return (centre * inverse, inverse)
-
-
-def normalize_back(upstream, normed, inverse):
-    return inverse * (
-        upstream
-        - jnp.mean(upstream, axis=-1, keepdims=True)
-        - normed * jnp.mean(upstream * normed, axis=-1, keepdims=True)
-    )
 
 
 def step_rates(tokens_all):
@@ -202,15 +188,21 @@
 
 
 def first_kernel(*refs):
-    qkv_s, proj_s, fc1_s, qkv_w, proj_w, fc1_w = refs[:6]
-    *sems, local = refs[6:]
-    qkv, proj, fc1 = (
-        Gather(w, s, r) for w, s, r in zip((qkv_w, proj_w, fc1_w), sems[0::2], sems[1::2])
+    small_s, qkv_s, proj_s, fc1_s = refs[:4]
+    *sems, local = refs[8:]
+    small, qkv, proj, fc1 = (
+        Gather(w, s, r) for w, s, r in zip(refs[4:8], sems[0::2], sems[1::2])
     )
     greet()
+    small.start_far(small_s, local.at[3])
     qkv.start_far(qkv_s, local.at[0])
     proj.start_far(proj_s, local.at[1])
     fc1.start_far(fc1_s, local.at[2])
+    small.finish_far(small_s, local.at[3])
+    small.spread()
+    small.cross()
+    small.close()
+    small.end()
     qkv.finish_far(qkv_s, local.at[0])
     qkv.spread()
     qkv.cross()
@@ -220,14 +212,13 @@
     fc1.finish_far(fc1_s, local.at[2])
 
 
-def first_gather(qkv_s, proj_s, fc1_s):
-    shards = (qkv_s, proj_s, fc1_s)
+def first_gather(*shards):
     return pl.pallas_call(
         first_kernel,
         out_shape=tuple(whole_shape(shard) for shard in shards),
-        in_specs=[VMEM] * 3,
-        out_specs=(ANY,) * 3,
-        scratch_shapes=gather_scratch(3, 3),
+        in_specs=[VMEM] * 4,
+        out_specs=(ANY,) * 4,
+        scratch_shapes=gather_scratch(4, 4),
         compiler_params=pltpu.CompilerParams(collective_id=0, has_side_effects=True),
         name="first_gather",
     )(*shards)
@@ -685,6 +676,238 @@
     return out[0], out[1], out[2], out[3:]
 
 
+def normed(values):
+    centre = values - jnp.mean(values, axis=-1, keepdims=True)
+    inverse = lax.rsqrt(jnp.mean(centre * centre, axis=-1, keepdims=True) + EPS)
+    return centre * inverse, inverse
+
+
+def row_of(table, slot, group):
+    return table[pl.ds(slot, 1), group * D : (group + 1) * D]
+
+
+def column_sums(values):
+    return jnp.sum(values, axis=0, keepdims=True)
+
+
+def times_across(left, right):
+    return lax.dot_general(left, right, (((1,), (1,)), ((), ())), preferred_element_type=WIDE)
+
+
+def tile(*shape):
+    return pl.BlockSpec((CHUNK,) + shape, lambda i, slots: (i,) + (0,) * len(shape))
+
+
+def half_tile(columns):
+    return pl.BlockSpec((2, CHUNK, columns), lambda i, slots: (0, i, 0))
+
+
+def fixed(*shape):
+    return pl.BlockSpec(
+        shape, lambda i, slots: (0,) * len(shape), pipeline_mode=pl.Buffered(1)
+    )
+
+
+def per_tile(rows, columns):
+    return pl.BlockSpec((1, rows, columns), lambda i, slots: (i, 0, 0))
+
+
+def tile_call(kernel, tokens, in_specs, out_specs, out_shapes, scratch, name, flops, traffic):
+    return pl.pallas_call(
+        kernel,
+        out_shape=tuple(jax.ShapeDtypeStruct(shape, dtype) for shape, dtype in out_shapes),
+        grid_spec=pltpu.PrefetchScalarGridSpec(
+            num_scalar_prefetch=1,
+            grid=(tokens // CHUNK,),
+            in_specs=in_specs,
+            out_specs=out_specs,
+            scratch_shapes=scratch,
+        ),
+        compiler_params=pltpu.CompilerParams(
+            dimension_semantics=("arbitrary",), vmem_limit_bytes=63 * 2**20
+        ),
+        cost_estimate=pl.CostEstimate(flops=flops, bytes_accessed=traffic, transcendentals=0),
+        name=name,
+    )
+
+
+def qkv_forward_kernel(slots, x_ref, table, bias, weight, act_ref, joint_ref):
+    slot = slots[pl.program_id(0)]
+    h1, _ = normed(x_ref[...].astype(WIDE))
+    act = (h1 * (1.0 + row_of(table, slot, 1)) + row_of(table, slot, 0)).astype(LOW)
+    act_ref[...] = act
+    joint = jnp.concatenate([times(act, weight[0]), times(act, weight[1])], axis=1)
+    joint_ref[...] = (joint + bias[...]).astype(LOW)
+
+
+def qkv_forward(slots, x_in, table, bias, weight):
+    tokens = x_in.shape[0]
+    wide = 3 * D
+    return tile_call(
+        qkv_forward_kernel,
+        tokens,
+        [tile(D), fixed(*table.shape), fixed(1, wide), fixed(*weight.shape)],
+        (tile(D), tile(wide)),
+        (((tokens, D), LOW), ((tokens, wide), LOW)),
+        [],
+        "qkv_forward",
+        2 * tokens * D * wide,
+        weight.size * 2 + tokens * D * 10,
+    )(slots, x_in, table, bias, weight)
+
+
+GELU = 0.7978845608028654
+CUBIC = 0.044715
+SPAN = 768
+
+
+def middle_kernel(
+    slots, x_ref, g_ref, mixed_ref, table, bias, proj, fc1, fc2,
+    block_ref, mlp_ref, hidden_ref, dpre_ref, dbranch_ref, dattn_ref, dmixed_ref, dx1_ref, sums_ref, dpre_sums,
+    slope,
+):
+    slot = slots[pl.program_id(0)]
+    gate1, shift2, scale2, gate2 = (row_of(table, slot, group) for group in (2, 3, 4, 5))
+    half = FF // 2
+    mixed = mixed_ref[...]
+    attn_out = jnp.concatenate([times(mixed, proj[0]), times(mixed, proj[1])], axis=1)
+    attn_out = attn_out + bias[:, 2 * D : 3 * D]
+    x1 = x_ref[...].astype(WIDE) + gate1 * attn_out
+    h2, inverse = normed(x1)
+    mlp_in = (h2 * (1.0 + scale2) + shift2).astype(LOW)
+    mlp_ref[...] = mlp_in
+    for side in range(2):
+        for at in range(0, half, SPAN):
+            column = side * half + at
+            pre = times(mlp_in, fc1[side, :, at : at + SPAN])
+            pre = pre + bias[:, 3 * D + column : 3 * D + column + SPAN]
+            square = pre * pre
+            bend = jnp.tanh(GELU * pre * (1.0 + CUBIC * square))
+            rise = 0.5 * (1.0 + bend)
+            hidden_ref[:, column : column + SPAN] = (pre * rise).astype(LOW)
+            slope[:, column : column + SPAN] = rise + 0.5 * GELU * pre * (1.0 - bend * bend) * (
+                1.0 + 3.0 * CUBIC * square
+            )
+    hidden = hidden_ref[...]
+    branch = jnp.concatenate([times(hidden, fc2[0]), times(hidden, fc2[1])], axis=1)
+    branch = branch + bias[:, 3 * D + FF :]
+    block_ref[...] = (x1 + gate2 * branch).astype(LOW)
+    g = g_ref[...].astype(WIDE)
+    dbranch = (gate2 * g).astype(LOW)
+    sums_ref[0, 3:4, :] = column_sums(g * branch)
+    sums_ref[0, 5:6, :] = column_sums(dbranch.astype(WIDE))
+    left, right = dbranch[:, : D // 2], dbranch[:, D // 2 :]
+    dbranch_ref[0] = left
+    dbranch_ref[1] = right
+    for side in range(2):
+        for at in range(0, half, SPAN):
+            column = side * half + at
+            rows = slice(column, column + SPAN)
+            dhidden = times_across(left, fc2[0, rows]) + times_across(right, fc2[1, rows])
+            dpre = (dhidden * slope[:, rows]).astype(LOW)
+            dpre_ref[side, :, at : at + SPAN] = dpre
+            dpre_sums[0, :, rows] = column_sums(dpre.astype(WIDE))
+    dmlp = times_across(dpre_ref[0], fc1[0]) + times_across(dpre_ref[1], fc1[1])
+    sums_ref[0, 1:2, :] = column_sums(dmlp)
+    sums_ref[0, 2:3, :] = column_sums(dmlp * h2)
+    dh2 = dmlp * (1.0 + scale2)
+    dx1 = g + inverse * (
+        dh2
+        - jnp.mean(dh2, axis=-1, keepdims=True)
+        - h2 * jnp.mean(dh2 * h2, axis=-1, keepdims=True)
+    )
+    dx1_ref[...] = dx1
+    sums_ref[0, 0:1, :] = column_sums(dx1 * attn_out)
+    dattn = (gate1 * dx1).astype(LOW)
+    sums_ref[0, 4:5, :] = column_sums(dattn.astype(WIDE))
+    left, right = dattn[:, : D // 2], dattn[:, D // 2 :]
+    dattn_ref[0] = left
+    dattn_ref[1] = right
+    dmixed_ref[...] = (times_across(left, proj[0]) + times_across(right, proj[1])).astype(LOW)
+    sums_ref[0, 6:8, :] = jnp.zeros((2, D), WIDE)
+
+
+def middle(slots, x_in, out_grad, mixed, table, bias, proj, fc1, fc2):
+    tokens = x_in.shape[0]
+    tiles = tokens // CHUNK
+    return tile_call(
+        middle_kernel,
+        tokens,
+        [
+            tile(D),
+            tile(D),
+            tile(D),
+            fixed(*table.shape),
+            fixed(*bias.shape),
+            fixed(*proj.shape),
+            fixed(*fc1.shape),
+            fixed(*fc2.shape),
+        ],
+        (
+            tile(D),
+            tile(D),
+            tile(FF),
+            half_tile(FF // 2),
+            half_tile(D // 2),
+            half_tile(D // 2),
+            tile(D),
+            tile(D),
+            per_tile(8, D),
+            per_tile(1, FF),
+        ),
+        (
+            ((tokens, D), LOW),
+            ((tokens, D), LOW),
+            ((tokens, FF), LOW),
+            ((2, tokens, FF // 2), LOW),
+            ((2, tokens, D // 2), LOW),
+            ((2, tokens, D // 2), LOW),
+            ((tokens, D), LOW),
+            ((tokens, D), WIDE),
+            ((tiles, 8, D), WIDE),
+            ((tiles, 1, FF), WIDE),
+        ),
+        [pltpu.VMEM((CHUNK, FF), WIDE)],
+        "middle",
+        4 * tokens * (D * D + 2 * D * FF),
+        (D * D + 2 * D * FF) * 2 + tokens * D * 40,
+    )(slots, x_in, out_grad, mixed, table, bias, proj, fc1, fc2)
+
+
+def qkv_backward_kernel(slots, joint_ref, x_ref, dx1_ref, table, weight, x_grad_ref, sums_ref, joint_sums):
+    slot = slots[pl.program_id(0)]
+    dact = times_across(joint_ref[0], weight[0]) + times_across(joint_ref[1], weight[1])
+    h1, inverse = normed(x_ref[...].astype(WIDE))
+    sums_ref[0, 0:1, :] = column_sums(dact)
+    sums_ref[0, 1:2, :] = column_sums(dact * h1)
+    sums_ref[0, 2:8, :] = jnp.zeros((6, D), WIDE)
+    dh1 = dact * (1.0 + row_of(table, slot, 1))
+    x_grad_ref[...] = dx1_ref[...] + inverse * (
+        dh1
+        - jnp.mean(dh1, axis=-1, keepdims=True)
+        - h1 * jnp.mean(dh1 * h1, axis=-1, keepdims=True)
+    )
+    for side in range(2):
+        joint_sums[0, side : side + 1, :] = column_sums(joint_ref[side].astype(WIDE))
+
+
+def qkv_backward(slots, joint, x_in, dx1, table, weight):
+    tokens = x_in.shape[0]
+    tiles = tokens // CHUNK
+    half = 3 * D // 2
+    return tile_call(
+        qkv_backward_kernel,
+        tokens,
+        [half_tile(half), tile(D), tile(D), fixed(*table.shape), fixed(*weight.shape)],
+        (tile(D), per_tile(8, D), per_tile(2, half)),
+        (((tokens, D), WIDE), ((tiles, 8, D), WIDE), ((tiles, 2, half), WIDE)),
+        [],
+        "qkv_backward",
+        2 * tokens * D * 3 * D,
+        weight.size * 2 + tokens * D * 18,
+    )(slots, joint, x_in, dx1, table, weight)
+
+
 def swap(values, axis):
     return lax.ppermute(values, axis, [(0, 1), (1, 0)])
 
@@ -751,88 +974,50 @@
     images = cond.shape[0] // 2
 
     cond_silu, silu_back = jax.vjp(jax.nn.silu, cond.astype(WIDE))
-    silu_all = lax.all_gather(cond_silu.astype(LOW), ROWS, axis=0, tiled=True)
+    half_silu = lax.dynamic_index_in_dim(
+        cond_silu.astype(LOW).reshape(-1, 2, width // 2), lax.axis_index("mod"), 1, False
+    )
+    own_bias = bias_weight.shape[0]
+    bias_block = jnp.pad(bias_weight.astype(LOW), (0, 8 * LANES - own_bias)).reshape(8, LANES)
+    blank = jnp.zeros((8, LANES // 2), LOW)
     ada_low = ada_weight.astype(LOW)
     ada_columns = lax.all_to_all(ada_low, ROWS, split_axis=1, concat_axis=0, tiled=True)
+    small_w, qkv_w, proj_w, fc1_w = first_gather(
+        jnp.concatenate([half_silu, bias_block, blank], axis=1),
+        qkv_weight.astype(LOW),
+        proj_weight.astype(LOW),
+        fc1_weight.astype(LOW),
+    )
+    small = small_w.reshape(2, row_devices * 8, -1)
+    silu_all = jnp.concatenate([small[0, :, : width // 2], small[1, :, : width // 2]], axis=1)
+    bias_all = small[:, :, width // 2 : width // 2 + LANES].reshape(2, row_devices, -1)
+    bias_full = jnp.swapaxes(bias_all[:, :, :own_bias], 0, 1).reshape(1, -1).astype(WIDE)
     adab_low = adab_weight.astype(LOW).astype(WIDE)
     mod_columns = (times(silu_all, ada_columns) + adab_low).astype(LOW)
     mod_rows = lax.all_to_all(mod_columns, ALL, split_axis=0, concat_axis=1, tiled=True)
-    modulation = jnp.swapaxes(
-        mod_rows.reshape(images, row_devices, 2, -1), 1, 2
-    ).reshape(images, -1)
-
-    bias_full = lax.all_gather(bias_weight.astype(LOW), ALL, axis=0, tiled=True).astype(WIDE)
-    qkv_w, proj_w, fc1_w = first_gather(
-        qkv_weight.astype(LOW), proj_weight.astype(LOW), fc1_weight.astype(LOW)
-    )
+    table = jnp.swapaxes(mod_rows.reshape(images, row_devices, 2, -1), 1, 2).reshape(images, -1)
+    table = table.astype(WIDE)
 
     def joined(whole):
         return whole.reshape(2, -1, whole.shape[-1])
 
     qkv_low = joined(qkv_w)
-
-    chooser = segments[:, None] == jnp.arange(images, dtype=jnp.int32)[None, :]
-    per_token = times(chooser.astype(LOW), modulation)
-    shift_attn, scale_attn, gate_attn, shift_mlp, scale_mlp, gate_mlp = [
-        per_token[:, group * width : (group + 1) * width] for group in range(6)
-    ]
-    residual = x_in.astype(WIDE)
-    first_norm, first_inverse = normalize(residual)
-    attn_input = (first_norm * (1.0 + scale_attn) + shift_attn).astype(LOW)
-    joint_proj = jnp.concatenate([times(attn_input, qkv_low[0]), times(attn_input, qkv_low[1])], 1)
+    slots = segments[::CHUNK]
     joint_bias = jnp.concatenate(
-        [bias_full[0:width], jnp.zeros((width,), WIDE), bias_full[width : 2 * width]]
-    )
-    joint_rows = (joint_proj + joint_bias).astype(LOW)
+        [bias_full[:, 0:width], jnp.zeros((1, width), WIDE), bias_full[:, width : 2 * width]], axis=1
+    )
+    attn_input, joint_rows = qkv_forward(slots, x_in, table, joint_bias, qkv_low)
     mixture, log_totals, proj_w, fc1_w, fc2_w = attend(
         joint_rows, segments, fc2_weight.astype(LOW), proj_w, fc1_w
     )
-    proj_low, fc1_low, fc2_low = joined(proj_w), joined(fc1_w), joined(fc2_w)
-    hidden_width = fc2_low.shape[1]
-    attn_out = (
-        jnp.concatenate([times(mixture, proj_low[0]), times(mixture, proj_low[1])], 1)
-        + bias_full[2 * width : 3 * width]
-    )
-    residual_mid = residual + gate_attn * attn_out
-    second_norm, second_inverse = normalize(residual_mid)
-    mlp_input = (second_norm * (1.0 + scale_mlp) + shift_mlp).astype(LOW)
-    pre_act = (
-        jnp.concatenate([times(mlp_input, fc1_low[0]), times(mlp_input, fc1_low[1])], 1)
-        + bias_full[3 * width : 3 * width + hidden_width]
-    )
-    hidden_full, gelu_back = jax.vjp(partial(jax.nn.gelu, approximate=True), pre_act)
-    hidden = hidden_full.astype(LOW)
-    branch = (
-        jnp.concatenate([times(hidden, fc2_low[0]), times(hidden, fc2_low[1])], 1)
-        + bias_full[3 * width + hidden_width :]
-    )
-    block_out = (residual_mid + gate_mlp * branch).astype(LOW)
-
-    def halves(values):
-        middle = values.shape[1] // 2
-        return jnp.stack([values[:, :middle], values[:, middle:]])
-
-    upstream = out_grad.astype(WIDE)
-    branch_grad = (gate_mlp * upstream).astype(LOW)
-    gate_mlp_grad = upstream * branch
-    branch_halves = halves(branch_grad)
+    (
+        block_out, mlp_input, hidden, pre_halves, branch_halves, attn_halves, mixture_grad, middle_grad, sums, pre_sums,
+    ) = middle(
+        slots, x_in, out_grad, mixture, table, bias_full, joined(proj_w), joined(fc1_w), joined(fc2_w)
+    )
     fc2_quads = chip_quads(hidden, branch_halves)
-    hidden_grad = times_back(branch_halves[0], fc2_low[0]) + times_back(branch_halves[1], fc2_low[1])
-    pre_grad = gelu_back(hidden_grad)[0].astype(LOW)
-    pre_halves = halves(pre_grad)
     fc1_quads = chip_quads(mlp_input, pre_halves)
-    mlp_grad = times_back(pre_halves[0], fc1_low[0]) + times_back(pre_halves[1], fc1_low[1])
-    scale_mlp_grad = mlp_grad * second_norm
-    middle_grad = upstream + normalize_back(
-        mlp_grad * (1.0 + scale_mlp), second_norm, second_inverse
-    )
-    attn_grad = (gate_attn * middle_grad).astype(LOW)
-    gate_attn_grad = middle_grad * attn_out
-    attn_halves = halves(attn_grad)
     proj_quads = chip_quads(mixture, attn_halves)
-    mixture_grad = (
-        times_back(attn_halves[0], proj_low[0]) + times_back(attn_halves[1], proj_low[1])
-    ).astype(LOW)
     joint_halves, fc2_shard, proj_shard, fc1_totals = attend_back(
         joint_rows,
         segments,
@@ -843,23 +1028,16 @@
         fc1_quads,
         proj_quads,
     )
-    query_grad = joint_halves[0, :, 0:width]
-    value_grad = joint_halves[1, :, width // 2 :]
+    x_grad, first_sums, joint_sums = qkv_backward(
+        slots, joint_halves, x_in, middle_grad, table, qkv_low
+    )
     qkv_quads = chip_quads(attn_input, joint_halves)
     qkv_shard, fc1_shard = last_scatter(qkv_quads, fc1_totals)
-    input_grad = times_back(joint_halves[0], qkv_low[0]) + times_back(joint_halves[1], qkv_low[1])
-    scale_attn_grad = input_grad * first_norm
-    x_grad = middle_grad + normalize_back(
-        input_grad * (1.0 + scale_attn), first_norm, first_inverse
-    )
-
-    token_mod_grad = jnp.concatenate(
-        [input_grad, scale_attn_grad, gate_attn_grad, mlp_grad, scale_mlp_grad, gate_mlp_grad],
-        axis=1,
-    )
-    slot_mod_grad = jnp.einsum(
-        "ts,tc->sc", chooser.astype(WIDE), token_mod_grad, precision=lax.Precision.HIGHEST
-    ).astype(LOW)
+
+    chooser = (slots[None, :] == jnp.arange(images, dtype=jnp.int32)[:, None]).astype(WIDE)
+    tile_mod_grad = jnp.concatenate([first_sums[:, 0:2], sums[:, 0:4]], axis=1)
+    slot_mod_grad = jnp.sum(chooser[:, :, None, None] * tile_mod_grad[None], axis=1)
+    slot_mod_grad = slot_mod_grad.reshape(images, -1).astype(LOW)
     half_grad = lax.all_to_all(slot_mod_grad, "mod", split_axis=1, concat_axis=0, tiled=True)
     mod_grad_all = lax.all_gather(half_grad, ROWS, axis=0, tiled=True)
     own_rows = ada_weight.shape[0]
@@ -874,10 +1052,15 @@
     silu_part = lax.all_to_all(silu_part, ROWS, split_axis=0, concat_axis=1, tiled=True)
     cond_grad = silu_back(silu_part + swap(silu_part, "mod"))[0]
 
+    joint_sum = jnp.sum(joint_sums, axis=0).reshape(-1)
+    sum_rows = jnp.sum(sums, axis=0)
     grad_bias = jnp.concatenate(
         [
-            jnp.sum(part.astype(WIDE), axis=0)
-            for part in (query_grad, value_grad, attn_grad, pre_grad, branch_grad)
+            joint_sum[0:width],
+            joint_sum[2 * width :],
+            sum_rows[4],
+            jnp.sum(pre_sums, axis=0).reshape(-1),
+            sum_rows[5],
         ]
     ).reshape(devices, -1)
     bias_shard = jnp.sum(

time: 1030 us -> 827 us (0.80)
  Pallas kernels: 415 us -> 567 us
  matrix products: 260 us -> 112 us
  other arithmetic: 109 us -> 17 us
  blocking collectives: 105 us -> 24.1 us
  local copies, waits for them, and re-layouts: 88.1 us -> 35 us
  starting transfers between devices: 28.3 us -> 44.1 us
    pallas_call x0 -> x3, Pallas kernels: none -> 138 us  [the longest x1 102 us: middle(): tile_call(middle_kernel, tokens, [tile(D), tile(D), tile(D), fixed(*table...]
    dot_general x9 -> x1, matrix products: 90.1 us -> 1.02 us  [times_back(): lax.dot_general(left, right, (((1,), (1,)), ((), ())), preferred_element_...]
    dot_general x42 -> x33, matrix products: 152 us -> 107 us  [times(): return jnp.dot(left, right, preferred_element_type=WIDE)]
    unnamed x1 -> x0, blocking collectives: 41.2 us -> none
    all_gather x1 -> x0, blocking collectives: 39.6 us -> none  [body(): silu_all = lax.all_gather(cond_silu.astype(LOW), ROWS, axis=0, tiled=True)]
    reduce_sum x8 -> x4, other arithmetic: 37.3 us -> 1.28 us  [the longest x1 0.85 us: body(): joint_sum = jnp.sum(joint_sums, axis=0).reshape(-1)]
    convert_element_type x5 -> x4, other arithmetic: 26.9 us -> 0.62 us  [the longest x1 0.58 us: body(): (slots[None, :] == jnp.arange(images, dtype=jnp.int32)[:, None]).astype(W...]
    slice x7 -> x6, local copies, waits for them, and re-layouts: 26.6 us -> 2.76 us  [the longest x1 1.11 us: body(): small[:, :, width // 2:width // 2 + LANES].reshape(2, row_devices, -1)]
  transfers between devices with their start and end apart: 22 -> 22, of which waited for: 3 -> 3; matrix products, arithmetic and copies ran while one was open for 12% -> 10% of each run, Pallas kernels for 7% -> 11%
where the time goes in v4:
time: 827 us; the launch traced here: 815 us
  Pallas kernels  567 us (69%)
  matrix products  112 us (14%)
  starting transfers between devices  44.1 us (5%)
  local copies, waits for them, and re-layouts  35 us (4%)
  blocking collectives  24.1 us (3%)
  other arithmetic  17 us (2%)
  waiting for transfers between devices  13.3 us (2%)
    pallas_call x1, Pallas kernels, attend(): pl.pallas_call(attend_kernel, out_shape=(jax.ShapeDtypeStruct((tokens, HE...  143 us
    pallas_call x1, Pallas kernels, attend_back(): pl.pallas_call(partial(attend_back_kernel, spans=len(spans)), out_shape=(...  132 us
    dot_general x33, matrix products, times(): return jnp.dot(left, right, preferred_element_type=WIDE)  107 us
    pallas_call x1, Pallas kernels, middle(): tile_call(middle_kernel, tokens, [tile(D), tile(D), tile(D), fixed(*table...  102 us
    pallas_call x1, Pallas kernels, first_gather(): pl.pallas_call(first_kernel, out_shape=tuple((whole_shape(shard) for shar...  88.6 us
    pallas_call x1, Pallas kernels, last_scatter(): pl.pallas_call(partial(last_kernel, spans=len(totals)), out_shape=(jax.Sh...  66.1 us
    all_gather x1, blocking collectives, body(): mod_grad_all = lax.all_gather(half_grad, ROWS, axis=0, tiled=True)  24.1 us
    pallas_call x1, Pallas kernels, qkv_backward(): tile_call(qkv_backward_kernel, tokens, [half_tile(half), tile(D), tile(D)...  19.2 us
  transfers between devices with their start and end apart: 22, of which 3 were waited for; matrix products, arithmetic and copies ran while one was open for 10% of the time, Pallas kernels for 11%

profile of v4, /device:TPU:0, one launch (start us, length us, event | category | flops | bytes accessed | tf_op | source)
XLA Modules:
  0.0 815.3 jit_solution(5164734529317370301)
XLA Ops:
  4.8 7.5 all-to-all-start
  15.4 88.6 %first_gather.1 = (bf16[2,4,2,2,8,768]{5,4,3,2,1,0:T(8,128)(2,1)}, bf16[2,4,2,2,72,1728]{5,4,3,2,1,0:T(8,128)(2,1)}, bf16[2,4,2,2,72,576]{5,4,3,2,1,0:T(8,128)(2,1)}, bf16[2,4,2,2,72,2304]{5,4,3,2,1,0:T(8,128)(2,1)}) custom-call(bf16[8,768]{1,0:T(8,128)(2,1)} %maximum_maximum_fusion.refs_0_, bf16[72,1728]{1,0:T(8,128)(2,1)} %convert_element_type.215.refs_1_, ...), custom_call_target="tpu_custom_call" | custom-call | tf_op jit(solution)/shard_map/first_gather/pallas_call | solution.py:216
  108.4 18.6 %all-to-all-start.1 = ((bf16[32,4,216]{2,1,0:T(4,128)(2,1)}), bf16[32,4,216]{2,1,0:T(4,128)(2,1)S(1)}, u32[]{:S(2)}, u32[]{:S(2)}) async-start(bf16[32,4,216]{2,1,0:T(4,128)(2,1)} %all_to_all.60), calls=%async_computation.1 | async-start | bytes 131072 | tf_op jit(solution)/shard_map/all_to_all | solution.py:997
  128.0 6.7 all-to-all-done.1
  135.5 17.5 %qkv_forward.1 = (bf16[1024,1152]{1,0:T(8,128)(2,1)}, bf16[1024,3456]{1,0:T(8,128)(2,1)}) custom-call(s32[4]{0:T(128)} %copy-done.44, bf16[1024,1152]{1,0:T(8,128)(2,1)} %x_ref.5, f32[4,6912]{1,0:T(4,128)} %reshape.366.table, f32[1,3456]{1,0:T(1,128)} %fusion.282.bias, bf16[2,1152,1728]{2,1,0:T(8,128)(2,1)} %bitcast.424), custom_call_target="tpu_custom_call" | custom-call | flops 8153726976 | bytes 19759104 | tf_op jit(solution)/shard_map/qkv_forward/pallas_call | solution.py:746
  153.0 142.6 %attend.1 = (bf16[1024,1152]{1,0:T(8,128)(2,1)S(1)}, f32[1024,128]{1,0:T(8,128)S(1)}, bf16[2,4,2,2,72,576]{5,4,3,2,1,0:T(8,128)(2,1)}, bf16[2,4,2,2,72,2304]{5,4...) custom-call(bf16[1024,3456]{1,0:T(8,128)(2,1)} %get-tuple-element.56.refs_0_, ...), custom_call_target="tpu_custom_call", output_to_operand_aliasing={{2}: (3, {}), {3}: (4, {})} | custom-call | tf_op jit(solution)/shard_map/attend/pallas_call | solution.py:313
  296.4 2.9 copy.143
  299.3 101.8 %middle.1 = (bf16[1024,1152]{1,0:T(8,128)(2,1)}, bf16[1024,1152]{1,0:T(8,128)(2,1)}, bf16[1024,4608]{1,0:T(8,128)(2,1)}, bf16[2,1024,2304]{2,1,0:T(8,128)(2,1)},...) custom-call(s32[4]{0:T(128)} %copy-done.44, ...), custom_call_target="tpu_custom_call" | custom-call | flops 48922361856 | bytes 71073792 | tf_op jit(solution)/shard_map/middle/pallas_call | solution.py:833
  403.4 2.7 fusion.173
  406.1 2.7 fusion.170
  408.8 2.8 copy.142
  411.6 5.1 fusion.25
  416.8 2.6 fusion.22
  419.4 2.7 fusion.19
  422.1 12.7 %copy.139 = bf16[1024,4608]{0,1:T(8,128)(2,1)} copy(bf16[1024,4608]{1,0:T(8,128)(2,1)} %get-tuple-element.66) | data formatting | bytes 18874368 | tf_op jit(solution)/shard_map/middle/pallas_call | solution.py:833
  434.9 5.3 fusion.129
  440.2 4.6 fusion.123
  444.8 3.2 fusion.126
  448.0 3.1 fusion.120
  451.5 2.4 fusion.164
  455.1 4.7 copy.151
  459.8 4.0 fusion.16
  470.1 2.5 add_convert_fusion.10.refs_14_
  472.9 2.5 add_convert_fusion.11.refs_13_
  475.7 5.5 add_convert_fusion.4.refs_12_
  481.6 5.0 add_convert_fusion.5.refs_11_
  486.9 2.6 add_convert_fusion.6.refs_10_
  489.6 2.6 add_convert_fusion.7.refs_9_
  492.2 3.2 add_convert_fusion.refs_8_
  495.4 3.3 add_convert_fusion.1.refs_7_
  498.7 3.1 add_convert_fusion.2.refs_6_
  501.8 3.1 add_convert_fusion.3.refs_5_
  504.9 131.7 %attend_back.1 = (bf16[2,1024,1728]{2,1,0:T(8,128)(2,1)}, f32[288,576]{1,0:T(8,128)}, f32[72,576]{1,0:T(8,128)}, bf16[4,72,2304]{2,1,0:T(8,128)(2,1)}) custom-call(bf16[1024,3456]{1,0:T(8,128)(2,1)} %get-tuple-element.56.refs_0_, s32[1024,1]{1,0:T(8,128)} %copy-done.1, bf16[1024,1152]{1,0:T(8,128)(2,1)} %copy-done, f32[1024,128]{1,0:T(8,128)} %copy-done.2, ...), custom_call_target="tpu_custom_call" | custom-call | tf_op jit(solution)/shard_map/attend_back/pallas_call | solution.py:652
  636.7 4.6 fusion.61
  641.3 4.4 fusion.58
  650.3 19.2 %qkv_backward.1 = (f32[1024,1152]{1,0:T(8,128)}, f32[4,8,1152]{2,1,0:T(8,128)}, f32[4,2,1728]{2,1,0:T(2,128)}) custom-call(s32[4]{0:T(128)} %copy-done.44, bf16[2,1024,1728]{2,1,0:T(8,128)(2,1)} %get-tuple-element.71.joint_ref, bf16[1024,1152]{1,0:T(8,128)(2,1)} %x_ref.5, f32[1024,1152]{1,0:T(8,128)} %get-tuple-element.72.dx1_ref, ...), custom_call_target="tpu_custom_call" | custom-call | flops 8153726976 | bytes 29196288 | tf_op jit(solution)/shard_map/qkv_backward/pallas_call | solution.py:898
  671.5 3.3 all-to-all-start.2
  676.5 3.2 add_multiply_fusion.1
  681.8 4.8 all-to-all-start.4
  686.7 24.1 %all_gather.3 = bf16[128,3456]{1,0:T(8,128)(2,1)S(1)} all-gather(bf16[8,3456]{1,0:T(8,128)(2,1)S(1)} %all_to_all.64), channel_id=1, replica_groups=mesh['far'=4,'near'=2,'core'=2,'mod'=2] {'far','near','core'}, dimensions={0}, use_global_device_ids=true | all-gather | bytes 940032 | tf_op jit(solution)/shard_map/all_gather | solution.py:1042
  710.8 3.9 add_multiply_fusion
  715.8 3.8 all-to-all-start.3
  721.7 4.7 all-to-all-done.3
  731.2 4.7 fusion.74.refs_3_
  735.9 4.7 fusion.77.refs_2_
  740.6 2.5 fusion.90.refs_1_
  743.1 2.5 fusion.93.refs_0_
  745.7 66.1 %last_scatter.1 = (f32[72,1728]{1,0:T(8,128)S(1)}, f32[72,2304]{1,0:T(8,128)S(1)}) custom-call(bf16[4,72,1728]{2,1,0:T(8,128)(2,1)S(1)} %fusion.93.refs_0_, bf16[4,72,1728]{2,1,0:T(8,128)(2,1)S(1)} %fusion.90.refs_1_, bf16[4,72,1728]{2,1,0:T(8,128)(2,1)} %fusion.77.refs_2_, bf16[4,72,1728]{2,1,0:T(8,128)(2,1)} %fusion.74.refs_3_, ...), custom_call_target="tpu_custom_call" | custom-call | tf_op jit(solution)/shard_map/last_scatter/pallas_call | solution.py:498
  (245 shorter events, 46.8 us)
Async XLA Ops:
  0.7 11.6 %copy-start.31 = (bf16[8,1152]{1,0:T(8,128)(2,1)S(1)}, bf16[8,1152]{1,0:T(8,128)(2,1)}, u32[]{:S(2)}) copy-start(bf16[8,1152]{1,0:T(8,128)(2,1)} %param.26) | copy-start | bytes 55300
  0.7 11.8 %copy-start.37 = (f32[288]{0:T(512)S(1)}, f32[288]{0:T(512)}, u32[]{:S(2)}) copy-start(f32[288]{0:T(512)} %param.41) | copy-start | bytes 3460
  0.7 11.8 %copy-start.9 = (f32[72,2304]{1,0:T(8,128)S(1)}, f32[72,2304]{1,0:T(8,128)}, u32[]{:S(2)}) copy-start(f32[72,2304]{1,0:T(8,128)} %param.35) | copy-start | bytes 1990660
  2.0 12.0 %copy-start.4 = (bf16[72,3456]{1,0:T(8,128)(2,1)}, bf16[72,3456]{1,0:T(8,128)(2,1)S(1)}, u32[]{:S(2)}) copy-start(bf16[72,3456]{1,0:T(8,128)(2,1)S(1)} %convert_element_type.218) | copy-start | bytes 1492996
  4.8 101.5 %copy-start.40 = (f32[1,216]{1,0:T(1,128)S(1)}, f32[1,216]{1,0:T(1,128)}, u32[]{:S(2)}) copy-start(f32[1,216]{1,0:T(1,128)} %param.47) | copy-start | bytes 2596
  4.8 101.7 %copy-start.39 = (s32[1024]{0:T(1024)S(1)}, s32[1024]{0:T(1024)}, u32[]{:S(2)}) copy-start(s32[1024]{0:T(1024)} %param.27) | copy-start | bytes 12292
  4.8 102.4 %all-to-all-start = ((bf16[72,16,216]{2,0,1:T(8,128)(2,1)}), bf16[72,16,216]{2,0,1:T(8,128)(2,1)S(1)}, u32[]{:S(2)}, u32[]{:S(2)}) async-start(bf16[72,16,216]{2,0,1:T(8,128)(2,1)} %copy.134), calls=%async_computation | async-start | bytes 1179648 | tf_op jit(solution)/shard_map/all_to_all | solution.py:984
  13.3 114.6 %copy-start.7 = (f32[288,576]{1,0:T(8,128)S(1)}, f32[288,576]{1,0:T(8,128)}, u32[]{:S(2)}) copy-start(f32[288,576]{1,0:T(8,128)} %param.38) | copy-start | bytes 1990660
  105.1 22.9 %copy-start.17 = (bf16[128,576]{1,0:T(8,128)(2,1)}, bf16[128,576]{1,0:T(8,128)(2,1)S(1)}, u32[]{:S(2)}) copy-start(bf16[128,576]{1,0:T(8,128)(2,1)S(1)} %get-tuple-element.107) | copy-start | bytes 442372
  105.1 22.9 %copy-start.19 = (bf16[128,576]{1,0:T(8,128)(2,1)}, bf16[128,576]{1,0:T(8,128)(2,1)S(1)}, u32[]{:S(2)}) copy-start(bf16[128,576]{1,0:T(8,128)(2,1)S(1)} %get-tuple-element.108) | copy-start | bytes 442372
  106.5 46.5 %copy-start.33 = (f32[1,9216]{1,0:T(1,128)}, f32[1,9216]{1,0:T(1,128)S(1)}, u32[]{:S(2)}) copy-start(f32[1,9216]{1,0:T(1,128)S(1)} %reshape.367.bias) | copy-start | bytes 110596
  106.6 29.0 %copy-start.44 = (s32[4]{0:T(128)}, s32[4]{0:T(128)S(1)}, u32[]{:S(2)}) copy-start(s32[4]{0:T(128)S(1)} %slice.39.slots) | copy-start | bytes 52
  108.4 26.2 %all-to-all-start.1 = ((bf16[32,4,216]{2,1,0:T(4,128)(2,1)}), bf16[32,4,216]{2,1,0:T(4,128)(2,1)S(1)}, u32[]{:S(2)}, u32[]{:S(2)}) async-start(bf16[32,4,216]{2,1,0:T(4,128)(2,1)} %all_to_all.60), calls=%async_computation.1 | async-start | bytes 131072 | tf_op jit(solution)/shard_map/all_to_all | solution.py:997
  127.9 25.1 %copy-start.1 = (s32[1024,1]{1,0:T(8,128)}, s32[1024,1]{1,0:T(8,128)S(1)}, u32[]{:S(2)}) copy-start(s32[1024,1]{1,0:T(8,128)S(1)} %copy.138.refs_1_) | copy-start | bytes 12292
  451.1 24.3 %collective-permute-start.7 = (bf16[4,72,2304]{2,1,0:T(8,128)(2,1)}, bf16[4,72,2304]{2,1,0:T(8,128)(2,1)}, u32[]{:S(2)}, u32[]{:S(2)}) collective-permute-start(bf16[4,72,2304]{2,1,0:T(8,128)(2,1)} %fusion.25), channel_id=1, source_target_pairs={{0,2},{2,0},{1,3},{3,1},{4,6},{6,4},{5,7},{7,5},{8,10},{10,8},{9,1... | collective-permute-start | bytes 3981320 | tf_op jit(solution)/shard_map/ppermute | solution.py:912
  453.9 10.6 %collective-permute-start.11 = (bf16[4,72,576]{2,1,0:T(8,128)(2,1)}, bf16[4,72,576]{2,1,0:T(8,128)(2,1)}, u32[]{:S(2)}, u32[]{:S(2)}) collective-permute-start(bf16[4,72,576]{2,1,0:T(8,128)(2,1)} %fusion.173), channel_id=1, source_target_pairs={{0,2},{2,0},{1,3},{3,1},{4,6},{6,4},{5,7},{7,5},{8,10},{10,8},{9,1... | collective-permute-start | bytes 995336 | tf_op jit(solution)/shard_map/ppermute | solution.py:912
  454.2 12.9 %collective-permute-start.10 = (bf16[4,72,576]{2,1,0:T(8,128)(2,1)}, bf16[4,72,576]{2,1,0:T(8,128)(2,1)}, u32[]{:S(2)}, u32[]{:S(2)}) collective-permute-start(bf16[4,72,576]{2,1,0:T(8,128)(2,1)} %fusion.170), channel_id=1, source_target_pairs={{0,2},{2,0},{1,3},{3,1},{4,6},{6,4},{5,7},{7,5},{8,10},{10,8},{9,1... | collective-permute-start | bytes 995336 | tf_op jit(solution)/shard_map/ppermute | solution.py:912
  454.5 15.3 %collective-permute-start.9 = (bf16[4,72,576]{2,1,0:T(8,128)(2,1)S(1)}, bf16[4,72,576]{2,1,0:T(8,128)(2,1)}, u32[]{:S(2)}, u32[]{:S(2)}) collective-permute-start(bf16[4,72,576]{2,1,0:T(8,128)(2,1)S(1)} %fusion.167), channel_id=1, source_target_pairs={{0,2},{2,0},{1,3},{3,1},{4,6},{6,4},{5,7},{7,5},{8,10},{10,8},{9,1... | collective-permute-start | bytes 995336 | tf_op jit(solution)/shard_map/ppermute | solution.py:912
  454.7 17.9 %collective-permute-start.8 = (bf16[4,72,576]{2,1,0:T(8,128)(2,1)}, bf16[4,72,576]{2,1,0:T(8,128)(2,1)}, u32[]{:S(2)}, u32[]{:S(2)}) collective-permute-start(bf16[4,72,576]{2,1,0:T(8,128)(2,1)} %fusion.164), channel_id=1, source_target_pairs={{0,2},{2,0},{1,3},{3,1},{4,6},{6,4},{5,7},{7,5},{8,10},{10,8},{9,1... | collective-permute-start | bytes 995336 | tf_op jit(solution)/shard_map/ppermute | solution.py:912
  464.5 16.7 %collective-permute-start.6 = (bf16[4,72,2304]{2,1,0:T(8,128)(2,1)S(1)}, bf16[4,72,2304]{2,1,0:T(8,128)(2,1)S(1)}, u32[]{:S(2)}, u32[]{:S(2)}) collective-permute-start(bf16[4,72,2304]{2,1,0:T(8,128)(2,1)S(1)} %copy-done.50), channel_id=1, source_target_pairs={{0,2},{2,0},{1,3},{3,1},{4,6},{6,4},{5,7},{7,5},{8,10},{10,8},{9,1... | collective-permute-start | bytes 3981320 | tf_op jit(solution)/shard_map/ppermute | solution.py:912
  467.0 19.6 %collective-permute-start.5 = (bf16[4,72,2304]{2,1,0:T(8,128)(2,1)S(1)}, bf16[4,72,2304]{2,1,0:T(8,128)(2,1)S(1)}, u32[]{:S(2)}, u32[]{:S(2)}) collective-permute-start(bf16[4,72,2304]{2,1,0:T(8,128)(2,1)S(1)} %copy-done.49), channel_id=1, source_target_pairs={{0,2},{2,0},{1,3},{3,1},{4,6},{6,4},{5,7},{7,5},{8,10},{10,8},{9,1... | collective-permute-start | bytes 3981320 | tf_op jit(solution)/shard_map/ppermute | solution.py:912
  469.9 19.7 %collective-permute-start.4 = (bf16[4,72,2304]{2,1,0:T(8,128)(2,1)S(1)}, bf16[4,72,2304]{2,1,0:T(8,128)(2,1)S(1)}, u32[]{:S(2)}, u32[]{:S(2)}) collective-permute-start(bf16[4,72,2304]{2,1,0:T(8,128)(2,1)S(1)} %fusion.16), channel_id=1, source_target_pairs={{0,2},{2,0},{1,3},{3,1},{4,6},{6,4},{5,7},{7,5},{8,10},{10,8},{9,1... | collective-permute-start | bytes 3981320 | tf_op jit(solution)/shard_map/ppermute | solution.py:912
  472.6 19.6 %collective-permute-start.3 = (bf16[4,288,576]{2,1,0:T(8,128)(2,1)S(1)}, bf16[4,288,576]{2,1,0:T(8,128)(2,1)S(1)}, u32[]{:S(2)}, u32[]{:S(2)}) collective-permute-start(bf16[4,288,576]{2,1,0:T(8,128)(2,1)S(1)} %copy-done.48), channel_id=1, source_target_pairs={{0,2},{2,0},{1,3},{3,1},{4,6},{6,4},{5,7},{7,5},{8,10},{10,8},{9,1... | collective-permute-start | bytes 3981320 | tf_op jit(solution)/shard_map/ppermute | solution.py:912
  472.9 14.0 %slice-start.7 = ((s8[9437184]{0:T(1024)(128)(4,1)}), s8[4194304]{0:T(1024)(128)(4,1)S(1)}, s32[]{:S(2)}) async-start(s8[9437184]{0:T(1024)(128)(4,1)} %bitcast.430), calls=%async_computation.12 | async-start | bytes 8388608
  475.4 20.0 %collective-permute-start.2 = (bf16[4,288,576]{2,1,0:T(8,128)(2,1)S(1)}, bf16[4,288,576]{2,1,0:T(8,128)(2,1)S(1)}, u32[]{:S(2)}, u32[]{:S(2)}) collective-permute-start(bf16[4,288,576]{2,1,0:T(8,128)(2,1)S(1)} %copy-done.47), channel_id=1, source_target_pairs={{0,2},{2,0},{1,3},{3,1},{4,6},{6,4},{5,7},{7,5},{8,10},{10,8},{9,1... | collective-permute-start | bytes 3981320 | tf_op jit(solution)/shard_map/ppermute | solution.py:912
  481.3 17.4 %collective-permute-start.1 = (bf16[4,288,576]{2,1,0:T(8,128)(2,1)S(1)}, bf16[4,288,576]{2,1,0:T(8,128)(2,1)S(1)}, u32[]{:S(2)}, u32[]{:S(2)}) collective-permute-start(bf16[4,288,576]{2,1,0:T(8,128)(2,1)S(1)} %copy-done.46), channel_id=1, source_target_pairs={{0,2},{2,0},{1,3},{3,1},{4,6},{6,4},{5,7},{7,5},{8,10},{10,8},{9,1... | collective-permute-start | bytes 3981320 | tf_op jit(solution)/shard_map/ppermute | solution.py:912
  486.7 15.2 %collective-permute-start = (bf16[4,288,576]{2,1,0:T(8,128)(2,1)S(1)}, bf16[4,288,576]{2,1,0:T(8,128)(2,1)S(1)}, u32[]{:S(2)}, u32[]{:S(2)}) collective-permute-start(bf16[4,288,576]{2,1,0:T(8,128)(2,1)S(1)} %copy-done.45), channel_id=1, source_target_pairs={{0,2},{2,0},{1,3},{3,1},{4,6},{6,4},{5,7},{7,5},{8,10},{10,8},{9,1... | collective-permute-start | bytes 3981320 | tf_op jit(solution)/shard_map/ppermute | solution.py:912
  650.3 20.2 %copy-start.36 = (f32[4,4]{1,0:T(4,128)S(1)}, f32[4,4]{1,0:T(4,128)}, u32[]{:S(2)}) copy-start(f32[4,4]{1,0:T(4,128)} %fusion.316) | copy-start | bytes 196
  650.3 25.5 %copy-start.34 = (f32[9216]{0:T(1024)S(1)}, f32[9216]{0:T(1024)}, u32[]{:S(2)}) copy-start(f32[9216]{0:T(1024)} %custom-call) | copy-start | bytes 110596
  650.3 26.1 %copy-start.8 = (f32[288,576]{1,0:T(8,128)S(1)}, f32[288,576]{1,0:T(8,128)}, u32[]{:S(2)}) copy-start(f32[288,576]{1,0:T(8,128)} %param.38) | copy-start | bytes 1990660
  671.5 10.3 %all-to-all-start.2 = ((bf16[4,2,3456]{2,0,1:T(4,128)(2,1)}), bf16[4,2,3456]{2,0,1:T(4,128)(2,1)S(1)}, u32[]{:S(2)}, u32[]{:S(2)}) async-start(bf16[4,2,3456]{2,0,1:T(4,128)(2,1)} %copy.148), calls=%async_computation.2 | async-start | bytes 110592 | tf_op jit(solution)/shard_map/all_to_all | solution.py:1041
  675.8 55.4 %collective-permute-start.16 = (bf16[4,72,1728]{2,1,0:T(8,128)(2,1)}, bf16[4,72,1728]{2,1,0:T(8,128)(2,1)}, u32[]{:S(2)}, u32[]{:S(2)}) collective-permute-start(bf16[4,72,1728]{2,1,0:T(8,128)(2,1)} %fusion.61), channel_id=1, source_target_pairs={{0,2},{2,0},{1,3},{3,1},{4,6},{6,4},{5,7},{7,5},{8,10},{10,8},{9,1... | collective-permute-start | bytes 2985992 | tf_op jit(solution)/shard_map/ppermute | solution.py:912
  675.9 67.3 %collective-permute-start.13 = (bf16[4,72,1728]{2,1,0:T(8,128)(2,1)}, bf16[4,72,1728]{2,1,0:T(8,128)(2,1)}, u32[]{:S(2)}, u32[]{:S(2)}) collective-permute-start(bf16[4,72,1728]{2,1,0:T(8,128)(2,1)} %fusion.52), channel_id=1, source_target_pairs={{0,2},{2,0},{1,3},{3,1},{4,6},{6,4},{5,7},{7,5},{8,10},{10,8},{9,1... | collective-permute-start | bytes 2985992 | tf_op jit(solution)/shard_map/ppermute | solution.py:912
  679.6 31.1 %copy-start.6 = (f32[72,3456]{1,0:T(8,128)S(1)}, f32[72,3456]{1,0:T(8,128)}, u32[]{:S(2)}) copy-start(f32[72,3456]{1,0:T(8,128)} %param.44) | copy-start | bytes 2985988
  679.6 31.1 %copy-start.18 = (bf16[128,576]{1,0:T(8,128)(2,1)S(1)}, bf16[128,576]{1,0:T(8,128)(2,1)}, u32[]{:S(2)}) copy-start(bf16[128,576]{1,0:T(8,128)(2,1)} %copy-done.17) | copy-start | bytes 442372
  681.3 54.6 %collective-permute-start.15 = (bf16[4,72,1728]{2,1,0:T(8,128)(2,1)}, bf16[4,72,1728]{2,1,0:T(8,128)(2,1)}, u32[]{:S(2)}, u32[]{:S(2)}) collective-permute-start(bf16[4,72,1728]{2,1,0:T(8,128)(2,1)} %fusion.58), channel_id=1, source_target_pairs={{0,2},{2,0},{1,3},{3,1},{4,6},{6,4},{5,7},{7,5},{8,10},{10,8},{9,1... | collective-permute-start | bytes 2985992 | tf_op jit(solution)/shard_map/ppermute | solution.py:912
  681.4 59.2 %collective-permute-start.14 = (bf16[4,72,1728]{2,1,0:T(8,128)(2,1)}, bf16[4,72,1728]{2,1,0:T(8,128)(2,1)}, u32[]{:S(2)}, u32[]{:S(2)}) collective-permute-start(bf16[4,72,1728]{2,1,0:T(8,128)(2,1)} %fusion.55), channel_id=1, source_target_pairs={{0,2},{2,0},{1,3},{3,1},{4,6},{6,4},{5,7},{7,5},{8,10},{10,8},{9,1... | collective-permute-start | bytes 2985992 | tf_op jit(solution)/shard_map/ppermute | solution.py:912
  681.8 34.0 %all-to-all-start.4 = ((f32[32,1,288]{2,1,0:T(1,128)}), f32[32,1,288]{2,1,0:T(1,128)}, u32[]{:S(2)}, u32[]{:S(2)}) async-start(f32[32,1,288]{2,1,0:T(1,128)} %all_to_all.69), calls=%async_computation.4 | async-start | bytes 98304 | tf_op jit(solution)/shard_map/all_to_all | solution.py:1067
  710.7 17.4 %copy-start.38 = (f32[288]{0:T(512)S(1)}, f32[288]{0:T(512)}, u32[]{:S(2)}) copy-start(f32[288]{0:T(512)} %param.41) | copy-start | bytes 3460
  710.7 17.4 %copy-start.42 = (f32[288]{0:T(512)S(1)}, f32[288]{0:T(512)}, u32[]{:S(2)}) copy-start(f32[288]{0:T(512)} %param.43) | copy-start | bytes 3460
  710.7 17.4 %copy-start.43 = (f32[288]{0:T(512)S(1)}, f32[288]{0:T(512)}, u32[]{:S(2)}) copy-start(f32[288]{0:T(512)} %param.42) | copy-start | bytes 3460
  710.8 19.8 %copy-start.32 = (bf16[8,1152]{1,0:T(8,128)(2,1)S(1)}, bf16[8,1152]{1,0:T(8,128)(2,1)}, u32[]{:S(2)}) copy-start(bf16[8,1152]{1,0:T(8,128)(2,1)} %param.26) | copy-start | bytes 55300
  710.8 20.4 %copy-start.12 = (bf16[1024,1152]{0,1:T(8,128)(2,1)S(1)}, bf16[1024,1152]{0,1:T(8,128)(2,1)}, u32[]{:S(2)}) copy-start(bf16[1024,1152]{0,1:T(8,128)(2,1)} %copy.151) | copy-start | bytes 7077892
  715.8 10.6 %all-to-all-start.3 = ((f32[16,8,72]{2,1,0:T(8,128)}), f32[16,8,72]{2,1,0:T(8,128)S(1)}, u32[]{:S(2)}, u32[]{:S(2)}) async-start(f32[16,8,72]{2,1,0:T(8,128)} %convolution_bitcast_fusion), calls=%async_computation.3 | async-start | bytes 131072 | tf_op jit(solution)/shard_map/all_to_all | solution.py:1052
  726.5 4.0 collective-permute-start.12
  745.7 66.2 %copy-start.10 = (f32[72,2304]{1,0:T(8,128)S(1)}, f32[72,2304]{1,0:T(8,128)}, u32[]{:S(2)}) copy-start(f32[72,2304]{1,0:T(8,128)} %param.35) | copy-start | bytes 1990660
  745.7 66.2 %copy-start.22 = (f32[72,2304]{1,0:T(8,128)S(1)}, f32[72,2304]{1,0:T(8,128)}, u32[]{:S(2)}) copy-start(f32[72,2304]{1,0:T(8,128)} %param.37) | copy-start | bytes 1990660
  745.7 66.2 %copy-start.23 = (f32[72,2304]{1,0:T(8,128)S(1)}, f32[72,2304]{1,0:T(8,128)}, u32[]{:S(2)}) copy-start(f32[72,2304]{1,0:T(8,128)} %param.36) | copy-start | bytes 1990660
  (40 other events, 192.8 us)
